TPU v7x, 32 devices: a whole 2x2x4 slice. The times are simulated.
32 devices in a mesh: dp: 2 (over core), expert: 4 (over y, x), shard: 4 (over z).
Axes of the slice: x: 2, y: 2, z: 4, core: 2. Of those that a mesh axis runs over, the one named last changes fastest.
Arguments:
- tokens: bfloat16 [2, 32, 64, 2048], P(None, ('dp', 'expert', 'shard')), may hold values from -6 to 6
- cotangent: bfloat16 [2, 32, 64, 2048], P(None, ('dp', 'expert', 'shard')), may hold values from -6 to 6
- lengths: int32 [2, 32], P(None, ('dp', 'expert', 'shard')), may hold values from 16 to 64, as said below
- routes: int32 [2, 32, 64, 8], P(None, ('dp', 'expert', 'shard')), may hold values from 0 to 15, all different within a row; in each aligned block of 64 rows (0 to 63, 64 to 127, ..., all dimensions but the last counted through in order) at most 64 rows name the same one
- w_query: bfloat16 [2048, 2048], P('shard'), may hold values from -0.125 to 0.125
- w_key: bfloat16 [2048, 2048], P('shard'), may hold values from -0.125 to 0.125
- w_value: bfloat16 [2048, 2048], P('shard'), may hold values from -0.125 to 0.125
- w_out: bfloat16 [2048, 2048], P('shard'), may hold values from -0.5 to 0.5
- w_router: bfloat16 [2048, 16], P('shard'), may hold values from -0.0625 to 0.0625
- g_attn: bfloat16 [2048], P('shard'), may hold values from 0.25 to 1.75
- g_ffn: bfloat16 [2048], P('shard'), may hold values from 0.25 to 1.75
- g_query: bfloat16 [2048], P('shard'), may hold values from 0.25 to 1.75
- g_key: bfloat16 [2048], P('shard'), may hold values from 0.25 to 1.75
- w_gate: bfloat16 [16, 2048, 1024], P(('expert', 'shard'), None, 'dp'), may hold values from -0.125 to 0.125
- w_up: bfloat16 [16, 2048, 1024], P(('expert', 'shard'), None, 'dp'), may hold values from -0.125 to 0.125
- w_down: bfloat16 [16, 1024, 2048], P(('expert', 'shard'), 'dp'), may hold values from -1.5 to 1.5
Outputs:
- mixed_out: bfloat16 [2, 32, 64, 2048], P(None, ('dp', 'expert', 'shard'))
- grad_tokens: float32 [2, 32, 64, 2048], P(None, ('dp', 'expert', 'shard'))
- grad_w_query: float32 [2048, 2048], P('shard')
- grad_w_key: float32 [2048, 2048], P('shard')
- grad_w_value: float32 [2048, 2048], P('shard')
- grad_w_out: float32 [2048, 2048], P('shard')
- grad_w_router: float32 [2048, 16], P('shard')
- grad_g_attn: float32 [2048], P('shard')
- grad_g_ffn: float32 [2048], P('shard')
- grad_g_query: float32 [2048], P('shard')
- grad_g_key: float32 [2048], P('shard')
- grad_w_gate: float32 [16, 2048, 1024], P(('expert', 'shard'), None, 'dp')
- grad_w_up: float32 [16, 2048, 1024], P(('expert', 'shard'), None, 'dp')
- grad_w_down: float32 [16, 1024, 2048], P(('expert', 'shard'), 'dp')
Inputs may be any that keep to these rules, and one draw needn't show every extreme that they name: `routes`: each row names 8 different experts. Among the 64 rows of one sequence no expert is named more than 64 times, and in some sequences an expert is named exactly 64 times. `lengths`: in every micro-batch at least one sequence has the full length 64.
All inputs are finite; a program needn't handle non-finite values.
Results may differ from a plain program's by a relative error of at most 0.022.
Values may be sent and summed in bfloat16 or wider, within the bound.
A program may use at most 320 MiB of HBM per device.

v0:
```python
import jax
import jax.numpy as jnp
from jax import lax
from jax.sharding import PartitionSpec as P

HEADS = 16
HDIM = 128


EPSILON = 1e-05


def matmul(left, right):
    return jnp.dot(left, right, preferred_element_type=jnp.float32)


def times_transposed(left, right):
    return lax.dot_general(
        left, right, (((1,), (1,)), ((), ())), preferred_element_type=jnp.float32
    )


def transposed_times(left, right):
    return lax.dot_general(
        left, right, (((0,), (0,)), ((), ())), preferred_element_type=jnp.float32
    )


def rms_norm(values, gain_vec):
    factor = lax.rsqrt(jnp.mean(values * values, axis=-1, keepdims=True) + EPSILON)
    return values * factor * gain_vec


def norm_back(values, gain_vec, incoming):
    factor = lax.rsqrt(jnp.mean(values * values, axis=-1, keepdims=True) + EPSILON)
    unit_rows = values * factor
    weighted = incoming * gain_vec
    d_values = factor * (
        weighted - unit_rows * jnp.mean(weighted * unit_rows, axis=-1, keepdims=True)
    )
    return (d_values, jnp.sum(incoming * unit_rows, axis=0))


def rope_tables(seq_count, head_size):
    half_dim = head_size // 2
    freqs = 10000.0 ** (-2.0 * jnp.arange(half_dim).astype(jnp.float32) / head_size)
    angles = jnp.arange(seq_count).astype(jnp.float32)[:, None] * freqs[None, :]
    cosine_table = jnp.concatenate([jnp.cos(angles), jnp.cos(angles)], axis=-1)
    sine_table = jnp.concatenate([jnp.sin(angles), jnp.sin(angles)], axis=-1)
    return (cosine_table, sine_table)


def rotate(head_rows, cosine_table, sine_table):
    half_dim = head_rows.shape[-1] // 2
    turned = jnp.concatenate([-head_rows[..., half_dim:], head_rows[..., :half_dim]], axis=-1)
    return head_rows * cosine_table[:, None, :] + turned * sine_table[:, None, :]


def rotate_back(incoming, cosine_table, sine_table):
    half_dim = incoming.shape[-1] // 2
    moved_part = incoming * sine_table[:, None, :]
    turned = jnp.concatenate([moved_part[..., half_dim:], -moved_part[..., :half_dim]], axis=-1)
    return incoming * cosine_table[:, None, :] + turned


def softmax_rows(scores):
    shifted = jnp.exp(scores - jnp.max(scores, axis=-1, keepdims=True))
    return shifted / jnp.sum(shifted, axis=-1, keepdims=True)


def dispatch_rows(buffer):
    return lax.all_to_all(buffer, ("expert", "shard"), split_axis=0, concat_axis=0, tiled=True)


def collect_rows(buffer):
    return lax.all_to_all(buffer, ("expert", "shard"), split_axis=0, concat_axis=0, tiled=True)


def dispatch_grads(buffer):
    return lax.all_to_all(buffer, ("expert", "shard"), split_axis=0, concat_axis=0, tiled=True)


def collect_grads(buffer):
    return lax.all_to_all(buffer, ("expert", "shard"), split_axis=0, concat_axis=0, tiled=True)


def to_experts(arrived, local_experts, capacity):
    sources = arrived.shape[0]
    model_width = arrived.shape[2]
    split_rows = arrived.reshape(sources, local_experts, capacity, model_width)
    return jnp.swapaxes(split_rows, 0, 1).reshape(local_experts, sources * capacity, model_width)


def from_experts(expert_token_rows, owners, capacity):
    local_experts = expert_token_rows.shape[0]
    model_width = expert_token_rows.shape[2]
    split_rows = expert_token_rows.reshape(local_experts, owners, capacity, model_width)
    return jnp.swapaxes(split_rows, 0, 1).reshape(owners, local_experts * capacity, model_width)


def local(
    tokens,
    cotangent,
    lengths,
    routes,
    w_query,
    w_key,
    w_value,
    w_out,
    w_router,
    g_attn,
    g_ffn,
    g_query,
    g_key,
    w_gate,
    w_up,
    w_down,
):
    micro_count = tokens.shape[0]
    seq_len = tokens.shape[2]
    model_width = tokens.shape[3]
    top_count = routes.shape[3]
    expert_count = w_router.shape[1]
    local_experts = w_gate.shape[0]
    owners = expert_count // local_experts
    capacity = min(seq_len, max(2, 2 * seq_len * top_count // expert_count))
    slot_total = expert_count * capacity
    gate_weight_complete, up_weight_complete, down_weight_complete = (
        lax.all_gather(w_gate, "dp", axis=2, tiled=True),
        lax.all_gather(w_up, "dp", axis=2, tiled=True),
        lax.all_gather(w_down, "dp", axis=1, tiled=True),
    )
    cosine_table, sine_table = rope_tables(seq_len, HDIM)
    places = jnp.arange(seq_len)
    slot_ids = jnp.arange(slot_total)
    expert_ids = jnp.arange(expert_count)
    score_scale = HDIM ** (-0.5)
    grad_query = jnp.zeros((model_width, model_width), jnp.float32)
    grad_key = jnp.zeros((model_width, model_width), jnp.float32)
    grad_value = jnp.zeros((model_width, model_width), jnp.float32)
    grad_out = jnp.zeros((model_width, model_width), jnp.float32)
    grad_router = jnp.zeros((model_width, expert_count), jnp.float32)
    grad_gain_attn = jnp.zeros((model_width,), jnp.float32)
    grad_gain_ffn = jnp.zeros((model_width,), jnp.float32)
    grad_gain_query = jnp.zeros((model_width,), jnp.float32)
    grad_gain_key = jnp.zeros((model_width,), jnp.float32)
    grad_gate = jnp.zeros(gate_weight_complete.shape, jnp.float32)
    grad_up = jnp.zeros(up_weight_complete.shape, jnp.float32)
    grad_down = jnp.zeros(down_weight_complete.shape, jnp.float32)
    outs_mixed = []
    outs_grad = []
    for micro_step in range(micro_count):
        layer_set = (
            lax.all_gather(w_query, "shard", axis=0, tiled=True),
            lax.all_gather(w_key, "shard", axis=0, tiled=True),
            lax.all_gather(w_value, "shard", axis=0, tiled=True),
            lax.all_gather(w_out, "shard", axis=0, tiled=True),
            lax.all_gather(w_router, "shard", axis=0, tiled=True),
            lax.all_gather(g_attn, "shard", axis=0, tiled=True),
            lax.all_gather(g_ffn, "shard", axis=0, tiled=True),
            lax.all_gather(g_query, "shard", axis=0, tiled=True),
            lax.all_gather(g_key, "shard", axis=0, tiled=True),
        )
        query_full, key_full, value_full, out_full, route_full = (
            layer_set[0],
            layer_set[1],
            layer_set[2],
            layer_set[3],
            layer_set[4],
        )
        gain_attn = layer_set[5].astype(jnp.float32)
        gain_ffn = layer_set[6].astype(jnp.float32)
        gain_query = layer_set[7].astype(jnp.float32)
        gain_key = layer_set[8].astype(jnp.float32)
        inputs = tokens[micro_step, 0].astype(jnp.float32)
        length = lengths[micro_step, 0]
        route_ids = routes[micro_step, 0]
        normed = rms_norm(inputs, gain_attn).astype(jnp.bfloat16)
        query_raw = matmul(normed, query_full)
        key_raw = matmul(normed, key_full)
        value_raw = matmul(normed, value_full)
        value_low = value_raw.astype(jnp.bfloat16).reshape(seq_len, HEADS, HDIM)
        query_low = rotate(
            rms_norm(query_raw, gain_query).reshape(seq_len, HEADS, HDIM), cosine_table, sine_table
        ).astype(jnp.bfloat16)
        key_low = rotate(
            rms_norm(key_raw, gain_key).reshape(seq_len, HEADS, HDIM), cosine_table, sine_table
        ).astype(jnp.bfloat16)
        allowed = (places[None, :] <= places[:, None]) & (places[None, :] < length)
        scores = (
            jnp.einsum("qhd,khd->hqk", query_low, key_low, preferred_element_type=jnp.float32)
            * score_scale
        )
        attn_probs = softmax_rows(jnp.where(allowed[None], scores, -1e30))
        probs_low = attn_probs.astype(jnp.bfloat16)
        mixed_low = (
            jnp.einsum("hqk,khd->qhd", probs_low, value_low, preferred_element_type=jnp.float32)
            .reshape(seq_len, model_width)
            .astype(jnp.bfloat16)
        )
        attn_part = matmul(mixed_low, out_full)
        hidden_state = inputs + attn_part
        ffn_in = rms_norm(hidden_state, gain_ffn).astype(jnp.bfloat16)
        logits = matmul(ffn_in, route_full)
        router = softmax_rows(logits)
        chosen = route_ids[:, :, None] == expert_ids[None, None, :]
        gate_vals = jnp.sum(jnp.where(chosen, router[:, None, :], 0.0), axis=2)
        flat_chosen = chosen.reshape(seq_len * top_count, expert_count).astype(jnp.int32)
        before = jnp.cumsum(flat_chosen, axis=0) - flat_chosen
        slot_rank = jnp.sum(before * flat_chosen, axis=1)
        target = route_ids.reshape(-1) * capacity + slot_rank
        placing = (slot_ids[:, None] == target[None, :]).astype(jnp.bfloat16)
        token_placing = jnp.sum(placing.reshape(slot_total, seq_len, top_count), axis=2)
        outgoing = matmul(token_placing, ffn_in).astype(jnp.bfloat16)
        arrived = dispatch_rows(outgoing.reshape(owners, local_experts * capacity, model_width))
        expert_token_rows = to_experts(arrived, local_experts, capacity)
        gate_pre = jnp.einsum(
            "qjs,qsy->qjy",
            expert_token_rows,
            gate_weight_complete,
            preferred_element_type=jnp.float32,
        )
        up_value = jnp.einsum(
            "qjs,qsy->qjy",
            expert_token_rows,
            up_weight_complete,
            preferred_element_type=jnp.float32,
        )
        sigmoid_gate = jax.nn.sigmoid(gate_pre)
        activated = gate_pre * sigmoid_gate
        inner_activation = (activated * up_value).astype(jnp.bfloat16)
        expert_out = jnp.einsum(
            "aqc,aco->aqo",
            inner_activation,
            down_weight_complete,
            preferred_element_type=jnp.float32,
        ).astype(jnp.bfloat16)
        returned = collect_rows(from_experts(expert_out, owners, capacity)).reshape(
            slot_total, model_width
        )
        picked = (
            jnp.take(returned, target, axis=0)
            .astype(jnp.float32)
            .reshape(seq_len, top_count, model_width)
        )
        expert_sum = jnp.sum(picked * gate_vals[:, :, None], axis=1)
        outs_mixed.append((hidden_state + expert_sum).astype(jnp.bfloat16))
        live_mask = (places < length).astype(jnp.float32)
        d_output = cotangent[micro_step, 0].astype(jnp.float32) * live_mask[:, None]
        d_gates = jnp.sum(picked * d_output[:, None, :], axis=2)
        d_slots = (
            (gate_vals[:, :, None] * d_output[:, None, :])
            .astype(jnp.bfloat16)
            .reshape(seq_len * top_count, model_width)
        )
        d_outgoing = matmul(placing, d_slots).astype(jnp.bfloat16)
        d_arrived = dispatch_grads(
            d_outgoing.reshape(owners, local_experts * capacity, model_width)
        )
        expert_output_gradient = to_experts(d_arrived, local_experts, capacity)
        d_inner = jnp.einsum(
            "azy,ajy->azj",
            expert_output_gradient,
            down_weight_complete,
            preferred_element_type=jnp.float32,
        )
        grad_down = grad_down + jnp.einsum(
            "qti,qtj->qij",
            inner_activation,
            expert_output_gradient,
            preferred_element_type=jnp.float32,
        )
        gate_preactivation_gradient = (
            d_inner * up_value * (sigmoid_gate + gate_pre * sigmoid_gate * (1.0 - sigmoid_gate))
        ).astype(jnp.bfloat16)
        up_projection_value_gradient = (d_inner * activated).astype(jnp.bfloat16)
        grad_gate = grad_gate + jnp.einsum(
            "hzo,hzg->hog",
            expert_token_rows,
            gate_preactivation_gradient,
            preferred_element_type=jnp.float32,
        )
        grad_up = grad_up + jnp.einsum(
            "hzo,hzg->hog",
            expert_token_rows,
            up_projection_value_gradient,
            preferred_element_type=jnp.float32,
        )
        d_rows = jnp.einsum(
            "ing,itg->int",
            gate_preactivation_gradient,
            gate_weight_complete,
            preferred_element_type=jnp.float32,
        )
        d_rows = (
            d_rows
            + jnp.einsum(
                "ing,itg->int",
                up_projection_value_gradient,
                up_weight_complete,
                preferred_element_type=jnp.float32,
            )
        ).astype(jnp.bfloat16)
        d_returned = collect_grads(from_experts(d_rows, owners, capacity)).reshape(
            slot_total, model_width
        )
        d_ffn_in = jnp.sum(
            jnp.take(d_returned, target, axis=0)
            .astype(jnp.float32)
            .reshape(seq_len, top_count, model_width),
            axis=1,
        )
        d_router = jnp.sum(jnp.where(chosen, d_gates[:, :, None], 0.0), axis=1)
        d_logits = (router * (d_router - jnp.sum(router * d_router, axis=1, keepdims=True))).astype(
            jnp.bfloat16
        )
        grad_router = grad_router + transposed_times(ffn_in, d_logits)
        d_ffn_in = d_ffn_in + times_transposed(d_logits, route_full)
        d_hidden_norm, d_gain_ffn = norm_back(hidden_state, gain_ffn, d_ffn_in)
        grad_gain_ffn = grad_gain_ffn + d_gain_ffn
        d_hidden = d_output + d_hidden_norm
        d_attn_low = d_hidden.astype(jnp.bfloat16)
        grad_out = grad_out + transposed_times(mixed_low, d_attn_low)
        d_mixed_wide = times_transposed(d_attn_low, out_full)
        d_mixed = d_mixed_wide.astype(jnp.bfloat16).reshape(seq_len, HEADS, HDIM)
        d_probs = jnp.einsum("qhd,khd->hqk", d_mixed, value_low, preferred_element_type=jnp.float32)
        d_value = (
            jnp.einsum("hqk,qhd->khd", probs_low, d_mixed, preferred_element_type=jnp.float32)
            .reshape(seq_len, model_width)
            .astype(jnp.bfloat16)
        )
        d_scores = (
            attn_probs * (d_probs - jnp.sum(attn_probs * d_probs, axis=-1, keepdims=True))
        ).astype(jnp.bfloat16)
        d_query = (
            jnp.einsum("hqk,khd->qhd", d_scores, key_low, preferred_element_type=jnp.float32)
            * score_scale
        )
        d_key = (
            jnp.einsum("hqk,qhd->khd", d_scores, query_low, preferred_element_type=jnp.float32)
            * score_scale
        )
        d_query_raw, d_gain_query = norm_back(
            query_raw,
            gain_query,
            rotate_back(d_query, cosine_table, sine_table).reshape(seq_len, model_width),
        )
        d_key_raw, d_gain_key = norm_back(
            key_raw,
            gain_key,
            rotate_back(d_key, cosine_table, sine_table).reshape(seq_len, model_width),
        )
        grad_gain_query = grad_gain_query + d_gain_query
        grad_gain_key = grad_gain_key + d_gain_key
        d_query_low = d_query_raw.astype(jnp.bfloat16)
        d_key_low = d_key_raw.astype(jnp.bfloat16)
        grad_query = grad_query + transposed_times(normed, d_query_low)
        grad_key = grad_key + transposed_times(normed, d_key_low)
        grad_value = grad_value + transposed_times(normed, d_value)
        d_normed = (
            times_transposed(d_query_low, query_full)
            + times_transposed(d_key_low, key_full)
            + times_transposed(d_value, value_full)
        )
        d_input_norm, d_gain_attn = norm_back(inputs, gain_attn, d_normed)
        grad_gain_attn = grad_gain_attn + d_gain_attn
        outs_grad.append(d_hidden + d_input_norm)
    layer_sums = (
        lax.psum_scatter(
            grad_query.astype(jnp.bfloat16), "shard", scatter_dimension=0, tiled=True
        ).astype(jnp.float32),
        lax.psum_scatter(
            grad_key.astype(jnp.bfloat16), "shard", scatter_dimension=0, tiled=True
        ).astype(jnp.float32),
        lax.psum_scatter(
            grad_value.astype(jnp.bfloat16), "shard", scatter_dimension=0, tiled=True
        ).astype(jnp.float32),
        lax.psum_scatter(
            grad_out.astype(jnp.bfloat16), "shard", scatter_dimension=0, tiled=True
        ).astype(jnp.float32),
        lax.psum_scatter(
            grad_router.astype(jnp.bfloat16), "shard", scatter_dimension=0, tiled=True
        ).astype(jnp.float32),
        lax.psum_scatter(
            grad_gain_attn.astype(jnp.bfloat16), "shard", scatter_dimension=0, tiled=True
        ).astype(jnp.float32),
        lax.psum_scatter(
            grad_gain_ffn.astype(jnp.bfloat16), "shard", scatter_dimension=0, tiled=True
        ).astype(jnp.float32),
        lax.psum_scatter(
            grad_gain_query.astype(jnp.bfloat16), "shard", scatter_dimension=0, tiled=True
        ).astype(jnp.float32),
        lax.psum_scatter(
            grad_gain_key.astype(jnp.bfloat16), "shard", scatter_dimension=0, tiled=True
        ).astype(jnp.float32),
    )
    layer_totals = (
        lax.psum(layer_sums[0].astype(jnp.bfloat16), ("dp", "expert")).astype(jnp.float32),
        lax.psum(layer_sums[1].astype(jnp.bfloat16), ("dp", "expert")).astype(jnp.float32),
        lax.psum(layer_sums[2].astype(jnp.bfloat16), ("dp", "expert")).astype(jnp.float32),
        lax.psum(layer_sums[3].astype(jnp.bfloat16), ("dp", "expert")).astype(jnp.float32),
        lax.psum(layer_sums[4].astype(jnp.bfloat16), ("dp", "expert")).astype(jnp.float32),
        lax.psum(layer_sums[5].astype(jnp.bfloat16), ("dp", "expert")).astype(jnp.float32),
        lax.psum(layer_sums[6].astype(jnp.bfloat16), ("dp", "expert")).astype(jnp.float32),
        lax.psum(layer_sums[7].astype(jnp.bfloat16), ("dp", "expert")).astype(jnp.float32),
        lax.psum(layer_sums[8].astype(jnp.bfloat16), ("dp", "expert")).astype(jnp.float32),
    )
    expert_totals = (
        lax.psum_scatter(
            grad_gate.astype(jnp.bfloat16), "dp", scatter_dimension=2, tiled=True
        ).astype(jnp.float32),
        lax.psum_scatter(
            grad_up.astype(jnp.bfloat16), "dp", scatter_dimension=2, tiled=True
        ).astype(jnp.float32),
        lax.psum_scatter(
            grad_down.astype(jnp.bfloat16), "dp", scatter_dimension=1, tiled=True
        ).astype(jnp.float32),
    )
    mixed_out = jnp.stack(outs_mixed)[:, None]
    grad_tokens = jnp.stack(outs_grad)[:, None]
    return (
        mixed_out,
        grad_tokens,
        layer_totals[0],
        layer_totals[1],
        layer_totals[2],
        layer_totals[3],
        layer_totals[4],
        layer_totals[5],
        layer_totals[6],
        layer_totals[7],
        layer_totals[8],
        expert_totals[0],
        expert_totals[1],
        expert_totals[2],
    )


def solution(mesh):
    placed = (
        P(None, ("dp", "expert", "shard"), None, None),
        P(None, ("dp", "expert", "shard"), None, None),
        P(None, ("dp", "expert", "shard")),
        P(None, ("dp", "expert", "shard"), None, None),
        P("shard", None),
        P("shard", None),
        P("shard", None),
        P("shard", None),
        P("shard", None),
        P("shard"),
        P("shard"),
        P("shard"),
        P("shard"),
        P(("expert", "shard"), None, "dp"),
        P(("expert", "shard"), None, "dp"),
        P(("expert", "shard"), "dp", None),
    )
    return jax.shard_map(
        local,
        mesh=mesh,
        in_specs=placed,
        out_specs=(
            P(None, ("dp", "expert", "shard"), None, None),
            P(None, ("dp", "expert", "shard"), None, None),
            P("shard", None),
            P("shard", None),
            P("shard", None),
            P("shard", None),
            P("shard", None),
            P("shard"),
            P("shard"),
            P("shard"),
            P("shard"),
            P(("expert", "shard"), None, "dp"),
            P(("expert", "shard"), None, "dp"),
            P(("expert", "shard"), "dp", None),
        ),
        check_vma=False,
    )
```

profile of v0, /device:TPU:13, one launch (start us, length us, event | category | flops | bytes accessed | tf_op | source)
XLA Modules:
  0.0 2437.4 jit_solution(535213645135037954)
XLA Ops:
  11.6 9.5 all-gather
  21.3 9.1 all-gather.2
  30.5 12.5 all-gather.1
  44.9 15.0 all-gather.3
  63.7 94.3 %all-gather.16.cloned.1.call-done = bf16[2048,2048]{1,0:T(8,128)(2,1)} async-done(((bf16[512,2048]{1,0:T(8,128)(2,1)}), bf16[2048,2048]{1,0:T(8,128)(2,1)}) %all-gather.16.cloned.1.call-update) | async-done | bytes 8388624 | tf_op jit(solution)/shard_map/all_gather | solution.py:155
  167.7 139.8 %all-gather.14.cloned.1.call-done = bf16[2048,2048]{1,0:T(8,128)(2,1)} async-done(((bf16[512,2048]{1,0:T(8,128)(2,1)}), bf16[2048,2048]{1,0:T(8,128)(2,1)}) %all-gather.14.cloned.1.call-update) | async-done | bytes 8388624 | tf_op jit(solution)/shard_map/all_gather | solution.py:154
  319.1 138.0 %all-gather.12.cloned.1.call-done = bf16[2048,2048]{1,0:T(8,128)(2,1)} async-done(((bf16[512,2048]{1,0:T(8,128)(2,1)}), bf16[2048,2048]{1,0:T(8,128)(2,1)}) %all-gather.12.cloned.1.call-update) | async-done | bytes 8388624 | tf_op jit(solution)/shard_map/all_gather | solution.py:156
  462.5 144.0 %all-gather.18.cloned.1.call-done = bf16[2048,2048]{1,0:T(8,128)(2,1)} async-done(((bf16[512,2048]{1,0:T(8,128)(2,1)}), bf16[2048,2048]{1,0:T(8,128)(2,1)}) %all-gather.18.cloned.1.call-update) | async-done | bytes 8388624 | tf_op jit(solution)/shard_map/all_gather | solution.py:157
  615.0 7.8 all-to-all-start
  624.1 93.9 %all-to-all-done = bf16[16,64,2048]{2,1,0:T(8,128)(2,1)} async-done(((bf16[16,64,2048]{2,1,0:T(8,128)(2,1)}), bf16[16,64,2048]{2,1,0:T(8,128)(2,1)}, u32[]{:S(2)}, u32[]{:S(2)}) %all-to-all-start) | async-done | bytes 4194336 | tf_op jit(solution)/shard_map/all_to_all | solution.py:72
  718.1 10.0 fusion.35
  728.0 12.1 multiply_convert_fusion.5
  740.1 9.3 fusion.37
  749.5 8.4 all-to-all-start.1
  757.8 97.4 %all_gather.56 = bf16[2048,16]{0,1:T(8,128)(2,1)S(1)} all-gather(bf16[512,16]{0,1:T(8,128)(2,1)S(1)} %copy-done.91), channel_id=1, replica_groups=mesh['dp'=2,'expert'=4,'shard'=4] {'shard'}, dimensions={0}, use_global_device_ids=true | all-gather | bytes 81920 | tf_op jit(solution)/shard_map/all_gather | solution.py:158
  872.0 101.5 %all_to_all.40 = bf16[16,64,2048]{2,1,0:T(8,128)(2,1)S(1)} all-to-all(bf16[16,64,2048]{2,1,0:T(8,128)(2,1)S(1)} %bitcast.544), channel_id=1, replica_groups=mesh['dp'=2,'expert'=4,'shard'=4] {'expert','shard'}, dimensions={0} | all-to-all | bytes 8388608 | tf_op jit(solution)/shard_map/all_to_all | solution.py:80
  973.4 10.6 multiply_convert_fusion.3
  990.4 7.7 add_convert_fusion.8
  998.1 8.2 all-to-all-start.5
  1039.7 57.9 %all-to-all-done.5 = bf16[16,64,2048]{2,1,0:T(8,128)(2,1)} async-done(((bf16[16,64,2048]{2,1,0:T(8,128)(2,1)}), bf16[16,64,2048]{2,1,0:T(8,128)(2,1)}, u32[]{:S(2)}, u32[]{:S(2)}) %all-to-all-start.5) | async-done | bytes 4194336 | tf_op jit(solution)/shard_map/all_to_all | solution.py:84
  1097.6 8.2 gather_fusion.2
  1115.3 97.9 %all_to_all.41 = bf16[16,64,2048]{2,1,0:T(8,128)(2,1)S(1)} all-to-all(bf16[16,64,2048]{2,1,0:T(8,128)(2,1)S(1)} %bitcast.517), channel_id=1, replica_groups=mesh['dp'=2,'expert'=4,'shard'=4] {'expert','shard'}, dimensions={0} | all-to-all | bytes 8388608 | tf_op jit(solution)/shard_map/all_to_all | solution.py:72
  1230.2 8.3 all-to-all-start.3
  1238.9 91.0 %all-to-all-done.3 = bf16[16,64,2048]{2,1,0:T(8,128)(2,1)} async-done(((bf16[16,64,2048]{2,1,0:T(8,128)(2,1)}), bf16[16,64,2048]{2,1,0:T(8,128)(2,1)}, u32[]{:S(2)}, u32[]{:S(2)}) %all-to-all-start.3) | async-done | bytes 4194336 | tf_op jit(solution)/shard_map/all_to_all | solution.py:76
  1344.7 104.3 %all_to_all.42 = bf16[16,64,2048]{2,1,0:T(8,128)(2,1)S(1)} all-to-all(bf16[16,64,2048]{2,1,0:T(8,128)(2,1)S(1)} %bitcast.545), channel_id=1, replica_groups=mesh['dp'=2,'expert'=4,'shard'=4] {'expert','shard'}, dimensions={0} | all-to-all | bytes 8388608 | tf_op jit(solution)/shard_map/all_to_all | solution.py:80
  1449.0 10.6 multiply_convert_fusion.1
  1466.0 7.7 add_convert_fusion.7
  1473.7 7.7 all-to-all-start.7
  1482.0 90.9 %all-to-all-done.7 = bf16[16,64,2048]{2,1,0:T(8,128)(2,1)} async-done(((bf16[16,64,2048]{2,1,0:T(8,128)(2,1)}), bf16[16,64,2048]{2,1,0:T(8,128)(2,1)}, u32[]{:S(2)}, u32[]{:S(2)}) %all-to-all-start.7) | async-done | bytes 4194336 | tf_op jit(solution)/shard_map/all_to_all | solution.py:84
  1572.9 8.2 gather_fusion.3
  1604.0 8.7 fusion.207
  1612.7 11.5 add_convert_fusion.3
  1628.5 8.3 fusion.205
  1636.7 12.3 add_convert_fusion.2
  1653.1 8.3 fusion.129
  1661.3 11.6 add_convert_fusion.1
  1673.8 8.2 fusion.137
  1682.0 11.5 add_convert_fusion
  1694.6 11.0 fusion.225
  1706.5 12.2 fusion.10
  1719.2 7.2 fusion.226
  1760.0 15.6 reduce-scatter.9.cloned.1.call-done
  1775.5 147.6 %reduce-scatter.11.cloned.1.call-done = bf16[512,2048]{1,0:T(8,128)(2,1)} async-done(((bf16[2048,2048]{1,0:T(8,128)(2,1)}), bf16[512,2048]{1,0:T(8,128)(2,1)}) %reduce-scatter.11.cloned.1.call-update) | async-done | bytes 2097168 | tf_op jit(solution)/shard_map/reduce_scatter | solution.py:372
  1923.1 147.4 %reduce-scatter.13.cloned.1.call-done = bf16[512,2048]{1,0:T(8,128)(2,1)} async-done(((bf16[2048,2048]{1,0:T(8,128)(2,1)}), bf16[512,2048]{1,0:T(8,128)(2,1)}) %reduce-scatter.13.cloned.1.call-update) | async-done | bytes 2097168 | tf_op jit(solution)/shard_map/reduce_scatter | solution.py:375
  2070.6 147.6 %reduce-scatter.15.cloned.1.call-done = bf16[512,2048]{1,0:T(8,128)(2,1)} async-done(((bf16[2048,2048]{1,0:T(8,128)(2,1)}), bf16[512,2048]{1,0:T(8,128)(2,1)}) %reduce-scatter.15.cloned.1.call-update) | async-done | bytes 2097168 | tf_op jit(solution)/shard_map/reduce_scatter | solution.py:378
  2237.2 11.7 all-reduce.6
  2249.2 28.3 %all-reduce.4 = (bf16[512,16]{0,1:T(8,128)(2,1)S(1)}, bf16[512]{0:T(512)(128)(2,1)S(1)}, bf16[512]{0:T(512)(128)(2,1)S(1)}, bf16[512]{0:T(512)(128)(2,1)S(1)}, bf16[512]{0:T(512)(128)(2,1)S(1)}) all-reduce(bf16[512,16]{0,1:T(8,128)(2,1)} %reduce-scatter.17.cloned.1.call-done, ...), channel_id=1, replica_groups=mesh['dp'=2,'expert'=4,'shard'=4] {'dp','expert'}, use_global_device_ids=true, to_apply=%region_55.57 | all-reduce | flops 10240 | bytes 40960 | tf_op jit(solution)/shard_map/psum | solution.py:402
  2296.8 122.0 %all-reduce.9.cloned.1.call-done = (bf16[512,2048]{1,0:T(8,128)(2,1)}, bf16[512,2048]{1,0:T(8,128)(2,1)}, bf16[512,2048]{1,0:T(8,128)(2,1)}, bf16[512,2048]{1,0:T(8,128)(2,1)}) async-done(((bf16[512,2048]{1,0:T(8,128)(2,1)}, bf16[512,2048]{1,0:T(8,128)(2,1)}, bf16[512,2048]{1,0:T(8,128)(2,1)}, bf16[512,2048]{1,0:T(8,128)(2,1)}), (bf16[512,2048]{1,0:T(8,128)(2,1)}, bf16[512,2048]{1,0:T(8,128)(2,1)}, ...) | async-done | bytes 8388624 | tf_op jit(solution)/shard_map/psum | solution.py:398
  (538 shorter events, 267.9 us)
Async XLA Ops:
  7.2 150.8 %all-gather.16.cloned.1.call-start = ((), (), s32[]{:S(2)}) async-start(), calls=%async_computation.18 | async-start | bytes 10485760 | tf_op jit(solution)/shard_map/all_gather | solution.py:155
  8.0 299.5 %all-gather.14.cloned.1.call-start = ((), (), s32[]{:S(2)}) async-start(), calls=%async_computation.17 | async-start | bytes 10485760 | tf_op jit(solution)/shard_map/all_gather | solution.py:154
  8.7 448.3 %all-gather.12.cloned.1.call-start = ((), (), s32[]{:S(2)}) async-start(), calls=%async_computation.16 | async-start | bytes 10485760 | tf_op jit(solution)/shard_map/all_gather | solution.py:156
  9.5 596.9 %all-gather.18.cloned.1.call-start = ((), (), s32[]{:S(2)}) async-start(), calls=%async_computation.19 | async-start | bytes 10485760 | tf_op jit(solution)/shard_map/all_gather | solution.py:157
  10.0 614.1 %all-gather.20.cloned.1.call-start = ((), (), s32[]{:S(2)}) async-start(), calls=%async_computation.20 | async-start | bytes 6291456 | tf_op jit(solution)/shard_map/all_gather | solution.py:129
  21.3 286.2 %copy-start.69 = (f32[64]{0:T(128)}, f32[64]{0:T(128)S(1)}, u32[]{:S(2)}) copy-start(f32[64]{0:T(128)S(1)} %add_rsqrt_fusion.7) | copy-start | bytes 772
  30.5 135.1 %copy-start.59 = (f32[4,1,512]{2,1,0:T(1,128)}, f32[4,1,512]{2,1,0:T(1,128)S(1)}, u32[]{:S(2)}) copy-start(f32[4,1,512]{2,1,0:T(1,128)S(1)} %convert_element_type.523) | copy-start | bytes 24580
  30.5 282.3 %copy-start.72 = (f32[64]{0:T(128)}, f32[64]{0:T(128)S(1)}, u32[]{:S(2)}) copy-start(f32[64]{0:T(128)S(1)} %add_rsqrt_fusion.3) | copy-start | bytes 772
  43.0 272.1 %copy-start.61 = (f32[4,1,512]{2,1,0:T(1,128)}, f32[4,1,512]{2,1,0:T(1,128)S(1)}, u32[]{:S(2)}) copy-start(f32[4,1,512]{2,1,0:T(1,128)S(1)} %convert_element_type.522) | copy-start | bytes 24580
  165.5 147.3 %copy-start.108 = (f32[64]{0:T(128)}, f32[64]{0:T(128)S(1)}, u32[]{:S(2)}) copy-start(f32[64]{0:T(128)S(1)} %add_rsqrt_fusion.1) | copy-start | bytes 772
  317.8 144.3 %copy-start.27 = (bf16[64,16,128]{2,0,1:T(8,128)(2,1)}, bf16[64,16,128]{2,0,1:T(8,128)(2,1)S(1)}, u32[]{:S(2)}) copy-start(bf16[64,16,128]{2,0,1:T(8,128)(2,1)S(1)} %get-tuple-element.147) | copy-start | bytes 786436
  317.8 144.3 %copy-start.29 = (bf16[64,16,128]{2,0,1:T(8,128)(2,1)}, bf16[64,16,128]{2,0,1:T(8,128)(2,1)S(1)}, u32[]{:S(2)}) copy-start(bf16[64,16,128]{2,0,1:T(8,128)(2,1)S(1)} %get-tuple-element.144) | copy-start | bytes 786436
  318.1 144.0 %copy-start.39 = (f32[16,64,64]{1,2,0:T(8,128)}, f32[16,64,64]{1,2,0:T(8,128)S(1)}, u32[]{:S(2)}) copy-start(f32[16,64,64]{1,2,0:T(8,128)S(1)} %fusion.63) | copy-start | bytes 786436
  319.1 143.1 %copy-start.79 = (f32[16,64]{1,0:T(8,128)}, f32[16,64]{1,0:T(8,128)S(1)}, u32[]{:S(2)}) copy-start(f32[16,64]{1,0:T(8,128)S(1)} %get-tuple-element.183) | copy-start | bytes 12292
  462.1 149.4 %copy-start.52 = (bf16[8,16,8,128]{3,2,1,0:T(8,128)(2,1)}, bf16[8,16,8,128]{3,2,1,0:T(8,128)(2,1)S(1)}, u32[]{:S(2)}) copy-start(bf16[8,16,8,128]{3,2,1,0:T(8,128)(2,1)S(1)} %fusion.68) | copy-start | bytes 786436
  462.5 149.1 %copy-start.32 = (bf16[16,8,8,128]{3,2,1,0:T(8,128)(2,1)}, bf16[16,8,8,128]{3,2,1,0:T(8,128)(2,1)S(1)}, u32[]{:S(2)}) copy-start(bf16[16,8,8,128]{3,2,1,0:T(8,128)(2,1)S(1)} %fusion.64) | copy-start | bytes 786436
  611.7 246.6 %copy-start.21 = (bf16[64,2048]{1,0:T(8,128)(2,1)}, bf16[64,2048]{1,0:T(8,128)(2,1)S(1)}, u32[]{:S(2)}) copy-start(bf16[64,2048]{1,0:T(8,128)(2,1)S(1)} %multiply_convert_fusion.13) | copy-start | bytes 786436
  615.0 103.1 %all-to-all-start = ((bf16[16,64,2048]{2,1,0:T(8,128)(2,1)}), bf16[16,64,2048]{2,1,0:T(8,128)(2,1)}, u32[]{:S(2)}, u32[]{:S(2)}) async-start(bf16[16,64,2048]{2,1,0:T(8,128)(2,1)} %bitcast.516), calls=%async_computation | async-start | bytes 8388608 | tf_op jit(solution)/shard_map/all_to_all | solution.py:72
  622.8 105.3 %all-gather.22.cloned.1.call-start = ((), (), s32[]{:S(2)}) async-start(), calls=%async_computation.21 | async-start | bytes 6291456 | tf_op jit(solution)/shard_map/all_gather | solution.py:130
  623.4 116.8 %all-gather.24.cloned.1.call-start = ((), (), s32[]{:S(2)}) async-start(), calls=%async_computation.22 | async-start | bytes 6291456 | tf_op jit(solution)/shard_map/all_gather | solution.py:131
  749.5 107.0 %copy-start.84 = (s32[512]{0:T(512)S(1)}, s32[512]{0:T(512)}, u32[]{:S(2)}) copy-start(s32[512]{0:T(512)} %copy-done.83) | copy-start | bytes 6148
  749.5 107.0 %copy-start.86 = (s32[512]{0:T(512)S(1)}, s32[512]{0:T(512)}, u32[]{:S(2)}) copy-start(s32[512]{0:T(512)} %copy-done.85) | copy-start | bytes 6148
  749.5 107.7 %copy-start.44 = (bf16[2,1,64,2048]{3,2,1,0:T(8,128)(2,1)S(1)}, bf16[2,1,64,2048]{3,2,1,0:T(8,128)(2,1)}, u32[]{:S(2)}) copy-start(bf16[2,1,64,2048]{3,2,1,0:T(8,128)(2,1)} %param.19) | copy-start | bytes 1572868
  749.5 109.1 %all-to-all-start.1 = ((bf16[16,64,2048]{2,1,0:T(8,128)(2,1)}), bf16[16,64,2048]{2,1,0:T(8,128)(2,1)}, u32[]{:S(2)}, u32[]{:S(2)}) async-start(bf16[16,64,2048]{2,1,0:T(8,128)(2,1)} %bitcast.541), calls=%async_computation.1 | async-start | bytes 8388608 | tf_op jit(solution)/shard_map/all_to_all | solution.py:76
  871.9 101.5 %copy-start.138 = (bf16[1,1024,2048]{2,1,0:T(8,128)(2,1)S(1)}, bf16[1,1024,2048]{2,1,0:T(8,128)(2,1)}, u32[]{:S(2)}) copy-start(bf16[1,1024,2048]{2,1,0:T(8,128)(2,1)} %all-gather.24.cloned.1.call-done) | copy-start | bytes 12582916
  872.0 101.5 %copy-start.142 = (f32[1024,1024]{1,0:T(8,128)S(1)}, f32[1024,1024]{1,0:T(8,128)}, u32[]{:S(2)}) copy-start(f32[1024,1024]{1,0:T(8,128)} %fusion.35) | copy-start | bytes 12582916
  998.1 99.5 %all-to-all-start.5 = ((bf16[16,64,2048]{2,1,0:T(8,128)(2,1)}), bf16[16,64,2048]{2,1,0:T(8,128)(2,1)}, u32[]{:S(2)}, u32[]{:S(2)}) async-start(bf16[16,64,2048]{2,1,0:T(8,128)(2,1)} %bitcast.540), calls=%async_computation.5 | async-start | bytes 8388608 | tf_op jit(solution)/shard_map/all_to_all | solution.py:84
  1033.1 64.5 %copy-start.90 = (s32[1024]{0:T(1024)S(1)}, s32[1024]{0:T(1024)}, u32[]{:S(2)}) copy-start(s32[1024]{0:T(1024)} %copy-done.89) | copy-start | bytes 12292
  1039.7 72.5 %copy-start.74 = (bf16[64,16]{0,1:T(8,128)(2,1)}, bf16[64,16]{0,1:T(8,128)(2,1)S(1)}, u32[]{:S(2)}) copy-start(bf16[64,16]{0,1:T(8,128)(2,1)S(1)} %multiply_convert_fusion.15) | copy-start | bytes 6148
  1114.0 124.6 %copy-start.14 = (bf16[64,2048]{1,0:T(8,128)(2,1)}, bf16[64,2048]{1,0:T(8,128)(2,1)S(1)}, u32[]{:S(2)}) copy-start(bf16[64,2048]{1,0:T(8,128)(2,1)S(1)} %get-tuple-element.162) | copy-start | bytes 786436
  1115.3 97.9 %copy-start.133 = (bf16[1,2048,1024]{2,1,0:T(8,128)(2,1)S(1)}, bf16[1,2048,1024]{2,1,0:T(8,128)(2,1)}, u32[]{:S(2)}) copy-start(bf16[1,2048,1024]{2,1,0:T(8,128)(2,1)} %all-gather.20.cloned.1.call-done) | copy-start | bytes 12582916
  1230.2 99.7 %all-to-all-start.3 = ((bf16[16,64,2048]{2,1,0:T(8,128)(2,1)}), bf16[16,64,2048]{2,1,0:T(8,128)(2,1)}, u32[]{:S(2)}, u32[]{:S(2)}) async-start(bf16[16,64,2048]{2,1,0:T(8,128)(2,1)} %bitcast.542), calls=%async_computation.3 | async-start | bytes 8388608 | tf_op jit(solution)/shard_map/all_to_all | solution.py:76
  1238.6 98.5 %copy-start.103 = (s32[512]{0:T(512)}, s32[512]{0:T(512)S(1)}, u32[]{:S(2)}) copy-start(s32[512]{0:T(512)S(1)} %get-tuple-element.115) | copy-start | bytes 6148
  1238.6 98.5 %copy-start.120 = (pred[512]{0:T(512)(128)(4,1)}, pred[512]{0:T(512)(128)(4,1)S(1)}, u32[]{:S(2)}) copy-start(pred[512]{0:T(512)(128)(4,1)S(1)} %get-tuple-element.114) | copy-start | bytes 1540
  1238.8 98.2 %copy-start.95 = (f32[64]{0:T(128)}, f32[64]{0:T(128)S(1)}, u32[]{:S(2)}) copy-start(f32[64]{0:T(128)S(1)} %get-tuple-element.198) | copy-start | bytes 772
  1238.9 98.2 %copy-start.100 = (f32[64]{0:T(128)}, f32[64]{0:T(128)S(1)}, u32[]{:S(2)}) copy-start(f32[64]{0:T(128)S(1)} %fusion.195) | copy-start | bytes 772
  1344.6 104.4 %copy-start.140 = (bf16[1,1024,2048]{2,1,0:T(8,128)(2,1)S(1)}, bf16[1,1024,2048]{2,1,0:T(8,128)(2,1)}, u32[]{:S(2)}) copy-start(bf16[1,1024,2048]{2,1,0:T(8,128)(2,1)} %all-gather.24.cloned.1.call-done) | copy-start | bytes 12582916
  1344.7 104.4 %copy-start.144 = (f32[1024,1024]{1,0:T(8,128)S(1)}, f32[1024,1024]{1,0:T(8,128)}, u32[]{:S(2)}) copy-start(f32[1024,1024]{1,0:T(8,128)} %copy-done.143) | copy-start | bytes 12582916
  1473.7 99.2 %all-to-all-start.7 = ((bf16[16,64,2048]{2,1,0:T(8,128)(2,1)}), bf16[16,64,2048]{2,1,0:T(8,128)(2,1)}, u32[]{:S(2)}, u32[]{:S(2)}) async-start(bf16[16,64,2048]{2,1,0:T(8,128)(2,1)} %bitcast.543), calls=%async_computation.7 | async-start | bytes 8388608 | tf_op jit(solution)/shard_map/all_to_all | solution.py:84
  1481.4 294.2 %reduce-scatter.9.cloned.1.call-start = ((), (), s32[]{:S(2)}) async-start(), calls=%async_computation.23 | async-start | bytes 10485760 | tf_op jit(solution)/shard_map/reduce_scatter | solution.py:369
  1624.3 298.9 %reduce-scatter.11.cloned.1.call-start = ((), (), s32[]{:S(2)}) async-start(), calls=%async_computation.24 | async-start | bytes 10485760 | tf_op jit(solution)/shard_map/reduce_scatter | solution.py:372
  1649.0 421.5 %reduce-scatter.13.cloned.1.call-start = ((), (), s32[]{:S(2)}) async-start(), calls=%async_computation.25 | async-start | bytes 10485760 | tf_op jit(solution)/shard_map/reduce_scatter | solution.py:375
  1672.9 545.2 %reduce-scatter.15.cloned.1.call-start = ((), (), s32[]{:S(2)}) async-start(), calls=%async_computation.26 | async-start | bytes 10485760 | tf_op jit(solution)/shard_map/reduce_scatter | solution.py:378
  1693.5 555.7 %reduce-scatter.17.cloned.1.call-start = ((), (), s32[]{:S(2)}) async-start(), calls=%async_computation.27 | async-start | bytes 81920 | tf_op jit(solution)/shard_map/reduce_scatter | solution.py:381
  1706.4 577.4 %reduce-scatter.19.cloned.1.call-start = ((), (), s32[]{:S(2)}) async-start(), calls=%async_computation.28 | async-start | bytes 6291456 | tf_op jit(solution)/shard_map/reduce_scatter | solution.py:409
  1718.7 569.8 %reduce-scatter.21.cloned.1.call-start = ((), (), s32[]{:S(2)}) async-start(), calls=%async_computation.29 | async-start | bytes 6291456 | tf_op jit(solution)/shard_map/reduce_scatter | solution.py:412
  1732.6 560.1 %reduce-scatter.23.cloned.1.call-start = ((), (), s32[]{:S(2)}) async-start(), calls=%async_computation.30 | async-start | bytes 6291456 | tf_op jit(solution)/shard_map/reduce_scatter | solution.py:415
  1746.0 672.8 %all-reduce.9.cloned.1.call-start = ((), (), s32[]{:S(2)}) async-start(), calls=%async_computation.31 | async-start | bytes 16777216 | tf_op jit(solution)/shard_map/psum | solution.py:398
  (127 other events, 789.8 us)
Sparse Core Ops, SparseCore 0:
  9.6 148.3 all-gather.15
  159.6 147.8 all-gather.13
  309.1 147.8 all-gather.11
  458.5 147.9 all-gather.17
  607.8 15.3 all-gather.19
  624.8 15.3 all-gather.21
  641.8 14.8 all-gather.23
  1624.4 151.0 reduce-scatter.8
  1777.9 145.1 reduce-scatter.10
  1925.3 145.1 reduce-scatter.12
  2072.9 145.1 reduce-scatter.14
  2220.8 15.5 reduce-scatter.16
  2239.4 15.3 reduce-scatter.18
  2257.5 13.3 reduce-scatter.20
  2273.8 13.3 reduce-scatter.22
  2290.9 127.8 all-reduce.8
where the time goes:
time: 2450 us; the launch traced here: 2440 us
  waiting for transfers between devices  1430 us (58%)
  blocking collectives  487 us (20%)
  matrix products  327 us (13%)
  other arithmetic  79.6 us (3%)
  local copies, waits for them, and re-layouts  50.4 us (2%)
  starting transfers between devices  41.9 us (2%)
    all_to_all x2, blocking collectives, dispatch_grads(): lax.all_to_all(buffer, ('expert', 'shard'), split_axis=0, concat_axis=0,...  206 us
    all_to_all x2, waiting for transfers between devices, collect_grads(): lax.all_to_all(buffer, ('expert', 'shard'), split_axis=0, concat_axis=0,...  149 us
    reduce_scatter x1, waiting for transfers between devices, local(): lax.psum_scatter(grad_out.astype(jnp.bfloat16), 'shard', scatter_dimensio...  148 us
    reduce_scatter x1, waiting for transfers between devices, local(): lax.psum_scatter(grad_key.astype(jnp.bfloat16), 'shard', scatter_dimensio...  148 us
    reduce_scatter x1, waiting for transfers between devices, local(): lax.psum_scatter(grad_value.astype(jnp.bfloat16), 'shard', scatter_dimens...  147 us
    all_gather x1, waiting for transfers between devices, local(): lax.all_gather(w_out, 'shard', axis=0, tiled=True)  144 us
    all_gather x1, waiting for transfers between devices, local(): lax.all_gather(w_query, 'shard', axis=0, tiled=True)  140 us
    all_gather x1, waiting for transfers between devices, local(): lax.all_gather(w_value, 'shard', axis=0, tiled=True)  138 us
  transfers between devices with their start and end apart: 21, of which 13 were waited for; matrix products, arithmetic and copies ran while one was open for 11% of the time, Pallas kernels for 0%

commit v1 on v0

--- a/solution.py
+++ b/solution.py
@@ -1,6 +1,10 @@
+import functools
+
 import jax
 import jax.numpy as jnp
 from jax import lax
+from jax.experimental import pallas as pl
+from jax.experimental.pallas import tpu as pltpu
 from jax.sharding import PartitionSpec as P
 
 HEADS = 16
@@ -68,6 +72,828 @@
     return shifted / jnp.sum(shifted, axis=-1, keepdims=True)
 
 
+MESH_ID = pl.DeviceIdType.MESH
+EXTRA = 128
+ANY = pl.BlockSpec(memory_space=pl.ANY)
+
+
+def place():
+    return lax.axis_index("dp"), lax.axis_index("expert"), lax.axis_index("shard")
+
+
+def x_of(e):
+    return e + 1 - 2 * lax.rem(e, 2)
+
+
+def y_of(e):
+    return lax.rem(e + 2, 4)
+
+
+def greet(peers):
+    barrier = pltpu.get_barrier_semaphore()
+    for peer in peers:
+        pl.semaphore_signal(barrier, inc=1, device_id=peer, device_id_type=MESH_ID)
+    pl.semaphore_wait(barrier, len(peers))
+
+
+class Copies:
+    def __init__(self):
+        self.started = []
+
+    def send(self, src, dst, send_sem, recv_sem, device, when=None):
+        copy = pltpu.make_async_remote_copy(
+            src_ref=src,
+            dst_ref=dst,
+            send_sem=send_sem,
+            recv_sem=recv_sem,
+            device_id=device,
+            device_id_type=MESH_ID,
+        )
+        if when is None:
+            copy.start()
+        else:
+            pl.when(when)(copy.start)
+        self.started.append((copy, when))
+
+    def drain(self):
+        for copy, when in self.started:
+            if when is None:
+                copy.wait_send()
+            else:
+                pl.when(when)(copy.wait_send)
+
+
+def arrived(ref, sem, other):
+    pltpu.make_async_remote_copy(
+        src_ref=ref,
+        dst_ref=ref,
+        send_sem=sem,
+        recv_sem=sem,
+        device_id=other,
+        device_id_type=MESH_ID,
+    ).wait_recv()
+
+
+class SemPool:
+    def __init__(self, ref):
+        self.ref = ref
+        self.used = 0
+
+    def take(self):
+        self.used += 1
+        assert self.used <= self.ref.shape[0]
+        return self.ref.at[self.used - 1]
+
+
+class Item:
+    def __init__(self, own, dst, recv, skip=False, cross=None, cross_recv=None):
+        self.own, self.dst, self.recv = own, dst, recv
+        self.skip, self.cross, self.cross_recv = skip, cross, cross_recv
+
+
+def gather_items(items, copies, pool):
+    dp, e, z = place()
+    px, py = x_of(e), y_of(e)
+    firsts, seconds = (px, py), (py, px)
+    diag = x_of(y_of(e))
+
+    def onward(item, h, ee, zz, targets, when):
+        ref = item.dst(zz, ee, h)
+        sem = item.recv.at[h, ee * 4 + zz]
+        for target, cond in targets:
+            copies.send(ref, ref, pool.take(), sem, target, cond)
+        if item.cross is not None:
+            copies.send(ref, ref, pool.take(), item.cross_recv.at[h, ee * 4 + zz], (1 - dp, e, z), when)
+
+    def wait_for(item, h, ee, zz, when):
+        def body():
+            arrived(item.dst(zz, ee, h), item.recv.at[h, ee * 4 + zz], (dp, e, z))
+        if when is None:
+            body()
+        else:
+            pl.when(when)(body)
+
+    def own_stage(k):
+        for sign in (-1, 1):
+            zz = z + sign * k
+            valid = (zz >= 0) & (zz <= 3)
+            nxt = z - sign
+            on = valid & (nxt >= 0) & (nxt <= 3)
+            for h in (0, 1):
+                for item in items:
+                    wait_for(item, h, e, zz, valid)
+                    onward(item, h, e, zz,
+                           [((dp, e, nxt), on), ((dp, firsts[h], z), valid), ((dp, seconds[h], z), valid)],
+                           valid)
+
+    def relay_stage(k):
+        for sign in (-1, 1) if k else (1,):
+            zz = z + sign * k
+            valid = (zz >= 0) & (zz <= 3) if k else None
+            for h in (0, 1):
+                for item in items:
+                    if k == 0 and item.skip:
+                        continue
+                    wait_for(item, h, firsts[h], zz, valid)
+                    onward(item, h, firsts[h], zz, [((dp, seconds[h], z), valid)], valid)
+
+    def last_stage(k):
+        for sign in (-1, 1) if k else (1,):
+            zz = z + sign * k
+            valid = (zz >= 0) & (zz <= 3) if k else None
+            for h in (0, 1):
+                for item in items:
+                    if k == 0 and item.skip:
+                        continue
+                    for ee in (seconds[h], diag):
+                        wait_for(item, h, ee, zz, valid)
+                        onward(item, h, ee, zz, [], valid)
+
+    for h in (0, 1):
+        for item in items:
+            own, dst, sem = item.own(h), item.dst(z, e, h), item.recv.at[h, e * 4 + z]
+            for sign in (-1, 1):
+                nxt = z + sign
+                copies.send(own, dst, pool.take(), sem, (dp, e, nxt), (nxt >= 0) & (nxt <= 3))
+            if not item.skip:
+                for target in (firsts[h], seconds[h]):
+                    copies.send(own, dst, pool.take(), sem, (dp, target, z))
+    own_stage(1)
+    relay_stage(0)
+    own_stage(2)
+    relay_stage(1)
+    own_stage(3)
+    relay_stage(2)
+    relay_stage(3)
+    for k in range(4):
+        last_stage(k)
+    for item in items:
+        if item.cross is not None:
+            for sign in (-1, 1):
+                for k in (1, 2, 3):
+                    zz = z + sign * k
+
+                    @pl.when((zz >= 0) & (zz <= 3))
+                    def _(item=item, zz=zz):
+                        for ee in range(4):
+                            for h in (0, 1):
+                                arrived(item.cross(zz, ee, h), item.cross_recv.at[h, ee * 4 + zz], (dp, e, z))
+
+
+def collect_kernel(
+    wq, wk, wv, wo, small, wg, wu, wd, dy,
+    full, small_all, wg_far, wu_far, wd_far, dy_all,
+    own4, load_sem, store_sem, recv_w, recv_x, recv_dy, recv_small, recv_far, send_sems,
+):
+    dp, e, z = place()
+    px, py = x_of(e), y_of(e)
+    loads = []
+    for m, ref in enumerate((wq, wk, wv, wo)):
+        load = pltpu.make_async_copy(ref, own4.at[m], load_sem.at[m])
+        load.start()
+        loads.append(load)
+    peers = [(dp, e, lax.rem(z + d, 4)) for d in (1, 2, 3)]
+    peers += [(dp, px, z), (dp, py, z), (1 - dp, e, z)]
+    greet(peers)
+    copies, pool = Copies(), SemPool(send_sems)
+    for load in loads:
+        load.wait()
+
+    def row(zz, ee, d, h):
+        return zz * 512 + ee * 128 + d * 64 + h * 32
+
+    def own_w(h):
+        return own4.at[:, pl.ds(pl.multiple_of(e * 128 + dp * 64 + h * 32, 32), 32), :]
+
+    def dst_w(d):
+        return lambda zz, ee, h: full.at[:, pl.ds(pl.multiple_of(row(zz, ee, d, h), 32), 32), :]
+
+    items = [
+        Item(own_w, dst_w(dp), recv_w, skip=True, cross=dst_w(1 - dp), cross_recv=recv_x),
+        Item(lambda h: dy.at[h], lambda zz, ee, h: dy_all.at[ee * 4 + zz, h], recv_dy),
+    ]
+    stores = [
+        pltpu.make_async_copy(own4, full.at[:, pl.ds(pl.multiple_of(z * 512, 512), 512), :], store_sem.at[0]),
+        pltpu.make_async_copy(dy, dy_all.at[e * 4 + z], store_sem.at[1]),
+        pltpu.make_async_copy(small, small_all.at[z], store_sem.at[2]),
+    ]
+    for store in stores:
+        store.start()
+    for d in (1, 2, 3):
+        copies.send(small, small_all.at[z], pool.take(), recv_small.at[z], (dp, e, lax.rem(z + d, 4)))
+    for i, (src, dst) in enumerate(((wg, wg_far), (wu, wu_far), (wd, wd_far))):
+        copies.send(src, dst, pool.take(), recv_far.at[i], (1 - dp, e, z))
+    gather_items(items, copies, pool)
+    for d in (1, 2, 3):
+        zz = lax.rem(z + d, 4)
+        arrived(small_all.at[zz], recv_small.at[zz], (dp, e, z))
+    for i, dst in enumerate((wg_far, wu_far, wd_far)):
+        arrived(dst, recv_far.at[i], (dp, e, z))
+    copies.drain()
+    for store in stores:
+        store.wait()
+
+
+def collect(wq, wk, wv, wo, small, wg, wu, wd, dy):
+    bf = jnp.bfloat16
+    dma = pltpu.SemaphoreType.DMA
+    return pl.pallas_call(
+        collect_kernel,
+        out_shape=(
+            jax.ShapeDtypeStruct((4, 2048, 2048), bf),
+            jax.ShapeDtypeStruct((4,) + small.shape, bf),
+            jax.ShapeDtypeStruct(wg.shape, bf),
+            jax.ShapeDtypeStruct(wu.shape, bf),
+            jax.ShapeDtypeStruct(wd.shape, bf),
+            jax.ShapeDtypeStruct((16,) + dy.shape, bf),
+        ),
+        in_specs=[ANY] * 8 + [pl.BlockSpec(memory_space=pltpu.VMEM)],
+        out_specs=(ANY,) * 6,
+        scratch_shapes=[
+            pltpu.VMEM((4, 512, 2048), bf),
+            dma((4,)),
+            dma((3,)),
+            dma((2, 16)),
+            dma((2, 16)),
+            dma((2, 16)),
+            dma((4,)),
+            dma((3,)),
+            dma((192,)),
+        ],
+        compiler_params=pltpu.CompilerParams(collective_id=0, has_side_effects=True, vmem_limit_bytes=24 * 2**20),
+        name="collect_weights",
+    )(wq, wk, wv, wo, small, wg, wu, wd, dy)
+
+
+def spread_kernel(rows, rows_all, store_sem, recv, send_sems):
+    dp, e, z = place()
+    px, py = x_of(e), y_of(e)
+    peers = [(dp, e, lax.rem(z + d, 4)) for d in (1, 2, 3)] + [(dp, px, z), (dp, py, z)]
+    greet(peers)
+    copies, pool = Copies(), SemPool(send_sems)
+    store = pltpu.make_async_copy(rows, rows_all.at[e * 4 + z], store_sem)
+    store.start()
+    gather_items([Item(lambda h: rows.at[h], lambda zz, ee, h: rows_all.at[ee * 4 + zz, h], recv)], copies, pool)
+    copies.drain()
+    store.wait()
+
+
+def spread(rows):
+    dma = pltpu.SemaphoreType.DMA
+    return pl.pallas_call(
+        spread_kernel,
+        out_shape=jax.ShapeDtypeStruct((16,) + rows.shape, rows.dtype),
+        in_specs=[pl.BlockSpec(memory_space=pltpu.VMEM)],
+        out_specs=ANY,
+        scratch_shapes=[dma(()), dma((2, 16)), dma((96,))],
+        compiler_params=pltpu.CompilerParams(collective_id=1, has_side_effects=True),
+        name="spread_rows",
+    )(rows)
+
+
+def combine_kernel(y_in, d_in, y_out, d_out, y_loc, d_loc, y_a, d_a, y_b, d_b, y_c, d_c,
+                   load_sem, a_sem, b_sem, c_sem, a_send, b_send, c_send):
+    dp, e, z = place()
+    px, py = x_of(e), y_of(e)
+    diag = x_of(y_of(e))
+    me = (dp, e, z)
+    loads = []
+    for i, (src, loc) in enumerate(((y_in, y_loc), (d_in, d_loc))):
+        load = pltpu.make_async_copy(src, loc, load_sem.at[i])
+        load.start()
+        loads.append(load)
+    greet([(dp, e, lax.rem(z + d, 4)) for d in (1, 2, 3)] + [(dp, px, z), (dp, py, z)])
+    firsts, seconds = (py, px), (px, py)
+    sets = ((0, y_in, y_loc, y_a, y_b, y_c, y_out), (1, d_in, d_loc, d_a, d_b, d_c, d_out))
+
+    def copy(src, dst, send_sem, recv_sem, device):
+        return pltpu.make_async_remote_copy(
+            src_ref=src, dst_ref=dst, send_sem=send_sem, recv_sem=recv_sem,
+            device_id=device, device_id_type=MESH_ID)
+
+    def a_copy(s, h, g, zz):
+        i, src, loc, a, b, c, out = s
+        ee = (diag, firsts[h])[g]
+        return copy(src.at[ee * 4 + zz, h], a.at[h, g, zz], a_send.at[i, h, g, zz], a_sem.at[i, h, g, zz],
+                    (dp, firsts[h], z))
+
+    def b_copy(s, h, zz):
+        i, src, loc, a, b, c, out = s
+        return copy(a.at[h, 0, zz], b.at[h, zz], b_send.at[i, h, zz], b_sem.at[i, h, zz], (dp, seconds[h], z))
+
+    def c_copy(s, h, zz):
+        i, src, loc, a, b, c, out = s
+        return copy(a.at[h, 1, zz], c.at[h, z], c_send.at[i, h, zz], c_sem.at[i, h, z], (dp, e, zz))
+
+    for g in (0, 1):
+        for s in sets:
+            for h in (0, 1):
+                def start_a(d, _, s=s, h=h, g=g):
+                    a_copy(s, h, g, lax.rem(z + d, 4)).start()
+                    return 0
+                lax.fori_loop(1, 5, start_a, 0)
+    for load in loads:
+        load.wait()
+
+    for s in sets:
+        i, src, loc, a, b, c, out = s
+        for h in (0, 1):
+            def relay(d, _, s=s, h=h, loc=loc, a=a):
+                zz = lax.rem(z + d, 4)
+                a_copy(s, h, 0, zz).wait_recv()
+                total = a[h, 0, zz].astype(jnp.float32) + loc[seconds[h] * 4 + zz, h].astype(jnp.float32)
+                a[h, 0, zz] = total.astype(a.dtype)
+                b_copy(s, h, zz).start()
+                return 0
+            lax.fori_loop(1, 5, relay, 0)
+    for s in sets:
+        i, src, loc, a, b, c, out = s
+        for h in (0, 1):
+            def finish(d, _, s=s, h=h, loc=loc, a=a, b=b):
+                zz = lax.rem(z + d, 4)
+                a_copy(s, h, 1, zz).wait_recv()
+                b_copy(s, h, zz).wait_recv()
+                total = (a[h, 1, zz].astype(jnp.float32) + loc[e * 4 + zz, h].astype(jnp.float32)
+                         + b[h, zz].astype(jnp.float32))
+                a[h, 1, zz] = total.astype(a.dtype)
+                c_copy(s, h, zz).start()
+                return 0
+            lax.fori_loop(1, 4, finish, 0)
+    for s in sets:
+        i, src, loc, a, b, c, out = s
+        for h in (0, 1):
+            a_copy(s, h, 1, z).wait_recv()
+            b_copy(s, h, z).wait_recv()
+            out[h] = (a[h, 1, z].astype(jnp.float32) + loc[e * 4 + z, h].astype(jnp.float32)
+                      + b[h, z].astype(jnp.float32))
+            for d in (1, 2, 3):
+                zz = lax.rem(z + d, 4)
+                arrived(c.at[h, zz], c_sem.at[i, h, zz], me)
+                out[h] += c[h, zz].astype(jnp.float32)
+    for s in sets:
+        for h in (0, 1):
+            def drain(d, _, s=s, h=h):
+                zz = lax.rem(z + d, 4)
+                a_copy(s, h, 0, zz).wait_send()
+                a_copy(s, h, 1, zz).wait_send()
+                b_copy(s, h, zz).wait_send()
+                return 0
+            lax.fori_loop(1, 5, drain, 0)
+
+            def drain_c(d, _, s=s, h=h):
+                c_copy(s, h, lax.rem(z + d, 4)).wait_send()
+                return 0
+            lax.fori_loop(1, 4, drain_c, 0)
+
+
+def combine(y_part, d_part):
+    dma = pltpu.SemaphoreType.DMA
+    bf = jnp.bfloat16
+    wide, narrow = y_part.shape[3], d_part.shape[3]
+    rows = y_part.shape[2]
+    vmem = pl.BlockSpec(memory_space=pltpu.VMEM)
+    return pl.pallas_call(
+        combine_kernel,
+        out_shape=(
+            jax.ShapeDtypeStruct((2, rows, wide), jnp.float32),
+            jax.ShapeDtypeStruct((2, rows, narrow), jnp.float32),
+        ),
+        in_specs=[ANY, ANY],
+        out_specs=(vmem, vmem),
+        scratch_shapes=[
+            pltpu.VMEM(y_part.shape, bf),
+            pltpu.VMEM(d_part.shape, bf),
+            pltpu.VMEM((2, 2, 4, rows, wide), bf),
+            pltpu.VMEM((2, 2, 4, rows, narrow), bf),
+            pltpu.VMEM((2, 4, rows, wide), bf),
+            pltpu.VMEM((2, 4, rows, narrow), bf),
+            pltpu.VMEM((2, 4, rows, wide), bf),
+            pltpu.VMEM((2, 4, rows, narrow), bf),
+            dma((2,)),
+            dma((2, 2, 2, 4)),
+            dma((2, 2, 4)),
+            dma((2, 2, 4)),
+            dma((2, 2, 2, 4)),
+            dma((2, 2, 4)),
+            dma((2, 2, 4)),
+        ],
+        compiler_params=pltpu.CompilerParams(collective_id=2, has_side_effects=True, vmem_limit_bytes=56 * 2**20),
+        name="combine_rows",
+    )(y_part, d_part)
+
+
+def total_kernel(gq, gk, gv, go, small, eg, eu, ed,
+                 out, small_out, eg_far, eu_far, ed_far,
+                 far, a, b, c, mine, work, s_z, s_all,
+                 work_sem, far_sem, a_sem, b_sem, c_sem, e_sem, sz_sem, sa_sem, g_sem,
+                 far_send, a_send, b_send, c_send, e_send, sz_send, sa_send, g_send, out_sem):
+    dp, e, z = place()
+    px, py = x_of(e), y_of(e)
+    diag = x_of(y_of(e))
+    firsts, seconds = (py, px), (px, py)
+    grads = (gq, gk, gv, go)
+    zs = [lax.rem(z + d, 4) for d in range(4)]
+    mates = [(lax.rem(dp + d // 4, 2), lax.rem(e + d % 4, 4), z) for d in range(1, 8)]
+    greet([(dp, e, zz) for zz in zs[1:]] + mates)
+
+    def copy(src, dst, send_sem, recv_sem, device):
+        return pltpu.make_async_remote_copy(
+            src_ref=src, dst_ref=dst, send_sem=send_sem, recv_sem=recv_sem,
+            device_id=device, device_id_type=MESH_ID)
+
+    def rows_of(ee, zz, d, h):
+        return pl.ds(pl.multiple_of(zz * 512 + ee * 128 + d * 64 + h * 32, 32), 32)
+
+    def far_copy(m, ee, zz, h):
+        return copy(grads[m].at[rows_of(ee, zz, 1 - dp, h)], far.at[h, ee, zz, m],
+                    far_send.at[h, ee, zz, m], far_sem.at[h, ee, zz, m], (1 - dp, e, z))
+
+    def load(m, ee, zz, h, slot):
+        return pltpu.make_async_copy(grads[m].at[rows_of(ee, zz, dp, h)], work.at[slot, m], work_sem.at[slot, m])
+
+    def groups(h):
+        return (diag, firsts[h], seconds[h], e)
+
+    def e_copy(i):
+        src, dst = ((eg, eg_far), (eu, eu_far), (ed, ed_far))[i]
+        return copy(src, dst, e_send.at[i], e_sem.at[i], (1 - dp, e, z))
+
+    def sz_copy(d):
+        return copy(small.at[zs[d]], s_z.at[z], sz_send.at[d - 1], sz_sem.at[z], (dp, e, zs[d]))
+
+    for d in (1, 2, 3):
+        sz_copy(d).start()
+    for g in range(4):
+        for h in (0, 1):
+            def start_far(zz, _, g=g, h=h):
+                for m in range(4):
+                    far_copy(m, groups(h)[g], zz, h).start()
+                return 0
+            lax.fori_loop(0, 4, start_far, 0)
+    for i in range(3):
+        e_copy(i).start()
+
+    def a_copy(h, g, zz):
+        return copy(far.at[h, groups(h)[g], zz], a.at[h, g, zz], a_send.at[h, g, zz], a_sem.at[h, g, zz],
+                    (dp, firsts[h], z))
+
+    def b_copy(h, zz):
+        return copy(far.at[h, seconds[h], zz], b.at[h, zz], b_send.at[h, zz], b_sem.at[h, zz], (dp, seconds[h], z))
+
+    def c_copy(h, zz):
+        return copy(far.at[h, e, zz], c.at[h, z], c_send.at[h, zz], c_sem.at[h, z], (dp, e, zz))
+
+    def load_step(n, slot):
+        g, h, zz = n // 8, lax.rem(n // 4, 2), lax.rem(n, 4)
+        ee = pick(g, h)
+        for m in range(4):
+            load(m, ee, zz, h, slot).start()
+
+    def pick(g, h):
+        first = jnp.where(h == 0, py, px)
+        second = jnp.where(h == 0, px, py)
+        return jnp.where(g == 0, diag, jnp.where(g == 1, first, jnp.where(g == 2, second, e)))
+
+    load_step(0, 0)
+
+    def near(n, _):
+        slot = lax.rem(n, 2)
+
+        @pl.when(n + 1 < 32)
+        def _():
+            load_step(n + 1, 1 - slot)
+
+        g, h, zz = n // 8, lax.rem(n // 4, 2), lax.rem(n, 4)
+        ee = pick(g, h)
+        for m in range(4):
+            load(m, ee, zz, h, slot).wait()
+            arrived(far.at[h, ee, zz, m], far_sem.at[h, ee, zz, m], (dp, e, z))
+        far[h, ee, zz] = (far[h, ee, zz].astype(jnp.float32) + work[slot].astype(jnp.float32)).astype(far.dtype)
+
+        @pl.when(g < 2)
+        def _():
+            first = jnp.where(h == 0, py, px)
+            copy(far.at[h, ee, zz], a.at[h, g, zz], a_send.at[h, g, zz], a_sem.at[h, g, zz], (dp, first, z)).start()
+        return 0
+
+    lax.fori_loop(0, 32, near, 0)
+
+    for h in (0, 1):
+        def relay(d, _, h=h):
+            zz = lax.rem(z + d, 4)
+            arrived(a.at[h, 0, zz], a_sem.at[h, 0, zz], (dp, e, z))
+            far[h, seconds[h], zz] = (far[h, seconds[h], zz].astype(jnp.float32)
+                                      + a[h, 0, zz].astype(jnp.float32)).astype(far.dtype)
+            b_copy(h, zz).start()
+            return 0
+        lax.fori_loop(1, 5, relay, 0)
+    for h in (0, 1):
+        def finish(d, _, h=h):
+            zz = lax.rem(z + d, 4)
+            arrived(a.at[h, 1, zz], a_sem.at[h, 1, zz], (dp, e, z))
+            arrived(b.at[h, zz], b_sem.at[h, zz], (dp, e, z))
+            far[h, e, zz] = (far[h, e, zz].astype(jnp.float32) + a[h, 1, zz].astype(jnp.float32)
+                             + b[h, zz].astype(jnp.float32)).astype(far.dtype)
+
+            @pl.when(d < 4)
+            def _():
+                c_copy(h, zz).start()
+            return 0
+        lax.fori_loop(1, 5, finish, 0)
+
+    def sa_copy(d):
+        return copy(mine_small, s_all.at[dp * 4 + e], sa_send.at[d - 1], sa_sem.at[dp * 4 + e], mates[d - 1])
+
+    slot_me = dp * 4 + e
+    for d in (1, 2, 3):
+        arrived(s_z.at[zs[d]], sz_sem.at[zs[d]], (dp, e, z))
+    s_all[slot_me] = (small[z] + s_z[zs[1]]) + (s_z[zs[2]] + s_z[zs[3]])
+    mine_small = s_all.at[slot_me]
+    for d in range(1, 8):
+        sa_copy(d).start()
+
+    def mine_at(d, ee):
+        return pl.ds(pl.multiple_of(ee * 128 + d * 64, 64), 64)
+
+    def g_copy(h, n):
+        return copy(mine.at[:, pl.ds(h * 32, 32)],
+                    out.at[:, pl.ds(pl.multiple_of(e * 128 + dp * 64 + h * 32, 32), 32)],
+                    g_send.at[h, n], g_sem.at[h, slot_me], mates[n])
+
+    locals_out = []
+    for h in (0, 1):
+        def last(m, _, h=h):
+            mine[m, pl.ds(h * 32, 32)] = (
+                (far[h, e, z, m].astype(jnp.float32) + c[h, zs[1], m].astype(jnp.float32))
+                + (c[h, zs[2], m].astype(jnp.float32) + c[h, zs[3], m].astype(jnp.float32))
+            ).astype(mine.dtype)
+            return 0
+        for d in (1, 2, 3):
+            arrived(c.at[h, zs[d]], c_sem.at[h, zs[d]], (dp, e, z))
+        lax.fori_loop(0, 4, last, 0)
+        for n in range(7):
+            g_copy(h, n).start()
+        keep = pltpu.make_async_copy(
+            mine.at[:, pl.ds(h * 32, 32)],
+            out.at[:, pl.ds(pl.multiple_of(e * 128 + dp * 64 + h * 32, 32), 32)],
+            out_sem.at[h])
+        keep.start()
+        locals_out.append(keep)
+    total = s_all[slot_me]
+    for d in range(1, 8):
+        other = lax.rem(dp + d // 4, 2) * 4 + lax.rem(e + d % 4, 4)
+        arrived(s_all.at[other], sa_sem.at[other], (dp, e, z))
+    small_out[...] = (((s_all[0] + s_all[1]) + (s_all[2] + s_all[3]))
+                      + ((s_all[4] + s_all[5]) + (s_all[6] + s_all[7])))
+    for h in (0, 1):
+        for d in range(1, 8):
+            od, oe = lax.rem(dp + d // 4, 2), lax.rem(e + d % 4, 4)
+            arrived(out.at[:, pl.ds(pl.multiple_of(oe * 128 + od * 64 + h * 32, 32), 32)],
+                    g_sem.at[h, od * 4 + oe], (dp, e, z))
+    for i in range(3):
+        e_copy(i).wait()
+    for d in (1, 2, 3):
+        sz_copy(d).wait_send()
+    for d in range(1, 8):
+        sa_copy(d).wait_send()
+    for h in (0, 1):
+        for n in range(7):
+            g_copy(h, n).wait_send()
+        locals_out[h].wait()
+        for g in range(4):
+            def drain_far(zz, _, g=g, h=h):
+                for m in range(4):
+                    far_copy(m, groups(h)[g], zz, h).wait_send()
+                return 0
+            lax.fori_loop(0, 4, drain_far, 0)
+
+        def drain(d, _, h=h):
+            zz = lax.rem(z + d, 4)
+            a_copy(h, 0, zz).wait_send()
+            a_copy(h, 1, zz).wait_send()
+            b_copy(h, zz).wait_send()
+
+            @pl.when(d < 4)
+            def _():
+                c_copy(h, zz).wait_send()
+            return 0
+        lax.fori_loop(1, 5, drain, 0)
+
+
+def total(gq, gk, gv, go, small, eg, eu, ed):
+    dma = pltpu.SemaphoreType.DMA
+    bf, f32 = jnp.bfloat16, jnp.float32
+    vmem = pl.BlockSpec(memory_space=pltpu.VMEM)
+    return pl.pallas_call(
+        total_kernel,
+        out_shape=(
+            jax.ShapeDtypeStruct((4, 512, 2048), bf),
+            jax.ShapeDtypeStruct(small.shape[1:], f32),
+            jax.ShapeDtypeStruct(eg.shape, bf),
+            jax.ShapeDtypeStruct(eu.shape, bf),
+            jax.ShapeDtypeStruct(ed.shape, bf),
+        ),
+        in_specs=[ANY] * 4 + [vmem] + [ANY] * 3,
+        out_specs=(ANY, vmem, ANY, ANY, ANY),
+        scratch_shapes=[
+            pltpu.VMEM((2, 4, 4, 4, 32, 2048), bf),
+            pltpu.VMEM((2, 2, 4, 4, 32, 2048), bf),
+            pltpu.VMEM((2, 4, 4, 32, 2048), bf),
+            pltpu.VMEM((2, 4, 4, 32, 2048), bf),
+            pltpu.VMEM((4, 64, 2048), bf),
+            pltpu.VMEM((2, 4, 32, 2048), bf),
+            pltpu.VMEM(small.shape, f32),
+            pltpu.VMEM((8,) + small.shape[1:], f32),
+            dma((2, 4)),
+            dma((2, 4, 4, 4)),
+            dma((2, 2, 4)),
+            dma((2, 4)),
+            dma((2, 4)),
+            dma((3,)),
+            dma((4,)),
+            dma((8,)),
+            dma((2, 8)),
+            dma((2, 4, 4, 4)),
+            dma((2, 2, 4)),
+            dma((2, 4)),
+            dma((2, 4)),
+            dma((3,)),
+            dma((3,)),
+            dma((7,)),
+            dma((2, 7)),
+            dma((2,)),
+        ],
+        compiler_params=pltpu.CompilerParams(collective_id=3, has_side_effects=True, vmem_limit_bytes=52 * 2**20),
+        name="total_grads",
+    )(gq, gk, gv, go, small, eg, eu, ed)
+
+
+def gathered(
+    tokens,
+    cotangent,
+    lengths,
+    routes,
+    w_query,
+    w_key,
+    w_value,
+    w_out,
+    w_router,
+    g_attn,
+    g_ffn,
+    g_query,
+    g_key,
+    w_gate,
+    w_up,
+    w_down,
+):
+    micro_count, _, seq_len, model_width = tokens.shape
+    expert_count = w_router.shape[1]
+    f32, bf = jnp.float32, jnp.bfloat16
+    places = jnp.arange(seq_len)
+    score_scale = HDIM ** (-0.5)
+    length = lengths[:, 0]
+    live = places[None, :] < length[:, None]
+    dy = jnp.where(live[:, :, None], cotangent[:, 0], jnp.zeros((), bf))
+    small = jnp.concatenate(
+        [w_router.T, g_attn[None], g_ffn[None], g_query[None], g_key[None],
+         jnp.zeros((32 - expert_count - 4, w_router.shape[0]), bf)], axis=0)
+    full, small_all, gate_far, up_far, down_far, dy_all = collect(
+        w_query, w_key, w_value, w_out, small, w_gate[0], w_up[0], w_down[0], dy)
+    query_full, key_full, value_full, out_full = full[0], full[1], full[2], full[3]
+    small_rows = jnp.swapaxes(small_all, 0, 1).reshape(32, model_width)
+    route_full = small_rows[:expert_count].T
+    gain_attn, gain_ffn, gain_query, gain_key = (
+        small_rows[expert_count + i].astype(f32) for i in range(4))
+
+    rows = micro_count * seq_len
+    cosine_one, sine_one = rope_tables(seq_len, HDIM)
+    cosine_table, sine_table = jnp.tile(cosine_one, (micro_count, 1)), jnp.tile(sine_one, (micro_count, 1))
+    inputs = tokens[:, 0].reshape(rows, model_width).astype(f32)
+    route_ids = routes[:, 0].reshape(rows, -1)
+    normed = rms_norm(inputs, gain_attn).astype(bf)
+    query_raw = matmul(normed, query_full)
+    key_raw = matmul(normed, key_full)
+    value_raw = matmul(normed, value_full)
+
+    def per_head(values):
+        return values.reshape(micro_count, seq_len, HEADS, HDIM)
+
+    value_low = per_head(value_raw.astype(bf))
+    query_low = per_head(rotate(
+        rms_norm(query_raw, gain_query).reshape(rows, HEADS, HDIM), cosine_table, sine_table).astype(bf))
+    key_low = per_head(rotate(
+        rms_norm(key_raw, gain_key).reshape(rows, HEADS, HDIM), cosine_table, sine_table).astype(bf))
+    allowed = (places[None, None, :] <= places[None, :, None]) & live[:, None, :]
+    scores = jnp.einsum("mqhd,mkhd->mhqk", query_low, key_low, preferred_element_type=f32) * score_scale
+    attn_probs = softmax_rows(jnp.where(allowed[:, None], scores, -1e30))
+    probs_low = attn_probs.astype(bf)
+    mixed_low = jnp.einsum("mhqk,mkhd->mqhd", probs_low, value_low, preferred_element_type=f32)
+    mixed_low = mixed_low.reshape(rows, model_width).astype(bf)
+    hidden_state = inputs + matmul(mixed_low, out_full)
+    ffn_in = rms_norm(hidden_state, gain_ffn).astype(bf)
+    router = softmax_rows(matmul(ffn_in, route_full))
+    expert_ids = jnp.arange(expert_count)
+    chosen = jnp.any(route_ids[:, :, None] == expert_ids[None, None, :], axis=1)
+    gates = jnp.where(chosen, router, 0.0)
+    gates_high = gates.astype(bf)
+    gates_low = (gates - gates_high.astype(f32)).astype(bf)
+    sent = jnp.concatenate(
+        [ffn_in, gates_high, gates_low, jnp.zeros((rows, EXTRA - 2 * expert_count), bf)], axis=1)
+    spread_rows = spread(sent.reshape(micro_count, seq_len, -1))
+
+    every = 16 * rows
+    wide_rows = spread_rows.reshape(every, -1)
+    dy_rows = dy_all.reshape(every, model_width)
+    expert_rows = wide_rows[:, :model_width]
+    mine = lax.axis_index("expert") * 4 + lax.axis_index("shard")
+    lane = jnp.arange(EXTRA)
+    pick = (lane == mine) | (lane == mine + expert_count)
+    gate_own = jnp.sum(jnp.where(pick[None], wide_rows[:, model_width:].astype(f32), 0.0), axis=1, keepdims=True)
+    dy_route = (gate_own * dy_rows.astype(f32)).astype(bf)
+    halves = ((w_gate[0], w_up[0], w_down[0]), (gate_far, up_far, down_far))
+    y_sum, d_sum, grads = 0.0, 0.0, []
+    for gate_w, up_w, down_w in halves:
+        gate_pre = matmul(expert_rows, gate_w)
+        up_value = matmul(expert_rows, up_w)
+        sigmoid_gate = jax.nn.sigmoid(gate_pre)
+        activated = gate_pre * sigmoid_gate
+        inner = (activated * up_value).astype(bf)
+        y_sum = y_sum + matmul(inner, down_w)
+        d_inner = times_transposed(dy_route, down_w)
+        d_gate = (d_inner * up_value * (sigmoid_gate + gate_pre * sigmoid_gate * (1.0 - sigmoid_gate))).astype(bf)
+        d_up = (d_inner * activated).astype(bf)
+        d_sum = d_sum + times_transposed(d_gate, gate_w) + times_transposed(d_up, up_w)
+        grads.append((transposed_times(expert_rows, d_gate), transposed_times(expert_rows, d_up),
+                      transposed_times(inner, dy_route)))
+    y_low = y_sum.astype(bf).astype(f32)
+    d_gate_own = jnp.sum(y_low * dy_rows.astype(f32), axis=1, keepdims=True)
+    dg_high = d_gate_own.astype(bf).astype(f32)
+    dg_low = d_gate_own - dg_high
+    extra = jnp.where(lane[None] == mine, dg_high, 0.0) + jnp.where(lane[None] == mine + expert_count, dg_low, 0.0)
+    y_part = jnp.concatenate([(gate_own * y_low).astype(bf), extra.astype(bf)], axis=1)
+    y_all, d_all = combine(y_part.reshape(16, micro_count, seq_len, -1),
+                           d_sum.astype(bf).reshape(16, micro_count, seq_len, -1))
+    y_all = y_all.reshape(rows, -1)
+    d_ffn_in = d_all.reshape(rows, -1)
+    mixed_out = (hidden_state + y_all[:, :model_width]).astype(bf)
+    d_gates = y_all[:, model_width:model_width + expert_count] + y_all[
+        :, model_width + expert_count:model_width + 2 * expert_count]
+    d_router = jnp.where(chosen, d_gates, 0.0)
+    d_output = dy.reshape(rows, model_width).astype(f32)
+    d_logits = (router * (d_router - jnp.sum(router * d_router, axis=1, keepdims=True))).astype(bf)
+    grad_router = transposed_times(d_logits, ffn_in)
+    d_ffn_in = d_ffn_in + times_transposed(d_logits, route_full)
+    d_hidden_norm, d_gain_ffn = norm_back(hidden_state, gain_ffn, d_ffn_in)
+    d_hidden = d_output + d_hidden_norm
+    d_attn_low = d_hidden.astype(bf)
+    grad_out = transposed_times(mixed_low, d_attn_low).astype(bf)
+    d_mixed = per_head(times_transposed(d_attn_low, out_full).astype(bf))
+    d_probs = jnp.einsum("mqhd,mkhd->mhqk", d_mixed, value_low, preferred_element_type=f32)
+    d_value = jnp.einsum("mhqk,mqhd->mkhd", probs_low, d_mixed, preferred_element_type=f32)
+    d_value = d_value.reshape(rows, model_width).astype(bf)
+    d_scores = (attn_probs * (d_probs - jnp.sum(attn_probs * d_probs, axis=-1, keepdims=True))).astype(bf)
+    d_query = jnp.einsum("mhqk,mkhd->mqhd", d_scores, key_low, preferred_element_type=f32) * score_scale
+    d_key = jnp.einsum("mhqk,mqhd->mkhd", d_scores, query_low, preferred_element_type=f32) * score_scale
+
+    def raw_back(raw, gain_vec, d_heads):
+        turned = rotate_back(d_heads.reshape(rows, HEADS, HDIM), cosine_table, sine_table)
+        return norm_back(raw, gain_vec, turned.reshape(rows, model_width))
+
+    d_query_raw, d_gain_query = raw_back(query_raw, gain_query, d_query)
+    d_key_raw, d_gain_key = raw_back(key_raw, gain_key, d_key)
+    d_query_low, d_key_low = d_query_raw.astype(bf), d_key_raw.astype(bf)
+    grad_query = transposed_times(normed, d_query_low).astype(bf)
+    grad_key = transposed_times(normed, d_key_low).astype(bf)
+    grad_value = transposed_times(normed, d_value).astype(bf)
+    d_normed = (times_transposed(d_query_low, query_full) + times_transposed(d_key_low, key_full)
+                + times_transposed(d_value, value_full))
+    d_input_norm, d_gain_attn = norm_back(inputs, gain_attn, d_normed)
+    grad_tokens = (d_hidden + d_input_norm).reshape(micro_count, 1, seq_len, model_width)
+
+    small_grads = jnp.concatenate(
+        [grad_router, d_gain_attn[None], d_gain_ffn[None], d_gain_query[None], d_gain_key[None],
+         jnp.zeros((24 - expert_count - 4, model_width), f32)], axis=0)
+    small_grads = jnp.swapaxes(small_grads.reshape(24, 4, model_width // 4), 0, 1)
+    near, away = grads
+    sums, small_sums, eg, eu, ed = total(
+        grad_query, grad_key, grad_value, grad_out, small_grads, *(g.astype(bf) for g in away))
+    expert_totals = [(g + other.astype(f32))[None] for g, other in zip(near, (eg, eu, ed))]
+    return (
+        mixed_out.reshape(micro_count, 1, seq_len, model_width),
+        grad_tokens,
+        sums[0].astype(f32),
+        sums[1].astype(f32),
+        sums[2].astype(f32),
+        sums[3].astype(f32),
+        small_sums[:expert_count].T,
+        small_sums[expert_count],
+        small_sums[expert_count + 1],
+        small_sums[expert_count + 2],
+        small_sums[expert_count + 3],
+        *expert_totals,
+    )
+
+
 def dispatch_rows(buffer):
     return lax.all_to_all(buffer, ("expert", "shard"), split_axis=0, concat_axis=0, tiled=True)
 
@@ -98,7 +924,7 @@
     return jnp.swapaxes(split_rows, 0, 1).reshape(owners, local_experts * capacity, model_width)
 
 
-def local(
+def exchanged(
     tokens,
     cotangent,
     lengths,
@@ -455,8 +1281,9 @@
         P(("expert", "shard"), None, "dp"),
         P(("expert", "shard"), "dp", None),
     )
+    sizes = (mesh.shape["dp"], mesh.shape["expert"], mesh.shape["shard"])
     return jax.shard_map(
-        local,
+        gathered if sizes == (2, 4, 4) else exchanged,
         mesh=mesh,
         in_specs=placed,
         out_specs=(

time: 2450 us -> 1120 us (0.46)
  waiting for transfers between devices: 1430 us -> 0 us
  Pallas kernels: 0 us -> 739 us
  blocking collectives: 487 us -> 0 us
  matrix products: 327 us -> 247 us
  starting transfers between devices: 41.9 us -> 0 us
  other arithmetic: 79.6 us -> 48.5 us
    pallas_call x0 -> x4, Pallas kernels: none -> 739 us  [the longest x1 279 us: total(): pl.pallas_call(total_kernel, out_shape=(jax.ShapeDtypeStruct((4, 512, 204...]
    all_gather x7 -> x0, waiting for transfers between devices: 516 us -> none  [the longest x1 144 us: local(): lax.all_gather(w_out, 'shard', axis=0, tiled=True)]
    reduce_scatter x8 -> x0, waiting for transfers between devices: 458 us -> none  [the longest x1 148 us: local(): lax.psum_scatter(grad_out.astype(jnp.bfloat16), 'shard', scatter_dimensio...]
    all_to_all x5 -> x0, waiting for transfers between devices: 334 us -> none  [the longest x2 149 us: collect_grads(): lax.all_to_all(buffer, ('expert', 'shard'), split_axis=0, concat_axis=0,...]
    all_to_all x3 -> x0, blocking collectives: 304 us -> none  [the longest x2 206 us: dispatch_grads(): lax.all_to_all(buffer, ('expert', 'shard'), split_axis=0, concat_axis=0,...]
    dot_general x30 -> x6, matrix products: 156 us -> 7.36 us  [the longest x1 3 us: gathered(): jnp.einsum('mhqk,mkhd->mqhd', probs_low, value_low, preferred_element_typ...]
    all_gather x5 -> x0, blocking collectives: 143 us -> none  [the longest x1 97.4 us: local(): lax.all_gather(w_router, 'shard', axis=0, tiled=True)]
    psum x1 -> x0, waiting for transfers between devices: 122 us -> none  [local(): lax.psum(layer_sums[0].astype(jnp.bfloat16), ('dp', 'expert'))]
  transfers between devices with their start and end apart: 21 -> 0, of which waited for: 13 -> 0; matrix products, arithmetic and copies ran while one was open for 11% -> 0% of each run, Pallas kernels for 0% -> 0%
where the time goes in v1:
time: 1120 us; the launch traced here: 1110 us
  Pallas kernels  739 us (66%)
  matrix products  247 us (22%)
  local copies, waits for them, and re-layouts  74.4 us (7%)
  other arithmetic  48.5 us (4%)
    pallas_call x1, Pallas kernels, total(): pl.pallas_call(total_kernel, out_shape=(jax.ShapeDtypeStruct((4, 512, 204...  279 us
    pallas_call x1, Pallas kernels, combine(): pl.pallas_call(combine_kernel, out_shape=(jax.ShapeDtypeStruct((2, rows,...  201 us
    pallas_call x1, Pallas kernels, collect(): pl.pallas_call(collect_kernel, out_shape=(jax.ShapeDtypeStruct((4, 2048,...  183 us
    dot_general x11, matrix products, times_transposed(): lax.dot_general(left, right, (((1,), (1,)), ((), ())), preferred_element_...  95.2 us
    dot_general x11, matrix products, matmul(): return jnp.dot(left, right, preferred_element_type=jnp.float32)  80 us
    pallas_call x1, Pallas kernels, spread(): pl.pallas_call(spread_kernel, out_shape=jax.ShapeDtypeStruct((16,) + rows...  77.4 us
    dot_general x11, matrix products, transposed_times(): lax.dot_general(left, right, (((0,), (0,)), ((), ())), preferred_element_...  64.5 us
    unnamed x227, local copies, waits for them, and re-layouts  22.6 us

profile of v1, /device:TPU:13, one launch (start us, length us, event | category | flops | bytes accessed | tf_op | source)
XLA Modules:
  0.0 1111.7 jit_solution(191146980040236225)
XLA Ops:
  17.3 182.5 %collect_weights.1 = (bf16[4,2048,2048]{2,1,0:T(8,128)(2,1)}, bf16[4,32,512]{2,1,0:T(8,128)(2,1)S(1)}, bf16[2048,512]{1,0:T(8,128)(2,1)S(1)}, bf16[2048,512]{1,0...) custom-call(bf16[512,2048]{1,0:T(8,128)(2,1)S(1)} %copy-done.3, ...), custom_call_target="tpu_custom_call" | custom-call | tf_op jit(solution)/shard_map/collect_weights/pallas_call | solution.py:300
  199.9 3.3 copy-done
  204.3 5.3 multiply_reduce_fusion.10
  209.6 6.0 multiply_reduce_fusion.11
  216.7 2.5 copy.162
  221.5 2.4 copy.159
  228.7 2.5 copy.161
  233.5 2.4 copy.157
  244.2 4.7 fusion.64
  249.0 3.0 fusion.67
  253.4 5.2 multiply_reduce_fusion.9
  261.9 77.4 %spread_rows.1 = bf16[16,2,64,2176]{3,2,1,0:T(8,128)(2,1)} custom-call(bf16[2,64,2176]{2,1,0:T(8,128)(2,1)} %bitcast.318), custom_call_target="tpu_custom_call" | custom-call | tf_op jit(solution)/shard_map/spread_rows/pallas_call | solution.py:343
  339.4 7.7 fusion.51
  347.1 6.7 multiply_convert_fusion.6
  354.8 8.2 multiply_convert_fusion.1
  363.0 7.7 fusion.53
  370.7 9.6 fusion.55
  380.3 10.0 multiply_convert_fusion.4
  390.4 8.1 fusion.101
  398.5 13.0 %copy.136 = f32[2048,2048]{0,1:T(8,128)} copy(bf16[2048,2048]{1,0:T(8,128)(2,1)} %bitcast.273) | data formatting | bytes 25165824 | tf_op jit(solution)/shard_map/convert_element_type | solution.py:829
  411.6 18.8 %multiply_convert_fusion = (bf16[2048,2048]{0,1:T(8,128)(2,1)S(1)}, f32[2048]{0:T(1024)S(1)}, bf16[2048,2048]{0,1:T(8,128)(2,1)}) fusion(f32[2048,2048]{0,1:T(8,128)} %copy.136, f32[2048]{0:T(1024)S(1)} %select_reduce_fusion, f32[2048,2048]{0,1:T(8,128)} %fusion.101, bf16[2048,512]{1,0:T(8,128)(2,1)} %get-tuple-element.162, bf16[512,2048]{1,0:T(8,128)(2,1)} %copy-done.1), kind=kOutput, calls=%fused_computation.6 | convolution fusion | flops 4332713984 | bytes 54542336 | tf_op jit(solution)/shard_map/dot_general | solution.py:18
  430.4 5.8 convolution_convert_fusion.4.ed
  437.0 9.5 multiply_convert_fusion.2
  446.5 8.2 fusion.116
  454.7 8.2 fusion.103
  463.0 8.2 fusion.106
  471.2 21.6 %add_convert_fusion = bf16[2048,2048]{1,0:T(8,128)(2,1)} fusion(f32[2048,2048]{1,0:T(8,128)} %fusion.116, f32[2048,2048]{1,0:T(8,128)} %fusion.106, f32[2048,2048]{1,0:T(8,128)} %fusion.103, bf16[2048,512]{1,0:T(8,128)(2,1)} %get-tuple-element.113, bf16[2048,512]{1,0:T(8,128)(2,1)S(1)} %get-tuple-element.30), kind=kOutput, calls=%fused_computation.5 | convolution fusion | flops 4311744512 | bytes 62914560 | tf_op jit(solution)/shard_map/dot_general | solution.py:22
  493.0 7.3 pad_maximum_fusion
  500.3 11.7 %copy.137 = bf16[2048,2176]{1,0:T(8,128)(2,1)} copy(bf16[2048,2176]{0,1:T(8,128)(2,1)} %pad_maximum_fusion) | data formatting | bytes 17825792 | tf_op jit(solution)/shard_map/concatenate | solution.py:833
  512.1 200.6 %combine_rows.1 = (f32[2,64,2176]{2,1,0:T(8,128)}, f32[2,64,2048]{2,1,0:T(8,128)}) custom-call(bf16[16,2,64,2176]{3,2,1,0:T(8,128)(2,1)} %bitcast.281, bf16[16,2,64,2048]{3,2,1,0:T(8,128)(2,1)} %bitcast.280), custom_call_target="tpu_custom_call" | custom-call | tf_op jit(solution)/shard_map/combine_rows/pallas_call | solution.py:455
  716.0 2.6 multiply_add_fusion.1
  718.6 6.3 fusion.61
  725.0 2.9 fusion.68
  735.5 2.6 multiply_reduce_fusion.1
  739.5 6.4 fusion.7
  746.0 7.3 fusion.32
  753.4 7.8 multiply_reduce_fusion.3
  761.2 5.7 convolution_convert_fusion.go
  766.9 5.6 convolution_convert_fusion.1.gv
  772.6 5.9 convolution_convert_fusion.2.gk
  778.5 5.7 convolution_convert_fusion.5.eu
  784.3 5.7 convolution_convert_fusion.6.eg
  790.0 5.7 convolution_convert_fusion.3.gq
  795.6 278.5 %total_grads.1 = (bf16[4,512,2048]{2,1,0:T(8,128)(2,1)}, f32[24,512]{1,0:T(8,128)S(1)}, bf16[2048,512]{1,0:T(8,128)(2,1)}, bf16[2048,512]{1,0:T(8,128)(2,1)}, bf16[512,2048]{1,0:T(8,128)(2,1)}) custom-call(bf16[2048,2048]{1,0:T(8,128)(2,1)} %convolution_convert_fusion.3.gq, bf16[2048,2048]{1,0:T(8,128)(2,1)} %convolution_convert_fusion.2.gk, ...), custom_call_target="tpu_custom_call" | custom-call | tf_op jit(solution)/shard_map/total_grads/pallas_call | solution.py:687
  1074.2 10.1 add_bitcast_fusion
  1084.4 7.8 add_bitcast_fusion.1
  1092.2 6.3 add_bitcast_fusion.2
  1098.5 10.2 bitcast_convert_fusion
  (313 shorter events, 57.9 us)
Async XLA Ops:
  1.4 240.1 %copy-start.87 = (pred[2,64]{1,0:T(4,128)(4,1)}, pred[2,64]{1,0:T(4,128)(4,1)S(1)}, u32[]{:S(2)}) copy-start(pred[2,64]{1,0:T(4,128)(4,1)S(1)} %iota_compare_fusion.2) | copy-start | bytes 388
  17.3 186.0 %copy-start.27 = (bf16[2,1,64,2048]{3,2,1,0:T(8,128)(2,1)S(1)}, bf16[2,1,64,2048]{3,2,1,0:T(8,128)(2,1)}, u32[]{:S(2)}) copy-start(bf16[2,1,64,2048]{3,2,1,0:T(8,128)(2,1)} %param.16) | copy-start | bytes 1572868
  203.2 35.1 %copy-start.62 = (f32[1,4,512]{2,0,1:T(1,128)}, f32[1,4,512]{2,0,1:T(1,128)S(1)}, u32[]{:S(2)}) copy-start(f32[1,4,512]{2,0,1:T(1,128)S(1)} %get-tuple-element.135) | copy-start | bytes 24580
  203.2 35.5 %copy-start.64 = (f32[1,4,512]{2,0,1:T(1,128)}, f32[1,4,512]{2,0,1:T(1,128)S(1)}, u32[]{:S(2)}) copy-start(f32[1,4,512]{2,0,1:T(1,128)S(1)} %get-tuple-element.136) | copy-start | bytes 24580
  203.2 55.5 %copy-start.66 = (f32[1,4,512]{2,0,1:T(1,128)}, f32[1,4,512]{2,0,1:T(1,128)S(1)}, u32[]{:S(2)}) copy-start(f32[1,4,512]{2,0,1:T(1,128)S(1)} %get-tuple-element.134) | copy-start | bytes 24580
  209.6 28.8 %copy-start.16 = (f32[128,2048]{1,0:T(8,128)}, f32[128,2048]{1,0:T(8,128)S(1)}, u32[]{:S(2)}) copy-start(f32[128,2048]{1,0:T(8,128)S(1)} %get-tuple-element.155) | copy-start | bytes 3145732
  215.6 22.8 %copy-start.76 = (f32[128]{0:T(128)}, f32[128]{0:T(128)S(1)}, u32[]{:S(2)}) copy-start(f32[128]{0:T(128)S(1)} %get-tuple-element.172) | copy-start | bytes 1540
  215.6 23.2 %copy-start.78 = (f32[128]{0:T(128)}, f32[128]{0:T(128)S(1)}, u32[]{:S(2)}) copy-start(f32[128]{0:T(128)S(1)} %get-tuple-element.173) | copy-start | bytes 1540
  249.0 9.6 copy-start.54
  258.7 80.6 %copy-start.83 = (f32[128]{0:T(128)}, f32[128]{0:T(128)S(1)}, u32[]{:S(2)}) copy-start(f32[128]{0:T(128)S(1)} %add_rsqrt_fusion.1) | copy-start | bytes 1540
  258.9 80.4 %copy-start.24 = (bf16[128,2048]{1,0:T(8,128)(2,1)}, bf16[128,2048]{1,0:T(8,128)(2,1)S(1)}, u32[]{:S(2)}) copy-start(bf16[128,2048]{1,0:T(8,128)(2,1)S(1)} %multiply_convert_fusion.12) | copy-start | bytes 1572868
  259.7 79.7 %copy-start.52 = (bf16[4,2,8,512]{3,2,0,1:T(8,128)(2,1)}, bf16[4,2,8,512]{3,2,0,1:T(8,128)(2,1)S(1)}, u32[]{:S(2)}) copy-start(bf16[4,2,8,512]{3,2,0,1:T(8,128)(2,1)S(1)} %copy.167) | copy-start | bytes 196612
  259.9 79.4 %copy-start.60 = (f32[128,16]{0,1:T(8,128)}, f32[128,16]{0,1:T(8,128)S(1)}, u32[]{:S(2)}) copy-start(f32[128,16]{0,1:T(8,128)S(1)} %get-tuple-element.161) | copy-start | bytes 24580
  259.9 79.4 %copy-start.74 = (f32[128]{0:T(128)}, f32[128]{0:T(128)S(1)}, u32[]{:S(2)}) copy-start(f32[128]{0:T(128)S(1)} %get-tuple-element.160) | copy-start | bytes 1540
  260.0 79.4 %copy-start.80 = (f32[128]{0:T(128)}, f32[128]{0:T(128)S(1)}, u32[]{:S(2)}) copy-start(f32[128]{0:T(128)S(1)} %fusion.97) | copy-start | bytes 1540
  339.4 7.7 copy-start.21
  363.0 17.3 %slice-start.6 = ((s8[8388608]{0:T(1024)(128)(4,1)}), s8[4194304]{0:T(1024)(128)(4,1)S(1)}, s32[]{:S(2)}) async-start(s8[8388608]{0:T(1024)(128)(4,1)} %bitcast.297), calls=%async_computation.6 | async-start | bytes 8388608
  370.7 9.6 copy-start.8
  370.7 9.6 slice-start.7
  390.3 8.2 copy-start.95
  411.6 18.8 %copy-start.35 = (bf16[2048,512]{1,0:T(8,128)(2,1)S(1)}, bf16[2048,512]{1,0:T(8,128)(2,1)}, u32[]{:S(2)}) copy-start(bf16[2048,512]{1,0:T(8,128)(2,1)} %get-tuple-element.162) | copy-start | bytes 6291460
  437.0 9.5 copy-start.15
  446.5 8.2 copy-start.97
  446.5 8.2 copy-start.10
  446.5 8.2 copy-start.94
  454.7 8.3 copy-start.13
  454.7 8.2 copy-start.92
  471.2 21.6 %copy-start.89 = (pred[128]{0:T(512)(128)(4,1)S(1)}, pred[128]{0:T(512)(128)(4,1)}, u32[]{:S(2)}) copy-start(pred[128]{0:T(512)(128)(4,1)} %get-tuple-element.170) | copy-start | bytes 388
  512.0 201.8 %copy-start.61 = (f32[128,16]{0,1:T(8,128)S(1)}, f32[128,16]{0,1:T(8,128)}, u32[]{:S(2)}) copy-start(f32[128,16]{0,1:T(8,128)} %copy-done.60) | copy-start | bytes 24580
  512.0 201.9 %copy-start.73 = (pred[128,16]{0,1:T(8,128)(4,1)S(1)}, pred[128,16]{0,1:T(8,128)(4,1)}, u32[]{:S(2)}) copy-start(pred[128,16]{0,1:T(8,128)(4,1)} %copy-done.72) | copy-start | bytes 6148
  512.0 201.9 %copy-start.75 = (f32[128]{0:T(128)S(1)}, f32[128]{0:T(128)}, u32[]{:S(2)}) copy-start(f32[128]{0:T(128)} %copy-done.74) | copy-start | bytes 1540
  512.0 201.9 %copy-start.81 = (f32[128]{0:T(128)S(1)}, f32[128]{0:T(128)}, u32[]{:S(2)}) copy-start(f32[128]{0:T(128)} %copy-done.80) | copy-start | bytes 1540
  512.0 201.9 %copy-start.25 = (bf16[128,2048]{1,0:T(8,128)(2,1)S(1)}, bf16[128,2048]{1,0:T(8,128)(2,1)}, u32[]{:S(2)}) copy-start(bf16[128,2048]{1,0:T(8,128)(2,1)} %copy-done.24) | copy-start | bytes 1572868
  512.0 202.1 %copy-start.23 = (f32[128,2048]{1,0:T(8,128)S(1)}, f32[128,2048]{1,0:T(8,128)}, u32[]{:S(2)}) copy-start(f32[128,2048]{1,0:T(8,128)} %copy-done.22) | copy-start | bytes 3145732
  512.0 202.1 %copy-start.53 = (bf16[4,2,8,512]{3,2,0,1:T(8,128)(2,1)S(1)}, bf16[4,2,8,512]{3,2,0,1:T(8,128)(2,1)}, u32[]{:S(2)}) copy-start(bf16[4,2,8,512]{3,2,0,1:T(8,128)(2,1)} %copy-done.52) | copy-start | bytes 196612
  512.0 202.1 %copy-start.67 = (f32[1,4,512]{2,0,1:T(1,128)S(1)}, f32[1,4,512]{2,0,1:T(1,128)}, u32[]{:S(2)}) copy-start(f32[1,4,512]{2,0,1:T(1,128)} %copy-done.66) | copy-start | bytes 24580
  512.0 202.1 %copy-start.84 = (f32[128]{0:T(128)S(1)}, f32[128]{0:T(128)}, u32[]{:S(2)}) copy-start(f32[128]{0:T(128)} %copy-done.83) | copy-start | bytes 1540
  753.4 7.8 copy-start.37
  766.9 11.6 %slice-start = ((s8[8912896]{0:T(1024)(128)(4,1)}), s8[4194304]{0:T(1024)(128)(4,1)S(1)}, s32[]{:S(2)}) async-start(s8[8912896]{0:T(1024)(128)(4,1)} %bitcast.287), calls=%async_computation | async-start | bytes 8388608
  766.9 11.6 %slice-start.1 = ((s8[8912896]{0:T(1024)(128)(4,1)}), s8[4194304]{0:T(1024)(128)(4,1)S(1)}, s32[]{:S(2)}) async-start(s8[8912896]{0:T(1024)(128)(4,1)} %bitcast.287), calls=%async_computation.1 | async-start | bytes 8388608
  795.6 278.6 %copy-start.96 = (bf16[2048,512]{1,0:T(8,128)(2,1)S(1)}, bf16[2048,512]{1,0:T(8,128)(2,1)}, u32[]{:S(2)}) copy-start(bf16[2048,512]{1,0:T(8,128)(2,1)} %copy-done.95) | copy-start | bytes 6291460
  795.6 288.7 %slice-start.3 = ((s8[8912896]{0:T(1024)(128)(4,1)}), s8[524288]{0:T(1024)(128)(4,1)S(1)}, s32[]{:S(2)}) async-start(s8[8912896]{0:T(1024)(128)(4,1)} %bitcast.291), calls=%async_computation.3 | async-start | bytes 1048576
  795.6 288.7 %slice-start.4 = ((s8[8912896]{0:T(1024)(128)(4,1)}), s8[4194304]{0:T(1024)(128)(4,1)S(1)}, s32[]{:S(2)}) async-start(s8[8912896]{0:T(1024)(128)(4,1)} %bitcast.291), calls=%async_computation.4 | async-start | bytes 8388608
  1074.2 10.2 slice-start.5
  1074.2 10.2 copy-start.91
  1084.4 7.8 copy-start.90
  1084.4 7.8 copy-start.93
  1098.5 11.4 %copy-start.51 = (f32[128,2048]{1,0:T(8,128)S(1)}, f32[128,2048]{1,0:T(8,128)}, u32[]{:S(2)}) copy-start(f32[128,2048]{1,0:T(8,128)} %get-tuple-element.167) | copy-start | bytes 3145732
  (61 other events, 227.3 us)

commit v2 on v1

--- a/solution.py
+++ b/solution.py
@@ -351,142 +351,440 @@
     )(rows)
 
 
-def combine_kernel(y_in, d_in, y_out, d_out, y_loc, d_loc, y_a, d_a, y_b, d_b, y_c, d_c,
-                   load_sem, a_sem, b_sem, c_sem, a_send, b_send, c_send):
+def times(left, right):
+    return jnp.dot(left, right, preferred_element_type=jnp.float32)
+
+
+def experts_kernel(
+    wide, dy, wg, wu, wd, wgf, wuf, wdf,
+    res, eg, eu, ed, part, a_buf, b_buf, c_buf,
+    WG, WU, WD, rows_in, dy_rows, hidden, saved, acc, stage, addend, turned, column, far_out,
+    w_sem, dy_sem, in_sem, part_sem, add_sem, col_sem, fin_sem, out_sem,
+    a_sem, b_sem, c_sem, a_send, b_send, c_send, gu_send, gu_sem, dn_send, dn_sem, free_sem,
+):
     dp, e, z = place()
     px, py = x_of(e), y_of(e)
     diag = x_of(y_of(e))
     me = (dp, e, z)
-    loads = []
-    for i, (src, loc) in enumerate(((y_in, y_loc), (d_in, d_loc))):
-        load = pltpu.make_async_copy(src, loc, load_sem.at[i])
-        load.start()
-        loads.append(load)
-    greet([(dp, e, lax.rem(z + d, 4)) for d in (1, 2, 3)] + [(dp, px, z), (dp, py, z)])
-    firsts, seconds = (py, px), (px, py)
-    sets = ((0, y_in, y_loc, y_a, y_b, y_c, y_out), (1, d_in, d_loc, d_a, d_b, d_c, d_out))
-
-    def copy(src, dst, send_sem, recv_sem, device):
+    far_core = (1 - dp, e, z)
+    f32, bf = jnp.float32, jnp.bfloat16
+    width = dy.shape[3]
+    half_f = wg.shape[1]
+    total_width = part.shape[3]
+
+    def local(src, dst, sem):
+        return pltpu.make_async_copy(src, dst, sem)
+
+    def remote(src, dst, send_sem, recv_sem, device):
         return pltpu.make_async_remote_copy(
             src_ref=src, dst_ref=dst, send_sem=send_sem, recv_sem=recv_sem,
             device_id=device, device_id_type=MESH_ID)
 
-    def a_copy(s, h, g, zz):
-        i, src, loc, a, b, c, out = s
-        ee = (diag, firsts[h])[g]
-        return copy(src.at[ee * 4 + zz, h], a.at[h, g, zz], a_send.at[i, h, g, zz], a_sem.at[i, h, g, zz],
-                    (dp, firsts[h], z))
-
-    def b_copy(s, h, zz):
-        i, src, loc, a, b, c, out = s
-        return copy(a.at[h, 0, zz], b.at[h, zz], b_send.at[i, h, zz], b_sem.at[i, h, zz], (dp, seconds[h], z))
-
-    def c_copy(s, h, zz):
-        i, src, loc, a, b, c, out = s
-        return copy(a.at[h, 1, zz], c.at[h, z], c_send.at[i, h, zz], c_sem.at[i, h, z], (dp, e, zz))
-
-    for g in (0, 1):
-        for s in sets:
-            for h in (0, 1):
-                def start_a(d, _, s=s, h=h, g=g):
-                    a_copy(s, h, g, lax.rem(z + d, 4)).start()
-                    return 0
-                lax.fori_loop(1, 5, start_a, 0)
-    for load in loads:
+    def column_of(c):
+        return jnp.where(c == 0, diag, jnp.where(c == 1, py, jnp.where(c == 2, px, e)))
+
+    def zed(i):
+        return lax.rem(z + jnp.where(i == 0, 2, jnp.where(i == 1, 1, jnp.where(i == 2, 3, 0))), 4)
+
+    def slot_of(s, i):
+        return column_of(s // 2) * 4 + zed(2 * lax.rem(s, 2) + i)
+
+    def rows_load(s, i, buf):
+        return local(wide.at[slot_of(s, i)], rows_in.at[buf, i], in_sem.at[buf, i])
+
+    weights = [
+        local(src, dst, w_sem.at[n])
+        for n, (src, dst) in enumerate((
+            (wg, WG.at[0]), (wu, WU.at[0]), (wd, WD.at[0]), (wgf, WG.at[1]), (wuf, WU.at[1]), (wdf, WD.at[1])))
+    ]
+    for i in range(2):
+        rows_load(0, i, 0).start()
+    weights[0].start()
+    weights[1].start()
+    dy_load = local(dy, dy_rows, dy_sem)
+    dy_load.start()
+    for load in weights[2:]:
+        load.start()
+    greet([(dp, e, lax.rem(z + d, 4)) for d in (1, 2, 3)] + [(dp, px, z), (dp, py, z), far_core])
+
+    def part_write(s, i):
+        return local(stage.at[lax.rem(s, 2), i], part.at[slot_of(s, i)], part_sem.at[lax.rem(s, 2), i])
+
+    def a_copy(h, g, slot, zz, target):
+        return remote(part.at[slot, h], a_buf.at[h, g, zz], a_send.at[h, g, zz], a_sem.at[h, g, zz], (dp, target, z))
+
+    def b_copy(h, slot, zz, target):
+        return remote(part.at[slot, h], b_buf.at[h, zz], b_send.at[h, zz], b_sem.at[h, zz], (dp, target, z))
+
+    def send_step(s):
+        c = s // 2
+        for i in range(2):
+            part_write(s, i).wait()
+            zz = zed(2 * lax.rem(s, 2) + i)
+
+            @pl.when(c == 0)
+            def _():
+                a_copy(0, 0, diag * 4 + zz, zz, py).start()
+                a_copy(1, 0, diag * 4 + zz, zz, px).start()
+
+            @pl.when(c == 1)
+            def _():
+                a_copy(0, 1, py * 4 + zz, zz, py).start()
+                b_copy(1, py * 4 + zz, zz, py).start()
+
+            @pl.when(c == 2)
+            def _():
+                a_copy(1, 1, px * 4 + zz, zz, px).start()
+                b_copy(0, px * 4 + zz, zz, px).start()
+
+    def addend_load(s, i):
+        h = jnp.where(s // 2 == 1, 1, 0)
+        zz = zed(2 * lax.rem(s, 2) + i)
+        return local(a_buf.at[h, 0, zz], addend.at[i], add_sem.at[i])
+
+    mine = e * 4 + z
+    lane = lax.broadcasted_iota(jnp.int32, (256, EXTRA), 1)
+    at_high, at_low = lane == mine, lane == mine + 16
+
+    weights[0].wait()
+    weights[1].wait()
+    dy_load.wait()
+
+    def step(s, _):
+        buf = lax.rem(s, 2)
+
+        @pl.when(s + 1 < 8)
+        def _():
+            for i in range(2):
+                rows_load(s + 1, i, 1 - buf).start()
+        for i in range(2):
+            rows_load(s, i, buf).wait()
+        slots = [slot_of(s, i) for i in range(2)]
+        extra = rows_in[buf, :, :, :, width:].reshape(256, EXTRA).astype(f32)
+        gate = jnp.sum(jnp.where(at_high | at_low, extra, 0.0), axis=1, keepdims=True)
+
+        def dy_step():
+            return jnp.concatenate([dy_rows[slot].reshape(128, width) for slot in slots], axis=0)
+
+        def put(ref, values, lo, hi):
+            for i in range(2):
+                ref[slots[i], :, lo:hi] = values[i * 128:(i + 1) * 128]
+
+        dy_route = (gate * dy_step().astype(f32)).astype(bf)
+        for n in range(2):
+            if n == 1:
+                @pl.when(s == 0)
+                def _():
+                    for load in weights[3:]:
+                        load.wait()
+
+                @pl.when(s > 0)
+                def _():
+                    send_step(s - 1)
+
+                @pl.when((s >= 2) & (s < 6))
+                def _():
+                    for i in range(2):
+                        h = jnp.where(s // 2 == 1, 1, 0)
+                        zz = zed(2 * lax.rem(s, 2) + i)
+                        arrived(a_buf.at[h, 0, zz], a_sem.at[h, 0, zz], me)
+                        addend_load(s, i).start()
+            x = rows_in[buf, :, :, :, :width].reshape(256, width)
+            gate_pre = times(x, WG[n])
+            up_value = times(x, WU[n])
+            sigmoid_gate = jax.nn.sigmoid(gate_pre)
+            activated = gate_pre * sigmoid_gate
+            inner = (activated * up_value).astype(bf)
+            put(hidden, inner, n * half_f, (n + 1) * half_f)
+            if n == 0:
+                @pl.when(s == 0)
+                def _():
+                    weights[2].wait()
+            d_inner = times_transposed(dy_route, WD[n])
+            d_gate = (d_inner * up_value * (sigmoid_gate + gate_pre * sigmoid_gate * (1.0 - sigmoid_gate))).astype(bf)
+            d_up = (d_inner * activated).astype(bf)
+            put(saved, d_gate, 2 * n * half_f, (2 * n + 1) * half_f)
+            put(saved, d_up, (2 * n + 1) * half_f, (2 * n + 2) * half_f)
+            if n == 0:
+                acc[0] = times(inner, WD[n])
+                acc[1] = times_transposed(d_gate, WG[n]) + times_transposed(d_up, WU[n])
+            else:
+                acc[0] += times(inner, WD[n])
+                acc[1] += times_transposed(d_gate, WG[n]) + times_transposed(d_up, WU[n])
+        y_low = acc[0].astype(bf).astype(f32)
+        d_own = jnp.sum(y_low * dy_step().astype(f32), axis=1, keepdims=True)
+        high = d_own.astype(bf).astype(f32)
+        tail = jnp.where(at_high, high, jnp.where(at_low, d_own - high, 0.0)).astype(bf)
+
+        def lay(values):
+            return values.reshape(2, 2, 64, values.shape[1])
+
+        stage[buf, :, :, :, :width] = lay((gate * y_low).astype(bf))
+        stage[buf, :, :, :, width:width + EXTRA] = lay(tail)
+        stage[buf, :, :, :, width + EXTRA:] = lay(acc[1].astype(bf))
+        for i in range(2):
+            dy_rows[slots[i]] = dy_route[i * 128:(i + 1) * 128].reshape(2, 64, width)
+
+        @pl.when((s >= 2) & (s < 6))
+        def _():
+            h = jnp.where(s // 2 == 1, 1, 0)
+            for i in range(2):
+                addend_load(s, i).wait()
+                stage[buf, i, h] = (stage[buf, i, h].astype(f32) + addend[i].astype(f32)).astype(bf)
+        for i in range(2):
+            part_write(s, i).start()
+        return 0
+
+    lax.fori_loop(0, 8, step, 0)
+    pl.semaphore_signal(free_sem, inc=1, device_id=far_core, device_id_type=MESH_ID)
+    for i in range(2):
+        part_write(7, i).wait()
+
+    def finish_loads(k):
+        zz = zed(k)
+        return (local(part.at[e * 4 + zz], stage.at[0, 0], fin_sem.at[0]),
+                local(a_buf.at[:, 1, zz], stage.at[0, 1], fin_sem.at[1]),
+                local(b_buf.at[:, zz], stage.at[1, 0], fin_sem.at[2]))
+
+    def begin(k):
+        zz = zed(k)
+        for h in range(2):
+            arrived(a_buf.at[h, 1, zz], a_sem.at[h, 1, zz], me)
+            arrived(b_buf.at[h, zz], b_sem.at[h, zz], me)
+        for load in finish_loads(k):
+            load.start()
+
+    def result_write(k):
+        return local(stage.at[1, 1], part.at[e * 4 + zed(k)], fin_sem.at[3])
+
+    def c_copy(k):
+        zz = zed(k)
+        return remote(part.at[e * 4 + zz], c_buf.at[z], c_send.at[k], c_sem.at[z], (dp, e, zz))
+
+    def close(k):
+        for load in finish_loads(k):
+            load.wait()
+        for h in range(2):
+            total = (stage[0, 0, h].astype(f32) + stage[0, 1, h].astype(f32)) + stage[1, 0, h].astype(f32)
+            if k < 3:
+                stage[1, 1, h] = total.astype(bf)
+            else:
+                res[h] = total
+        if k < 3:
+            result_write(k).start()
+
+    def fire(k):
+        result_write(k).wait()
+        c_copy(k).start()
+
+    def turn_hidden(n):
+        turned[...] = hidden[:, :, pl.ds(pl.multiple_of(n * 256, 256), 256)].reshape(2048, 256).T
+
+    def down_block(dst):
+        def col(j, _):
+            cc = pl.ds(pl.multiple_of(j * 512, 512), 512)
+            dst(cc, times(turned[...], dy_rows[:, :, :, cc].reshape(2048, 512)))
+            return 0
+        lax.fori_loop(0, 4, col, 0)
+
+    def column_load(n):
+        return local(wide.at[:, :, :, pl.ds(pl.multiple_of(n * 256, 256), 256)], column.at[lax.rem(n, 2)],
+                     col_sem.at[lax.rem(n, 2)])
+
+    def down_send(n):
+        return remote(far_out.at[n], WD.at[1, pl.ds(n * 256, 256)], dn_send.at[n], dn_sem.at[n], far_core)
+
+    column_load(0).start()
+    for n in range(2):
+        turn_hidden(2 + n)
+
+        def to_far(cc, values, n=n):
+            far_out[n, :, cc] = values.astype(bf)
+        down_block(to_far)
+        if n == 0:
+            pl.semaphore_wait(free_sem, 1)
+        down_send(n).start()
+
+    def row_block(n):
+        return pl.ds(pl.multiple_of(n * 256, 256), 256)
+
+    def gu_copy(n, w):
+        buf = lax.rem(n, 2)
+        return remote(far_out.at[buf, :, w * 512:(w + 1) * 512], WG.at[w, row_block(n)],
+                      gu_send.at[buf, w], gu_sem.at[n, w], far_core)
+
+    def gu_out(n, w):
+        buf = lax.rem(n, 2)
+        return local(acc.at[buf, :, w * 512:(w + 1) * 512], (eg, eu)[w].at[row_block(n)], out_sem.at[buf, w])
+
+    def settle(n):
+        buf = lax.rem(n, 2)
+        for w in range(2):
+            arrived(WG.at[w, row_block(n)], gu_sem.at[n, w], me)
+            acc[buf, :, w * 512:(w + 1) * 512] += WG[w, row_block(n)].astype(f32)
+            gu_out(n, w).start()
+
+    def gate_up(n, _):
+        buf = lax.rem(n, 2)
+
+        @pl.when(n + 1 < 8)
+        def _():
+            column_load(n + 1).start()
+        column_load(n).wait()
+        turned[...] = column[buf].reshape(2048, 256).T
+
+        @pl.when(n < 2)
+        def _():
+            for k in range(2):
+                @pl.when(n == k)
+                def _(k=k):
+                    down_send(k).wait_send()
+
+        @pl.when(n >= 2)
+        def _():
+            for w in range(2):
+                gu_copy(n - 2, w).wait_send()
+                gu_out(n - 2, w).wait()
+
+        def far_col(j, _):
+            cc = pl.ds(pl.multiple_of(j * 512, 512), 512)
+            src = pl.ds(pl.multiple_of(1024 + j * 512, 512), 512)
+            far_out[buf, :, cc] = times(turned[...], saved[:, :, src].reshape(2048, 512)).astype(bf)
+            return 0
+
+        def near_col(j, _):
+            cc = pl.ds(pl.multiple_of(j * 512, 512), 512)
+            acc[buf, :, cc] = times(turned[...], saved[:, :, cc].reshape(2048, 512))
+            return 0
+        lax.fori_loop(0, 2, far_col, 0)
+        for w in range(2):
+            gu_copy(n, w).start()
+        lax.fori_loop(0, 2, near_col, 0)
+
+        @pl.when(n > 0)
+        def _():
+            settle(n - 1)
+        for at, act in ((2, lambda: begin(0)), (3, lambda: close(0)), (4, lambda: fire(0)),
+                        (5, lambda: begin(1)), (6, lambda: close(1)), (7, lambda: fire(1))):
+            pl.when(n == at)(act)
+        return 0
+
+    lax.fori_loop(0, 8, gate_up, 0)
+    settle(7)
+    for n in (6, 7):
+        for w in range(2):
+            gu_copy(n, w).wait_send()
+            gu_out(n, w).wait()
+
+    def down_out(n):
+        return local(acc.at[n], ed.at[pl.ds(n * 256, 256)], out_sem.at[n, 0])
+
+    for n in range(2):
+        turn_hidden(n)
+
+        def keep(cc, values, n=n):
+            acc[n, :, cc] = values
+        down_block(keep)
+        arrived(WD.at[1, pl.ds(n * 256, 256)], dn_sem.at[n], me)
+        acc[n] += WD[1, pl.ds(n * 256, 256)].astype(f32)
+        down_out(n).start()
+    begin(2)
+    close(2)
+    fire(2)
+    begin(3)
+    close(3)
+    for k in range(3):
+        zz = zed(k)
+        arrived(c_buf.at[zz], c_sem.at[zz], me)
+        load = local(c_buf.at[zz], stage.at[0, 0], fin_sem.at[0])
+        load.start()
         load.wait()
-
-    for s in sets:
-        i, src, loc, a, b, c, out = s
-        for h in (0, 1):
-            def relay(d, _, s=s, h=h, loc=loc, a=a):
-                zz = lax.rem(z + d, 4)
-                a_copy(s, h, 0, zz).wait_recv()
-                total = a[h, 0, zz].astype(jnp.float32) + loc[seconds[h] * 4 + zz, h].astype(jnp.float32)
-                a[h, 0, zz] = total.astype(a.dtype)
-                b_copy(s, h, zz).start()
-                return 0
-            lax.fori_loop(1, 5, relay, 0)
-    for s in sets:
-        i, src, loc, a, b, c, out = s
-        for h in (0, 1):
-            def finish(d, _, s=s, h=h, loc=loc, a=a, b=b):
-                zz = lax.rem(z + d, 4)
-                a_copy(s, h, 1, zz).wait_recv()
-                b_copy(s, h, zz).wait_recv()
-                total = (a[h, 1, zz].astype(jnp.float32) + loc[e * 4 + zz, h].astype(jnp.float32)
-                         + b[h, zz].astype(jnp.float32))
-                a[h, 1, zz] = total.astype(a.dtype)
-                c_copy(s, h, zz).start()
-                return 0
-            lax.fori_loop(1, 4, finish, 0)
-    for s in sets:
-        i, src, loc, a, b, c, out = s
-        for h in (0, 1):
-            a_copy(s, h, 1, z).wait_recv()
-            b_copy(s, h, z).wait_recv()
-            out[h] = (a[h, 1, z].astype(jnp.float32) + loc[e * 4 + z, h].astype(jnp.float32)
-                      + b[h, z].astype(jnp.float32))
-            for d in (1, 2, 3):
-                zz = lax.rem(z + d, 4)
-                arrived(c.at[h, zz], c_sem.at[i, h, zz], me)
-                out[h] += c[h, zz].astype(jnp.float32)
-    for s in sets:
-        for h in (0, 1):
-            def drain(d, _, s=s, h=h):
-                zz = lax.rem(z + d, 4)
-                a_copy(s, h, 0, zz).wait_send()
-                a_copy(s, h, 1, zz).wait_send()
-                b_copy(s, h, zz).wait_send()
-                return 0
-            lax.fori_loop(1, 5, drain, 0)
-
-            def drain_c(d, _, s=s, h=h):
-                c_copy(s, h, lax.rem(z + d, 4)).wait_send()
-                return 0
-            lax.fori_loop(1, 4, drain_c, 0)
-
-
-def combine(y_part, d_part):
+        for h in range(2):
+            res[h] += stage[0, 0, h].astype(f32)
+    for n in range(2):
+        down_out(n).wait()
+    for k in range(3):
+        c_copy(k).wait_send()
+
+    def drain(zz, _):
+        a_copy(0, 0, diag * 4 + zz, zz, py).wait_send()
+        a_copy(1, 0, diag * 4 + zz, zz, px).wait_send()
+        a_copy(0, 1, py * 4 + zz, zz, py).wait_send()
+        b_copy(1, py * 4 + zz, zz, py).wait_send()
+        a_copy(1, 1, px * 4 + zz, zz, px).wait_send()
+        b_copy(0, px * 4 + zz, zz, px).wait_send()
+        return 0
+    lax.fori_loop(0, 4, drain, 0)
+
+
+def experts(wide, dy, near, far):
     dma = pltpu.SemaphoreType.DMA
-    bf = jnp.bfloat16
-    wide, narrow = y_part.shape[3], d_part.shape[3]
-    rows = y_part.shape[2]
-    vmem = pl.BlockSpec(memory_space=pltpu.VMEM)
-    return pl.pallas_call(
-        combine_kernel,
+    bf, f32 = jnp.bfloat16, jnp.float32
+    wg, wu, wd = near
+    width, half_f = wg.shape
+    rows = wide.shape[2]
+    total_width = 2 * width + EXTRA
+    shape = jax.ShapeDtypeStruct
+    every = 16 * 2 * rows
+    outs = pl.pallas_call(
+        experts_kernel,
         out_shape=(
-            jax.ShapeDtypeStruct((2, rows, wide), jnp.float32),
-            jax.ShapeDtypeStruct((2, rows, narrow), jnp.float32),
+            shape((2, rows, total_width), f32),
+            shape((width, half_f), f32),
+            shape((width, half_f), f32),
+            shape((half_f, width), f32),
+            shape((16, 2, rows, total_width), bf),
+            shape((2, 2, 4, rows, total_width), bf),
+            shape((2, 4, rows, total_width), bf),
+            shape((4, 2, rows, total_width), bf),
         ),
-        in_specs=[ANY, ANY],
-        out_specs=(vmem, vmem),
+        in_specs=[ANY] * 8,
+        out_specs=(pl.BlockSpec(memory_space=pltpu.VMEM),) + (ANY,) * 7,
         scratch_shapes=[
-            pltpu.VMEM(y_part.shape, bf),
-            pltpu.VMEM(d_part.shape, bf),
-            pltpu.VMEM((2, 2, 4, rows, wide), bf),
-            pltpu.VMEM((2, 2, 4, rows, narrow), bf),
-            pltpu.VMEM((2, 4, rows, wide), bf),
-            pltpu.VMEM((2, 4, rows, narrow), bf),
-            pltpu.VMEM((2, 4, rows, wide), bf),
-            pltpu.VMEM((2, 4, rows, narrow), bf),
+            pltpu.VMEM((2, width, half_f), bf),
+            pltpu.VMEM((2, width, half_f), bf),
+            pltpu.VMEM((2, half_f, width), bf),
+            pltpu.VMEM((2, 2, 2, rows, width + EXTRA), bf),
+            pltpu.VMEM((16, 2, rows, width), bf),
+            pltpu.VMEM((16, 2 * rows, 2 * half_f), bf),
+            pltpu.VMEM((16, 2 * rows, 4 * half_f), bf),
+            pltpu.VMEM((2, 256, width), f32),
+            pltpu.VMEM((2, 2, 2, rows, total_width), bf),
+            pltpu.VMEM((2, rows, total_width), bf),
+            pltpu.VMEM((256, every), bf),
+            pltpu.VMEM((2, 16, 2, rows, 256), bf),
+            pltpu.VMEM((2, 256, width), bf),
+            dma((6,)),
+            dma(()),
+            dma((2, 2)),
+            dma((2, 2)),
             dma((2,)),
-            dma((2, 2, 2, 4)),
+            dma((2,)),
+            dma((4,)),
+            dma((2, 2)),
             dma((2, 2, 4)),
+            dma((2, 4)),
+            dma((4,)),
             dma((2, 2, 4)),
-            dma((2, 2, 2, 4)),
-            dma((2, 2, 4)),
-            dma((2, 2, 4)),
+            dma((2, 4)),
+            dma((3,)),
+            dma((2, 2)),
+            dma((8, 2)),
+            dma((2,)),
+            dma((2,)),
+            pltpu.SemaphoreType.REGULAR,
         ],
-        compiler_params=pltpu.CompilerParams(collective_id=2, has_side_effects=True, vmem_limit_bytes=56 * 2**20),
-        name="combine_rows",
-    )(y_part, d_part)
-
-
-def total_kernel(gq, gk, gv, go, small, eg, eu, ed,
-                 out, small_out, eg_far, eu_far, ed_far,
+        compiler_params=pltpu.CompilerParams(collective_id=2, has_side_effects=True, vmem_limit_bytes=62 * 2**20),
+        name="owned_expert",
+    )(wide, dy, *near, *far)
+    return outs[:4]
+
+
+def total_kernel(gq, gk, gv, go, small,
+                 out, small_out,
                  far, a, b, c, mine, work, s_z, s_all,
-                 work_sem, far_sem, a_sem, b_sem, c_sem, e_sem, sz_sem, sa_sem, g_sem,
-                 far_send, a_send, b_send, c_send, e_send, sz_send, sa_send, g_send, out_sem):
+                 work_sem, far_sem, a_sem, b_sem, c_sem, sz_sem, sa_sem, g_sem,
+                 far_send, a_send, b_send, c_send, sz_send, sa_send, g_send, out_sem):
     dp, e, z = place()
     px, py = x_of(e), y_of(e)
     diag = x_of(y_of(e))
@@ -513,10 +811,6 @@
 
     def groups(h):
         return (diag, firsts[h], seconds[h], e)
-
-    def e_copy(i):
-        src, dst = ((eg, eg_far), (eu, eu_far), (ed, ed_far))[i]
-        return copy(src, dst, e_send.at[i], e_sem.at[i], (1 - dp, e, z))
 
     def sz_copy(d):
         return copy(small.at[zs[d]], s_z.at[z], sz_send.at[d - 1], sz_sem.at[z], (dp, e, zs[d]))
@@ -530,8 +824,6 @@
                     far_copy(m, groups(h)[g], zz, h).start()
                 return 0
             lax.fori_loop(0, 4, start_far, 0)
-    for i in range(3):
-        e_copy(i).start()
 
     def a_copy(h, g, zz):
         return copy(far.at[h, groups(h)[g], zz], a.at[h, g, zz], a_send.at[h, g, zz], a_sem.at[h, g, zz],
@@ -650,8 +942,6 @@
             od, oe = lax.rem(dp + d // 4, 2), lax.rem(e + d % 4, 4)
             arrived(out.at[:, pl.ds(pl.multiple_of(oe * 128 + od * 64 + h * 32, 32), 32)],
                     g_sem.at[h, od * 4 + oe], (dp, e, z))
-    for i in range(3):
-        e_copy(i).wait()
     for d in (1, 2, 3):
         sz_copy(d).wait_send()
     for d in range(1, 8):
@@ -680,7 +970,7 @@
         lax.fori_loop(1, 5, drain, 0)
 
 
-def total(gq, gk, gv, go, small, eg, eu, ed):
+def total(gq, gk, gv, go, small):
     dma = pltpu.SemaphoreType.DMA
     bf, f32 = jnp.bfloat16, jnp.float32
     vmem = pl.BlockSpec(memory_space=pltpu.VMEM)
@@ -689,12 +979,9 @@
         out_shape=(
             jax.ShapeDtypeStruct((4, 512, 2048), bf),
             jax.ShapeDtypeStruct(small.shape[1:], f32),
-            jax.ShapeDtypeStruct(eg.shape, bf),
-            jax.ShapeDtypeStruct(eu.shape, bf),
-            jax.ShapeDtypeStruct(ed.shape, bf),
         ),
-        in_specs=[ANY] * 4 + [vmem] + [ANY] * 3,
-        out_specs=(ANY, vmem, ANY, ANY, ANY),
+        in_specs=[ANY] * 4 + [vmem],
+        out_specs=(ANY, vmem),
         scratch_shapes=[
             pltpu.VMEM((2, 4, 4, 4, 32, 2048), bf),
             pltpu.VMEM((2, 2, 4, 4, 32, 2048), bf),
@@ -709,7 +996,6 @@
             dma((2, 2, 4)),
             dma((2, 4)),
             dma((2, 4)),
-            dma((3,)),
             dma((4,)),
             dma((8,)),
             dma((2, 8)),
@@ -718,14 +1004,13 @@
             dma((2, 4)),
             dma((2, 4)),
             dma((3,)),
-            dma((3,)),
             dma((7,)),
             dma((2, 7)),
             dma((2,)),
         ],
         compiler_params=pltpu.CompilerParams(collective_id=3, has_side_effects=True, vmem_limit_bytes=52 * 2**20),
         name="total_grads",
-    )(gq, gk, gv, go, small, eg, eu, ed)
+    )(gq, gk, gv, go, small)
 
 
 def gathered(
@@ -801,40 +1086,10 @@
         [ffn_in, gates_high, gates_low, jnp.zeros((rows, EXTRA - 2 * expert_count), bf)], axis=1)
     spread_rows = spread(sent.reshape(micro_count, seq_len, -1))
 
-    every = 16 * rows
-    wide_rows = spread_rows.reshape(every, -1)
-    dy_rows = dy_all.reshape(every, model_width)
-    expert_rows = wide_rows[:, :model_width]
-    mine = lax.axis_index("expert") * 4 + lax.axis_index("shard")
-    lane = jnp.arange(EXTRA)
-    pick = (lane == mine) | (lane == mine + expert_count)
-    gate_own = jnp.sum(jnp.where(pick[None], wide_rows[:, model_width:].astype(f32), 0.0), axis=1, keepdims=True)
-    dy_route = (gate_own * dy_rows.astype(f32)).astype(bf)
-    halves = ((w_gate[0], w_up[0], w_down[0]), (gate_far, up_far, down_far))
-    y_sum, d_sum, grads = 0.0, 0.0, []
-    for gate_w, up_w, down_w in halves:
-        gate_pre = matmul(expert_rows, gate_w)
-        up_value = matmul(expert_rows, up_w)
-        sigmoid_gate = jax.nn.sigmoid(gate_pre)
-        activated = gate_pre * sigmoid_gate
-        inner = (activated * up_value).astype(bf)
-        y_sum = y_sum + matmul(inner, down_w)
-        d_inner = times_transposed(dy_route, down_w)
-        d_gate = (d_inner * up_value * (sigmoid_gate + gate_pre * sigmoid_gate * (1.0 - sigmoid_gate))).astype(bf)
-        d_up = (d_inner * activated).astype(bf)
-        d_sum = d_sum + times_transposed(d_gate, gate_w) + times_transposed(d_up, up_w)
-        grads.append((transposed_times(expert_rows, d_gate), transposed_times(expert_rows, d_up),
-                      transposed_times(inner, dy_route)))
-    y_low = y_sum.astype(bf).astype(f32)
-    d_gate_own = jnp.sum(y_low * dy_rows.astype(f32), axis=1, keepdims=True)
-    dg_high = d_gate_own.astype(bf).astype(f32)
-    dg_low = d_gate_own - dg_high
-    extra = jnp.where(lane[None] == mine, dg_high, 0.0) + jnp.where(lane[None] == mine + expert_count, dg_low, 0.0)
-    y_part = jnp.concatenate([(gate_own * y_low).astype(bf), extra.astype(bf)], axis=1)
-    y_all, d_all = combine(y_part.reshape(16, micro_count, seq_len, -1),
-                           d_sum.astype(bf).reshape(16, micro_count, seq_len, -1))
-    y_all = y_all.reshape(rows, -1)
-    d_ffn_in = d_all.reshape(rows, -1)
+    expert_sums, *expert_grads = experts(
+        spread_rows, dy_all, (w_gate[0], w_up[0], w_down[0]), (gate_far, up_far, down_far))
+    y_all = expert_sums.reshape(rows, -1)
+    d_ffn_in = y_all[:, model_width + EXTRA:]
     mixed_out = (hidden_state + y_all[:, :model_width]).astype(bf)
     d_gates = y_all[:, model_width:model_width + expert_count] + y_all[
         :, model_width + expert_count:model_width + 2 * expert_count]
@@ -874,10 +1129,7 @@
         [grad_router, d_gain_attn[None], d_gain_ffn[None], d_gain_query[None], d_gain_key[None],
          jnp.zeros((24 - expert_count - 4, model_width), f32)], axis=0)
     small_grads = jnp.swapaxes(small_grads.reshape(24, 4, model_width // 4), 0, 1)
-    near, away = grads
-    sums, small_sums, eg, eu, ed = total(
-        grad_query, grad_key, grad_value, grad_out, small_grads, *(g.astype(bf) for g in away))
-    expert_totals = [(g + other.astype(f32))[None] for g, other in zip(near, (eg, eu, ed))]
+    sums, small_sums = total(grad_query, grad_key, grad_value, grad_out, small_grads)
     return (
         mixed_out.reshape(micro_count, 1, seq_len, model_width),
         grad_tokens,
@@ -890,7 +1142,7 @@
         small_sums[expert_count + 1],
         small_sums[expert_count + 2],
         small_sums[expert_count + 3],
-        *expert_totals,
+        *(g[None] for g in expert_grads),
     )
 
 

time: 1120 us -> 948 us (0.85)
  matrix products: 247 us -> 86.2 us
  Pallas kernels: 739 us -> 766 us
  local copies, waits for them, and re-layouts: 74.4 us -> 51.3 us
  other arithmetic: 48.5 us -> 31.5 us
    dot_general x11 -> x5, matrix products: 95.2 us -> 29.9 us  [times_transposed(): lax.dot_general(left, right, (((1,), (1,)), ((), ())), preferred_element_...]
    dot_general x11 -> x5, matrix products: 80 us -> 24.5 us  [matmul(): return jnp.dot(left, right, preferred_element_type=jnp.float32)]
    dot_general x11 -> x5, matrix products: 64.5 us -> 24.1 us  [transposed_times(): lax.dot_general(left, right, (((0,), (0,)), ((), ())), preferred_element_...]
    pallas_call x1, Pallas kernels: 201 us -> 228 us  [experts(): pl.pallas_call(experts_kernel, out_shape=(shape((2, rows, total_width), f...]
    convert_element_type x1 -> x0, local copies, waits for them, and re-layouts: 13 us -> none  [gathered(): d_gate_own = jnp.sum(y_low * dy_rows.astype(f32), axis=1, keepdims=True)]
    concatenate x1 -> x0, local copies, waits for them, and re-layouts: 11.7 us -> none  [gathered(): jnp.concatenate([(gate_own * y_low).astype(bf), extra.astype(bf)], axis=1)]
    unnamed x227 -> x89, local copies, waits for them, and re-layouts: 22.6 us -> 25.3 us
where the time goes in v2:
time: 948 us; the launch traced here: 937 us
  Pallas kernels  766 us (81%)
  matrix products  86.2 us (9%)
  local copies, waits for them, and re-layouts  51.3 us (5%)
  other arithmetic  31.5 us (3%)
    pallas_call x1, Pallas kernels, total(): pl.pallas_call(total_kernel, out_shape=(jax.ShapeDtypeStruct((4, 512, 204...  278 us
    pallas_call x1, Pallas kernels, experts(): pl.pallas_call(experts_kernel, out_shape=(shape((2, rows, total_width), f...  228 us
    pallas_call x1, Pallas kernels, collect(): pl.pallas_call(collect_kernel, out_shape=(jax.ShapeDtypeStruct((4, 2048,...  183 us
    pallas_call x1, Pallas kernels, spread(): pl.pallas_call(spread_kernel, out_shape=jax.ShapeDtypeStruct((16,) + rows...  77.4 us
    dot_general x5, matrix products, times_transposed(): lax.dot_general(left, right, (((1,), (1,)), ((), ())), preferred_element_...  29.9 us
    unnamed x89, local copies, waits for them, and re-layouts  25.3 us
    dot_general x5, matrix products, matmul(): return jnp.dot(left, right, preferred_element_type=jnp.float32)  24.5 us
    dot_general x5, matrix products, transposed_times(): lax.dot_general(left, right, (((0,), (0,)), ((), ())), preferred_element_...  24.1 us

profile of v2, /device:TPU:13, one launch (start us, length us, event | category | flops | bytes accessed | tf_op | source)
XLA Modules:
  0.0 936.7 jit_solution(647680045877175114)
XLA Ops:
  1.4 1.1 bitcast_select_fusion.1.dy
  6.2 1.6 copy-done
  7.8 1.6 copy-done.1
  9.4 1.6 copy-done.2
  11.0 1.6 copy-done.7
  12.6 1.6 copy-done.8
  14.2 1.6 copy-done.9
  15.8 1.6 copy-done.10
  17.4 182.5 %collect_weights.1 = (bf16[4,2048,2048]{2,1,0:T(8,128)(2,1)}, bf16[4,32,512]{2,1,0:T(8,128)(2,1)S(1)}, bf16[2048,512]{1,0:T(8,128)(2,1)S(1)}, bf16[2048,512]{1,0...) custom-call(bf16[512,2048]{1,0:T(8,128)(2,1)S(1)} %copy-done.7, ...), custom_call_target="tpu_custom_call" | custom-call | tf_op jit(solution)/shard_map/collect_weights/pallas_call | solution.py:300
  200.4 9.5 %multiply_reduce_fusion.10 = (f32[128]{0:T(128)S(1)}, f32[128,2048]{1,0:T(8,128)S(1)}) fusion(bf16[128,2048]{1,0:T(8,128)(2,1)S(1)} %bitcast.255, bf16[4,2048,2048]{2,1,0:T(8,128)(2,1)} %get-tuple-element.27), kind=kOutput, calls=%fused_computation.91 | convolution fusion | flops 1074265984 | bytes 9961984 | tf_op jit(solution)/shard_map/dot_general | solution.py:18
  209.9 4.7 multiply_reduce_fusion.11
  214.7 1.2 multiply_multiply_fusion
  215.9 2.5 copy.146
  218.5 2.3 slice_negate_fusion.2
  220.7 2.4 copy.143
  223.2 2.4 copy.144
  225.6 1.1 multiply_multiply_fusion.1
  226.7 2.5 copy.145
  229.2 2.3 slice_negate_fusion.3
  231.5 2.4 copy.141
  233.9 2.4 copy.142
  240.6 1.2 fusion.86
  241.8 4.6 fusion.48
  246.6 2.2 fusion.51
  249.2 5.3 multiply_reduce_fusion.9
  257.2 77.4 %spread_rows.1.wide = bf16[16,2,64,2176]{3,2,1,0:T(8,128)(2,1)} custom-call(bf16[2,64,2176]{2,1,0:T(8,128)(2,1)} %bitcast.262), custom_call_target="tpu_custom_call" | custom-call | tf_op jit(solution)/shard_map/spread_rows/pallas_call | solution.py:343
  334.6 228.4 %owned_expert.1 = (f32[2,64,4224]{2,1,0:T(8,128)}, f32[2048,512]{1,0:T(8,128)}, f32[2048,512]{1,0:T(8,128)}, f32[512,2048]{1,0:T(8,128)}, bf16[16,2,64,4224]{3,2...) custom-call(bf16[16,2,64,2176]{3,2,1,0:T(8,128)(2,1)} %spread_rows.1, ...), custom_call_target="tpu_custom_call" | custom-call | tf_op jit(solution)/shard_map/owned_expert/pallas_call | solution.py:729
  563.0 1.0 fusion.82
  564.4 2.1 multiply_reduce_fusion.2
  566.6 2.9 multiply_add_fusion.1
  569.5 6.4 fusion.45
  576.7 2.9 fusion.52
  579.7 2.3 copy.135
  581.9 1.6 multiply_reduce_fusion.7
  587.5 2.6 multiply_reduce_fusion.1
  591.5 6.5 fusion.5
  598.0 7.4 fusion.28
  605.5 7.6 multiply_reduce_fusion.3
  613.2 5.6 convolution_convert_fusion.go
  618.8 6.9 convolution_convert_fusion.1.gv
  625.6 5.6 convolution_convert_fusion.2.gk
  631.2 5.9 convolution_convert_fusion.3.gq
  637.1 277.6 %total_grads.1 = (bf16[4,512,2048]{2,1,0:T(8,128)(2,1)}, f32[24,512]{1,0:T(8,128)S(1)}) custom-call(bf16[2048,2048]{1,0:T(8,128)(2,1)} %convolution_convert_fusion.3.gq, bf16[2048,2048]{1,0:T(8,128)(2,1)} %convolution_convert_fusion.2.gk, bf16[2048,2048]{1,0:T(8,128)(2,1)} %convolution_convert_fusion.1.gv, bf16[2048,2048]{1,0:T(8,128)(2,1)} %convolution_convert_fusion.go, ...), custom_call_target="tpu_custom_call" | custom-call | tf_op jit(solution)/shard_map/total_grads/pallas_call | solution.py:977
  914.7 10.2 %bitcast_convert_fusion = (f32[512,2048]{1,0:T(8,128)}, f32[512,2048]{1,0:T(8,128)}, f32[512,2048]{1,0:T(8,128)}, f32[512,2048]{1,0:T(8,128)}) fusion(bf16[4,512,2048]{2,1,0:T(8,128)(2,1)} %get-tuple-element.33), kind=kLoop, calls=%fused_computation.35 | loop fusion | flops 4194304 | bytes 25165824 | tf_op jit(solution)/shard_map/convert_element_type | solution.py:1139
  926.1 1.3 multiply_add_fusion
  927.4 4.8 copy.219
  932.3 2.0 copy.220
  934.3 2.0 copy.221
  (143 shorter events, 20.0 us)
Async XLA Ops:
  0.6 199.3 %copy-start.14 = (bf16[2,1,64,2048]{3,2,1,0:T(8,128)(2,1)S(1)}, bf16[2,1,64,2048]{3,2,1,0:T(8,128)(2,1)}, u32[]{:S(2)}) copy-start(bf16[2,1,64,2048]{3,2,1,0:T(8,128)(2,1)} %param.16) | copy-start | bytes 1572868
  6.2 1.6 copy-start
  7.8 1.6 copy-start.1
  9.4 1.6 copy-start.2
  11.0 1.6 copy-start.7
  12.6 1.6 copy-start.8
  14.2 1.6 copy-start.9
  15.8 1.6 copy-start.10
  199.9 14.7 %copy-start.3 = (bf16[16,2,64,2048]{3,2,1,0:T(8,128)(2,1)}, bf16[16,2,64,2048]{3,2,1,0:T(8,128)(2,1)S(1)}, u32[]{:S(2)}) copy-start(bf16[16,2,64,2048]{3,2,1,0:T(8,128)(2,1)S(1)} %get-tuple-element.28.dy) | copy-start | bytes 25165828
  199.9 14.7 %copy-start.4 = (bf16[2048,512]{1,0:T(8,128)(2,1)}, bf16[2048,512]{1,0:T(8,128)(2,1)S(1)}, u32[]{:S(2)}) copy-start(bf16[2048,512]{1,0:T(8,128)(2,1)S(1)} %get-tuple-element.29.wgf) | copy-start | bytes 6291460
  199.9 14.7 %copy-start.5 = (bf16[2048,512]{1,0:T(8,128)(2,1)}, bf16[2048,512]{1,0:T(8,128)(2,1)S(1)}, u32[]{:S(2)}) copy-start(bf16[2048,512]{1,0:T(8,128)(2,1)S(1)} %get-tuple-element.30.wuf) | copy-start | bytes 6291460
  199.9 14.7 %copy-start.6 = (bf16[512,2048]{1,0:T(8,128)(2,1)}, bf16[512,2048]{1,0:T(8,128)(2,1)S(1)}, u32[]{:S(2)}) copy-start(bf16[512,2048]{1,0:T(8,128)(2,1)S(1)} %get-tuple-element.31.wdf) | copy-start | bytes 6291460
  200.4 41.4 %copy-start.25 = (bf16[2,1,64,2048]{3,2,1,0:T(8,128)(2,1)}, bf16[2,1,64,2048]{3,2,1,0:T(8,128)(2,1)S(1)}, u32[]{:S(2)}) copy-start(bf16[2,1,64,2048]{3,2,1,0:T(8,128)(2,1)S(1)} %multiply_convert_fusion.5) | copy-start | bytes 1572868
  214.7 22.0 %copy-start.11 = (f32[128,2048]{1,0:T(8,128)}, f32[128,2048]{1,0:T(8,128)S(1)}, u32[]{:S(2)}) copy-start(f32[128,2048]{1,0:T(8,128)S(1)} %get-tuple-element.141) | copy-start | bytes 3145732
  236.3 1.2 copy-start.16
  236.3 1.5 copy-start.17
  236.3 1.9 copy-start.18
  236.3 2.2 copy-start.19
  239.1 7.5 copy-start.26
  239.1 7.5 copy-start.28
  239.7 1.0 copy-start.35
  246.6 7.9 copy-start.37
  248.8 7.0 copy-start.38
  249.2 6.3 copy-start.23
  254.6 1.0 copy-start.13
  569.5 12.5 %copy-start.22 = (f32[2,16,64,64]{2,3,1,0:T(8,128)S(1)}, f32[2,16,64,64]{2,3,1,0:T(8,128)}, u32[]{:S(2)}) copy-start(f32[2,16,64,64]{2,3,1,0:T(8,128)} %get-tuple-element.145) | copy-start | bytes 1572868
  579.7 4.2 copy-start.29
  579.7 5.1 copy-start.27
  586.0 1.5 copy-start.12
  590.4 7.6 copy-start.30
  590.7 0.8 copy-start.32
  598.0 7.5 copy-start.15
  598.0 7.5 copy-start.34
  605.4 7.8 copy-start.24
  618.8 6.9 copy-start.33
  625.6 5.6 copy-start.31
  914.7 11.4 %copy-start.36 = (f32[128,2048]{1,0:T(8,128)S(1)}, f32[128,2048]{1,0:T(8,128)}, u32[]{:S(2)}) copy-start(f32[128,2048]{1,0:T(8,128)} %get-tuple-element.153) | copy-start | bytes 3145732
  924.9 7.4 copy-start.21
  927.4 6.8 copy-start.20

commit v3 on v2

--- a/solution.py
+++ b/solution.py
@@ -2,6 +2,7 @@
 
 import jax
 import jax.numpy as jnp
+import numpy as np
 from jax import lax
 from jax.experimental import pallas as pl
 from jax.experimental.pallas import tpu as pltpu
@@ -151,204 +152,535 @@
         self.skip, self.cross, self.cross_recv = skip, cross, cross_recv
 
 
-def gather_items(items, copies, pool):
-    dp, e, z = place()
-    px, py = x_of(e), y_of(e)
-    firsts, seconds = (px, py), (py, px)
-    diag = x_of(y_of(e))
-
-    def onward(item, h, ee, zz, targets, when):
+class Gather:
+    def __init__(self, item, copies, pool):
+        self.item, self.copies, self.pool = item, copies, pool
+        self.dp, self.e, self.z = place()
+        self.px, self.py = x_of(self.e), y_of(self.e)
+        self.diag = x_of(self.py)
+        self.firsts, self.seconds = (self.px, self.py), (self.py, self.px)
+
+    def send(self, h, ee, zz, target, zt, when, own=False):
+        item = self.item
         ref = item.dst(zz, ee, h)
-        sem = item.recv.at[h, ee * 4 + zz]
-        for target, cond in targets:
-            copies.send(ref, ref, pool.take(), sem, target, cond)
+        self.copies.send(item.own(h) if own else ref, ref, self.pool.take(), item.recv.at[h, ee * 4 + zz],
+                         (self.dp, target, zt), when)
+
+    def across(self, h, ee, zz, when):
+        item = self.item
         if item.cross is not None:
-            copies.send(ref, ref, pool.take(), item.cross_recv.at[h, ee * 4 + zz], (1 - dp, e, z), when)
-
-    def wait_for(item, h, ee, zz, when):
+            ref = item.dst(zz, ee, h)
+            self.copies.send(ref, ref, self.pool.take(), item.cross_recv.at[h, ee * 4 + zz],
+                             (1 - self.dp, self.e, self.z), when)
+
+    def wait(self, h, ee, zz, when):
         def body():
-            arrived(item.dst(zz, ee, h), item.recv.at[h, ee * 4 + zz], (dp, e, z))
+            arrived(self.item.dst(zz, ee, h), self.item.recv.at[h, ee * 4 + zz], (self.dp, self.e, self.z))
         if when is None:
             body()
         else:
             pl.when(when)(body)
 
-    def own_stage(k):
+    def steps(self, k):
+        if k == 0:
+            return [(self.z, None, 1)]
+        out = []
+        for sign in (-1, 1):
+            zz = self.z + sign * k
+            out.append((zz, (zz >= 0) & (zz <= 3), sign))
+        return out
+
+    def begin_z(self):
+        for h in (0, 1):
+            for sign in (-1, 1):
+                nxt = self.z + sign
+                self.send(h, self.e, self.z, self.e, nxt, (nxt >= 0) & (nxt <= 3), own=True)
+
+    def begin_plane(self):
+        for h in (0, 1):
+            for target in (self.firsts[h], self.seconds[h]):
+                self.send(h, self.e, self.z, target, self.z, None, own=True)
+
+    def own_stage(self, k):
+        for zz, valid, sign in self.steps(k):
+            nxt = self.z - sign
+            for h in (0, 1):
+                self.wait(h, self.e, zz, valid)
+                self.send(h, self.e, zz, self.e, nxt, valid & (nxt >= 0) & (nxt <= 3))
+                self.send(h, self.e, zz, self.firsts[h], self.z, valid)
+                self.send(h, self.e, zz, self.seconds[h], self.z, valid)
+                self.across(h, self.e, zz, valid)
+
+    def relay_stage(self, k):
+        if k == 0 and self.item.skip:
+            return
+        for zz, valid, _ in self.steps(k):
+            for h in (0, 1):
+                self.wait(h, self.firsts[h], zz, valid)
+                self.send(h, self.firsts[h], zz, self.seconds[h], self.z, valid)
+                self.across(h, self.firsts[h], zz, valid)
+
+    def last_stage(self, k):
+        if k == 0 and self.item.skip:
+            return
+        for zz, valid, _ in self.steps(k):
+            for h in (0, 1):
+                for ee in (self.seconds[h], self.diag):
+                    self.wait(h, ee, zz, valid)
+                    self.across(h, ee, zz, valid)
+
+    def cross_stage(self):
+        if self.item.cross is None:
+            return
+        for k in (1, 2, 3):
+            for zz, valid, _ in self.steps(k):
+                @pl.when(valid)
+                def _(zz=zz):
+                    for ee in range(4):
+                        for h in (0, 1):
+                            arrived(self.item.cross(zz, ee, h), self.item.cross_recv.at[h, ee * 4 + zz],
+                                    (self.dp, self.e, self.z))
+
+    def both_ways(self, h, ee, own=False):
+        for sign in (-1, 1):
+            nxt = self.z + sign
+            self.send(h, ee, self.z, self.e, nxt, (nxt >= 0) & (nxt <= 3), own=own)
+
+    def plane_relay(self):
+        for h in (0, 1):
+            self.wait(h, self.firsts[h], self.z, None)
+            self.send(h, self.firsts[h], self.z, self.seconds[h], self.z, None)
+
+    def line_begin(self, group):
+        for h in (0, 1):
+            if group == 0:
+                self.both_ways(h, self.e, own=True)
+                self.both_ways(h, self.firsts[h])
+            else:
+                for ee in (self.seconds[h], self.diag):
+                    self.wait(h, ee, self.z, None)
+                    self.both_ways(h, ee)
+
+    def line_stage(self, k, group):
+        for zz, valid, sign in self.steps(k):
+            nxt = self.z - sign
+            for h in (0, 1):
+                for ee in ((self.e, self.firsts[h]), (self.seconds[h], self.diag))[group]:
+                    self.wait(h, ee, zz, valid)
+                    self.send(h, ee, zz, self.e, nxt, valid & (nxt >= 0) & (nxt <= 3))
+
+
+class Plane:
+    def __init__(self, own, all_rows, recv, send, relay, cross):
+        self.own, self.all_rows, self.recv = own, all_rows, recv
+        self.send, self.relay, self.cross = send, relay, cross
+        self.dp, self.e, self.z = place()
+        px, py = x_of(self.e), y_of(self.e)
+        self.plane = (px, py, x_of(py))
+        self.half = all_rows.shape[1] // 2
+
+    def at(self, ref, h):
+        return ref.at[pl.ds(h * self.half, self.half)]
+
+    def copy(self, src, slot, h, send_sem, device):
+        return pltpu.make_async_remote_copy(
+            src_ref=src, dst_ref=self.at(self.all_rows.at[slot], h), send_sem=send_sem,
+            recv_sem=self.recv.at[h, slot], device_id=device, device_id_type=MESH_ID)
+
+    def first(self, n, h):
+        target = (1 - self.dp, self.e, self.z) if n == 2 else (self.dp, self.plane[n], self.z)
+        return self.copy(self.at(self.own, h), self.dp * 4 + self.e, h, self.send.at[n, h], target)
+
+    def on(self, h):
+        slot = self.dp * 4 + self.plane[h]
+        return self.copy(self.at(self.all_rows.at[slot], h), slot, h, self.relay.at[h],
+                         (self.dp, self.plane[1 - h], self.z))
+
+    def over(self, n, h):
+        slot = self.dp * 4 + self.plane[n]
+        return self.copy(self.at(self.all_rows.at[slot], h), slot, h, self.cross.at[n, h],
+                         (1 - self.dp, self.e, self.z))
+
+    def wait(self, h, slot):
+        arrived(self.at(self.all_rows.at[slot], h), self.recv.at[h, slot], (self.dp, self.e, self.z))
+
+    def begin(self):
+        for n in range(3):
+            for h in (0, 1):
+                self.first(n, h).start()
+
+    def pass_on(self):
+        for h in (0, 1):
+            self.wait(h, self.dp * 4 + self.plane[h])
+            self.on(h).start()
+            self.over(h, h).start()
+
+    def end(self):
+        for h in (0, 1):
+            self.wait(h, self.dp * 4 + self.plane[1 - h])
+            self.over(1 - h, h).start()
+        for h in (0, 1):
+            self.wait(h, self.dp * 4 + self.plane[2])
+            self.over(2, h).start()
+
+    def end_cross(self):
+        for ee in range(4):
+            for h in (0, 1):
+                self.wait(h, (1 - self.dp) * 4 + ee)
+
+    def drain(self):
+        for h in (0, 1):
+            for n in range(3):
+                self.first(n, h).wait_send()
+                self.over(n, h).wait_send()
+            self.on(h).wait_send()
+
+
+def mates_of():
+    dp, e, z = place()
+    return [(lax.rem(dp + d // 4, 2), lax.rem(e + d % 4, 4), z) for d in range(1, 8)]
+
+
+def columns_of(d, ee):
+    return pl.ds(pl.multiple_of(ee * 512 + d * 256, 256), 256)
+
+
+def as_column(row, count):
+    return jnp.broadcast_to(row, (count, row.shape[1])).T
+
+
+def as_row(column):
+    return jnp.broadcast_to(column, (column.shape[0], 128)).T[0:1]
+
+
+def chosen_experts(route_ids):
+    lane = lax.broadcasted_iota(jnp.int32, (route_ids.shape[0], EXTRA), 1)
+    found = route_ids[:, 0:1] == lane
+    for r in range(1, route_ids.shape[1]):
+        found = found | (route_ids[:, r:r + 1] == lane)
+    return found
+
+
+def allowed_keys(live_row):
+    rows = live_row.shape[1]
+    i = lax.broadcasted_iota(jnp.int32, (rows, rows), 0)
+    j = lax.broadcasted_iota(jnp.int32, (rows, rows), 1)
+    half = rows // 2
+    return ((i < half) == (j < half)) & (j <= i) & (live_row > 0.5)
+
+
+def front_kernel(
+    tok, cot, live, route_ids, cosine, sine, route_in, gains_in, wq, wk, wv, wo, wg, wu, wd,
+    q_raw, k_raw, q_low, k_low, v_low, squares, lives, mixed, hidden, ffn_in, router, small_rows, dy,
+    rows_all, w_cols, w_out, wide_all, dy_all, wg_far, wu_far, wd_far,
+    X, Wc, Wo, R, small, normed, mixed_cols, mixed_own, parts, sent, load_sem, store_sem, x_recv, x_send, x_relay, x_cross,
+    recv_w, recv_o, cross_o, recv_a, recv_b, recv_r, recv_small, recv_far, recv_live, recv_sq, recv_mix,
+    mate_send, send_sems,
+):
+    dp, e, z = place()
+    px, py = x_of(e), y_of(e)
+    me, far = (dp, e, z), (1 - dp, e, z)
+    f32, bf = jnp.float32, jnp.bfloat16
+    rows, width = tok.shape
+    quarter = width // 4
+    slot_z = e * 4 + z
+    slot_me = dp * 4 + e
+    mates = mates_of()
+    own_cols = columns_of(dp, e)
+
+    def local(src, dst, sem):
+        return pltpu.make_async_copy(src, dst, sem)
+
+    z_rows = pl.ds(pl.multiple_of(z * 512, 512), 512)
+    loads = [local(ref.at[:, own_cols], Wc.at[m, z_rows], load_sem.at[m]) for m, ref in enumerate((wq, wk, wv))]
+    loads.append(local(wo, Wo.at[z_rows], load_sem.at[3]))
+    for load in loads:
+        load.start()
+    unit = (lax.broadcasted_iota(jnp.int32, (16, 16), 0) == lax.broadcasted_iota(jnp.int32, (16, 16), 1)).astype(bf)
+    small[0:16] = times_transposed(unit, route_in[...]).astype(bf)
+    small[16:] = gains_in[...]
+    dy_live = jnp.where(as_column(live[0:1], rows)[:, :1] > 0.5, cot[...].astype(f32), 0.0)
+    dy[...] = dy_live.astype(bf).reshape(dy.shape)
+    greet([(dp, e, lax.rem(z + d, 4)) for d in (1, 2, 3)] + mates)
+    copies, pool = Copies(), SemPool(send_sems)
+
+    def to_mates(src, dst, recv_at, kind):
+        for n, mate in enumerate(mates):
+            copies.send(src(mate), dst, mate_send.at[kind, n], recv_at, mate)
+
+    def cols_piece(zz, h):
+        return Wc.at[:, pl.ds(pl.multiple_of(zz * 512 + h * 256, 256), 256), :]
+
+    def cols_send(zz, h, sign, when):
+        nxt = z + sign
+        on = (nxt >= 0) & (nxt <= 3)
+        copies.send(cols_piece(zz, h), cols_piece(zz, h), pool.take(), recv_w.at[h, zz], (dp, e, nxt),
+                    on if when is None else on & when)
+
+    def cols_stage(k):
         for sign in (-1, 1):
             zz = z + sign * k
             valid = (zz >= 0) & (zz <= 3)
-            nxt = z - sign
-            on = valid & (nxt >= 0) & (nxt <= 3)
             for h in (0, 1):
-                for item in items:
-                    wait_for(item, h, e, zz, valid)
-                    onward(item, h, e, zz,
-                           [((dp, e, nxt), on), ((dp, firsts[h], z), valid), ((dp, seconds[h], z), valid)],
-                           valid)
-
-    def relay_stage(k):
-        for sign in (-1, 1) if k else (1,):
-            zz = z + sign * k
-            valid = (zz >= 0) & (zz <= 3) if k else None
-            for h in (0, 1):
-                for item in items:
-                    if k == 0 and item.skip:
-                        continue
-                    wait_for(item, h, firsts[h], zz, valid)
-                    onward(item, h, firsts[h], zz, [((dp, seconds[h], z), valid)], valid)
-
-    def last_stage(k):
-        for sign in (-1, 1) if k else (1,):
-            zz = z + sign * k
-            valid = (zz >= 0) & (zz <= 3) if k else None
-            for h in (0, 1):
-                for item in items:
-                    if k == 0 and item.skip:
-                        continue
-                    for ee in (seconds[h], diag):
-                        wait_for(item, h, ee, zz, valid)
-                        onward(item, h, ee, zz, [], valid)
-
-    for h in (0, 1):
-        for item in items:
-            own, dst, sem = item.own(h), item.dst(z, e, h), item.recv.at[h, e * 4 + z]
-            for sign in (-1, 1):
-                nxt = z + sign
-                copies.send(own, dst, pool.take(), sem, (dp, e, nxt), (nxt >= 0) & (nxt <= 3))
-            if not item.skip:
-                for target in (firsts[h], seconds[h]):
-                    copies.send(own, dst, pool.take(), sem, (dp, target, z))
-    own_stage(1)
-    relay_stage(0)
-    own_stage(2)
-    relay_stage(1)
-    own_stage(3)
-    relay_stage(2)
-    relay_stage(3)
-    for k in range(4):
-        last_stage(k)
-    for item in items:
-        if item.cross is not None:
-            for sign in (-1, 1):
-                for k in (1, 2, 3):
-                    zz = z + sign * k
-
-                    @pl.when((zz >= 0) & (zz <= 3))
-                    def _(item=item, zz=zz):
-                        for ee in range(4):
-                            for h in (0, 1):
-                                arrived(item.cross(zz, ee, h), item.cross_recv.at[h, ee * 4 + zz], (dp, e, z))
-
-
-def collect_kernel(
-    wq, wk, wv, wo, small, wg, wu, wd, dy,
-    full, small_all, wg_far, wu_far, wd_far, dy_all,
-    own4, load_sem, store_sem, recv_w, recv_x, recv_dy, recv_small, recv_far, send_sems,
-):
-    dp, e, z = place()
-    px, py = x_of(e), y_of(e)
-    loads = []
-    for m, ref in enumerate((wq, wk, wv, wo)):
-        load = pltpu.make_async_copy(ref, own4.at[m], load_sem.at[m])
-        load.start()
-        loads.append(load)
-    peers = [(dp, e, lax.rem(z + d, 4)) for d in (1, 2, 3)]
-    peers += [(dp, px, z), (dp, py, z), (1 - dp, e, z)]
-    greet(peers)
-    copies, pool = Copies(), SemPool(send_sems)
+                @pl.when(valid)
+                def _(zz=zz, h=h):
+                    arrived(cols_piece(zz, h), recv_w.at[h, zz], me)
+                cols_send(zz, h, -sign, valid)
+
+    def out_piece(d):
+        def at(zz, ee, h):
+            return Wo.at[pl.ds(pl.multiple_of(zz * 512 + ee * 128 + d * 64 + h * 32, 32), 32), :]
+        return at
+
+    out_at = out_piece(dp)
+    cuts = (32, 32)
+    out_g = Gather(Item(lambda h: out_at(z, e, h), out_at, recv_o, skip=True, cross=out_piece(1 - dp),
+                        cross_recv=cross_o), copies, pool)
+    dy_a = Gather(Item(lambda h: dy.at[h, 0:cuts[h]], lambda zz, ee, h: dy_all.at[ee * 4 + zz, h, 0:cuts[h]], recv_a),
+                  copies, pool)
+    dy_b = Gather(Item(lambda h: dy.at[h, cuts[h]:64], lambda zz, ee, h: dy_all.at[ee * 4 + zz, h, cuts[h]:64], recv_b),
+                  copies, pool)
+    b_all = Gather(Item(lambda h: wide_all.at[slot_z, h], lambda zz, ee, h: wide_all.at[ee * 4 + zz, h], recv_r),
+                   copies, pool)
+    x_plane = Plane(normed, X, x_recv, x_send, x_relay, x_cross)
+
+    for d in (1, 2, 3):
+        copies.send(small, small_rows.at[z], pool.take(), recv_small.at[z], (dp, e, lax.rem(z + d, 4)))
+    to_mates(lambda mate: live, lives.at[slot_me], recv_live.at[slot_me], 0)
+    small_store = local(small, small_rows.at[z], store_sem.at[0])
+    small_store.start()
+    dy_store = local(dy, dy_all.at[slot_z], store_sem.at[1])
+    dy_store.start()
     for load in loads:
         load.wait()
-
-    def row(zz, ee, d, h):
-        return zz * 512 + ee * 128 + d * 64 + h * 32
-
-    def own_w(h):
-        return own4.at[:, pl.ds(pl.multiple_of(e * 128 + dp * 64 + h * 32, 32), 32), :]
-
-    def dst_w(d):
-        return lambda zz, ee, h: full.at[:, pl.ds(pl.multiple_of(row(zz, ee, d, h), 32), 32), :]
-
-    items = [
-        Item(own_w, dst_w(dp), recv_w, skip=True, cross=dst_w(1 - dp), cross_recv=recv_x),
-        Item(lambda h: dy.at[h], lambda zz, ee, h: dy_all.at[ee * 4 + zz, h], recv_dy),
-    ]
-    stores = [
-        pltpu.make_async_copy(own4, full.at[:, pl.ds(pl.multiple_of(z * 512, 512), 512), :], store_sem.at[0]),
-        pltpu.make_async_copy(dy, dy_all.at[e * 4 + z], store_sem.at[1]),
-        pltpu.make_async_copy(small, small_all.at[z], store_sem.at[2]),
-    ]
-    for store in stores:
-        store.start()
-    for d in (1, 2, 3):
-        copies.send(small, small_all.at[z], pool.take(), recv_small.at[z], (dp, e, lax.rem(z + d, 4)))
-    for i, (src, dst) in enumerate(((wg, wg_far), (wu, wu_far), (wd, wd_far))):
-        copies.send(src, dst, pool.take(), recv_far.at[i], (1 - dp, e, z))
-    gather_items(items, copies, pool)
+    for h in (0, 1):
+        for sign in (-1, 1):
+            cols_send(z, h, sign, None)
+    small_store.wait()
     for d in (1, 2, 3):
         zz = lax.rem(z + d, 4)
-        arrived(small_all.at[zz], recv_small.at[zz], (dp, e, z))
+        arrived(small_rows.at[zz], recv_small.at[zz], me)
+    for zz in range(4):
+        R[:, zz * quarter:(zz + 1) * quarter] = small_rows[zz]
+
+    def gain(i):
+        return R[16 + i:17 + i, :].astype(f32)
+
+    def factor(values):
+        return lax.rsqrt(jnp.mean(values * values, axis=1, keepdims=True) + EPSILON)
+
+    x = tok[...].astype(f32)
+    normed[...] = (x * factor(x) * gain(0)).astype(bf)
+    x_plane.begin()
+    x_keep = local(normed, X.at[slot_me], store_sem.at[2])
+    x_keep.start()
+    lives[slot_me] = live[...]
+    dy_a.begin_plane()
+    dy_b.begin_plane()
+    cols_stage(1)
+    out_g.begin_z()
+    x_plane.pass_on()
+    for i, (src, dst) in enumerate(((wg, wg_far), (wu, wu_far), (wd, wd_far))):
+        copies.send(src, dst, pool.take(), recv_far.at[i], far)
+    dy_a.relay_stage(0)
+    dy_b.plane_relay()
+    cols_stage(2)
+    x_plane.end()
+    out_g.own_stage(1)
+    dy_a.begin_z()
+    x_plane.end_cross()
+    x_keep.wait()
+    for n in range(7):
+        od, oe, _ = mates[n]
+        arrived(lives.at[od * 4 + oe], recv_live.at[od * 4 + oe], me)
+    rows_store = local(X, rows_all, store_sem.at[3])
+    rows_store.start()
+    cols_stage(3)
+    cols_store = local(Wc, w_cols, store_sem.at[5])
+    cols_store.start()
+    out_g.relay_stage(1)
+
+    def project(g, _):
+        at = pl.ds(g * 4, 4)
+        block = X[at].reshape(4 * rows, width)
+        for m, ref in enumerate((q_raw, k_raw)):
+            ref[at] = jnp.dot(block, Wc[m], preferred_element_type=f32).reshape(4, rows, 256)
+        v_low[at] = jnp.dot(block, Wc[2], preferred_element_type=f32).astype(bf).reshape(4, rows, 256)
+        for i in range(4):
+            for m, ref in enumerate((q_raw, k_raw)):
+                values = ref[g * 4 + i]
+                parts[slot_me, m, pl.ds(g * 4 + i, 1), :] = as_row(jnp.sum(values * values, axis=1, keepdims=True))
+        return 0
+
+    lax.fori_loop(0, 2, project, 0)
+    to_mates(lambda mate: parts.at[slot_me], parts.at[slot_me], recv_sq.at[slot_me], 1)
+    out_g.own_stage(2)
+    dy_b.line_begin(0)
+    for n in range(7):
+        od, oe, _ = mates[n]
+        arrived(parts.at[od * 4 + oe], recv_sq.at[od * 4 + oe], me)
+    squares[...] = (((parts[0] + parts[1]) + (parts[2] + parts[3]))
+                    + ((parts[4] + parts[5]) + (parts[6] + parts[7]))) * (1.0 / width)
+    cos_t = jnp.concatenate([cosine[...]] * 2, axis=0)
+    sin_t = jnp.concatenate([sine[...]] * 2, axis=0)
+
+    def attend(d, _):
+        allowed = allowed_keys(lives[d][0:1])
+        for m, (raw, low) in enumerate(((q_raw, q_low), (k_raw, k_low))):
+            scale = lax.rsqrt(as_column(squares[m, pl.ds(d, 1), :], HDIM) + EPSILON)
+            for hh in range(2):
+                cc = slice(hh * HDIM, (hh + 1) * HDIM)
+                gains = R[18 + m:19 + m, pl.ds(pl.multiple_of(e * 512 + dp * 256 + hh * HDIM, HDIM), HDIM)].astype(f32)
+                u = raw[d, :, cc] * scale * gains
+                low[d, :, cc] = (u * cos_t + pltpu.roll(u, HDIM // 2, 1) * sin_t).astype(bf)
+        for hh in range(2):
+            cc = slice(hh * HDIM, (hh + 1) * HDIM)
+            scores = times_transposed(q_low[d, :, cc], k_low[d, :, cc]) * (HDIM ** (-0.5))
+            probs = softmax_rows(jnp.where(allowed, scores, -1e30))
+            mixed_cols[d, :, cc] = jnp.dot(probs.astype(bf), v_low[d, :, cc], preferred_element_type=f32).astype(bf)
+        return 0
+
+    lax.fori_loop(0, 4, attend, 0)
+    out_g.relay_stage(2)
+    out_g.own_stage(3)
+    dy_b.line_begin(1)
+    lax.fori_loop(4, 8, attend, 0)
+    to_mates(lambda mate: mixed_cols.at[mate[0] * 4 + mate[1]], mixed_own.at[:, own_cols], recv_mix.at[slot_me], 2)
+    mixed_own[:, own_cols] = mixed_cols[slot_me]
+    out_g.last_stage(1)
+    out_g.relay_stage(3)
+    dy_a.own_stage(1)
+    for n in range(7):
+        od, oe, _ = mates[n]
+        arrived(mixed_own.at[:, columns_of(od, oe)], recv_mix.at[od * 4 + oe], me)
+    mixed[...] = mixed_own[...]
+    out_g.last_stage(2)
+    dy_b.line_stage(1, 0)
+    dy_a.relay_stage(1)
+    out_g.last_stage(3)
+    out_g.cross_stage()
+    full_o = local(Wo, w_out, store_sem.at[4])
+    full_o.start()
+
+    def out_col(j, _):
+        cc = pl.ds(pl.multiple_of(j * 512, 512), 512)
+        hidden[:, cc] = tok[:, cc].astype(f32) + jnp.dot(mixed[...], Wo[:, cc], preferred_element_type=f32)
+        return 0
+
+    lax.fori_loop(0, 4, out_col, 0)
+    h1 = hidden[...]
+    b = (h1 * factor(h1) * gain(1)).astype(bf)
+    ffn_in[...] = b
+    lane = lax.broadcasted_iota(jnp.int32, (rows, EXTRA), 1)
+    logits = jnp.where(lane < 16, times_transposed(b, R[...]), -1e30)
+    picks = softmax_rows(logits)
+    router[...] = picks
+    gates = jnp.where(chosen_experts(route_ids[...]), picks, 0.0)
+    high = gates.astype(bf).astype(f32)
+    extra = high + pltpu.roll(gates - high, 16, 1)
+    sent[:, :, :width] = b.reshape(2, rows // 2, width)
+    sent[:, :, width:] = extra.astype(bf).reshape(2, rows // 2, EXTRA)
+    keep = local(sent, wide_all.at[slot_z], store_sem.at[6])
+    keep.start()
+    keep.wait()
+    b_all.begin_plane()
+    b_all.begin_z()
+    dy_a.own_stage(2)
+    dy_b.line_stage(1, 1)
+    dy_a.relay_stage(2)
+    b_all.relay_stage(0)
+    b_all.own_stage(1)
+    dy_a.own_stage(3)
+    dy_b.line_stage(2, 0)
+    b_all.relay_stage(1)
+    b_all.own_stage(2)
+    dy_a.relay_stage(3)
+    dy_b.line_stage(2, 1)
+    b_all.relay_stage(2)
+    b_all.own_stage(3)
+    b_all.relay_stage(3)
+    for group in (0, 1):
+        dy_b.line_stage(3, group)
+    for k in range(4):
+        dy_a.last_stage(k)
+    for k in range(4):
+        b_all.last_stage(k)
     for i, dst in enumerate((wg_far, wu_far, wd_far)):
-        arrived(dst, recv_far.at[i], (dp, e, z))
+        arrived(dst, recv_far.at[i], me)
     copies.drain()
-    for store in stores:
+    x_plane.drain()
+    for store in (dy_store, full_o, rows_store, cols_store):
         store.wait()
 
 
-def collect(wq, wk, wv, wo, small, wg, wu, wd, dy):
-    bf = jnp.bfloat16
+def front(tok, cot, live, route_ids, cosine, sine, route_in, gains_in, *weights):
+    bf, f32 = jnp.bfloat16, jnp.float32
     dma = pltpu.SemaphoreType.DMA
+    shape = jax.ShapeDtypeStruct
+    vmem = pl.BlockSpec(memory_space=pltpu.VMEM)
+    rows, width = tok.shape
+    wg, wu, wd = weights[4:]
     return pl.pallas_call(
-        collect_kernel,
+        front_kernel,
         out_shape=(
-            jax.ShapeDtypeStruct((4, 2048, 2048), bf),
-            jax.ShapeDtypeStruct((4,) + small.shape, bf),
-            jax.ShapeDtypeStruct(wg.shape, bf),
-            jax.ShapeDtypeStruct(wu.shape, bf),
-            jax.ShapeDtypeStruct(wd.shape, bf),
-            jax.ShapeDtypeStruct((16,) + dy.shape, bf),
+            shape((8, rows, 256), f32),
+            shape((8, rows, 256), f32),
+            shape((8, rows, 256), bf),
+            shape((8, rows, 256), bf),
+            shape((8, rows, 256), bf),
+            shape((2, 8, rows), f32),
+            shape((8, 8, rows), f32),
+            shape((rows, width), bf),
+            shape((rows, width), f32),
+            shape((rows, width), bf),
+            shape((rows, EXTRA), f32),
+            shape((4, EXTRA, width // 4), bf),
+            shape((2, rows // 2, width), bf),
+            shape((8, rows, width), bf),
+            shape((3, width, 256), bf),
+            shape((width, width), bf),
+            shape((16, 2, rows // 2, width + EXTRA), bf),
+            shape((16, 2, rows // 2, width), bf),
+            shape(wg.shape, bf),
+            shape(wu.shape, bf),
+            shape(wd.shape, bf),
         ),
-        in_specs=[ANY] * 8 + [pl.BlockSpec(memory_space=pltpu.VMEM)],
-        out_specs=(ANY,) * 6,
+        in_specs=[vmem] * 8 + [ANY] * 7,
+        out_specs=(vmem,) * 13 + (ANY,) * 8,
         scratch_shapes=[
-            pltpu.VMEM((4, 512, 2048), bf),
+            pltpu.VMEM((8, rows, width), bf),
+            pltpu.VMEM((3, width, 256), bf),
+            pltpu.VMEM((width, width), bf),
+            pltpu.VMEM((EXTRA, width), bf),
+            pltpu.VMEM((EXTRA, width // 4), bf),
+            pltpu.VMEM((rows, width), bf),
+            pltpu.VMEM((8, rows, 256), bf),
+            pltpu.VMEM((rows, width), bf),
+            pltpu.VMEM((8, 2, 8, rows), f32),
+            pltpu.VMEM((2, rows // 2, width + EXTRA), bf),
             dma((4,)),
-            dma((3,)),
+            dma((7,)),
+            dma((2, 8)),
+            dma((3, 2)),
+            dma((2,)),
+            dma((3, 2)),
+            dma((2, 4)),
+            dma((2, 16)),
+            dma((2, 16)),
             dma((2, 16)),
             dma((2, 16)),
             dma((2, 16)),
             dma((4,)),
             dma((3,)),
-            dma((192,)),
+            dma((8,)),
+            dma((8,)),
+            dma((8,)),
+            dma((3, 7)),
+            dma((330,)),
         ],
-        compiler_params=pltpu.CompilerParams(collective_id=0, has_side_effects=True, vmem_limit_bytes=24 * 2**20),
-        name="collect_weights",
-    )(wq, wk, wv, wo, small, wg, wu, wd, dy)
-
-
-def spread_kernel(rows, rows_all, store_sem, recv, send_sems):
-    dp, e, z = place()
-    px, py = x_of(e), y_of(e)
-    peers = [(dp, e, lax.rem(z + d, 4)) for d in (1, 2, 3)] + [(dp, px, z), (dp, py, z)]
-    greet(peers)
-    copies, pool = Copies(), SemPool(send_sems)
-    store = pltpu.make_async_copy(rows, rows_all.at[e * 4 + z], store_sem)
-    store.start()
-    gather_items([Item(lambda h: rows.at[h], lambda zz, ee, h: rows_all.at[ee * 4 + zz, h], recv)], copies, pool)
-    copies.drain()
-    store.wait()
-
-
-def spread(rows):
-    dma = pltpu.SemaphoreType.DMA
-    return pl.pallas_call(
-        spread_kernel,
-        out_shape=jax.ShapeDtypeStruct((16,) + rows.shape, rows.dtype),
-        in_specs=[pl.BlockSpec(memory_space=pltpu.VMEM)],
-        out_specs=ANY,
-        scratch_shapes=[dma(()), dma((2, 16)), dma((96,))],
-        compiler_params=pltpu.CompilerParams(collective_id=1, has_side_effects=True),
-        name="spread_rows",
-    )(rows)
+        compiler_params=pltpu.CompilerParams(collective_id=0, has_side_effects=True, vmem_limit_bytes=62 * 2**20),
+        name="attention_front",
+    )(tok, cot, live, route_ids, cosine, sine, route_in, gains_in, *weights)
 
 
 def times(left, right):
@@ -357,8 +689,8 @@
 
 def experts_kernel(
     wide, dy, wg, wu, wd, wgf, wuf, wdf,
-    res, eg, eu, ed, part, a_buf, b_buf, c_buf,
-    WG, WU, WD, rows_in, dy_rows, hidden, saved, acc, stage, addend, turned, column, far_out,
+    res, eg, eu, ed, part, a_buf, b_buf,
+    c_buf, WG, WU, WD, rows_in, dy_rows, hidden, saved, acc, stage, addend, turned, column, far_out,
     w_sem, dy_sem, in_sem, part_sem, add_sem, col_sem, fin_sem, out_sem,
     a_sem, b_sem, c_sem, a_send, b_send, c_send, gu_send, gu_sem, dn_send, dn_sem, free_sem,
 ):
@@ -386,8 +718,14 @@
     def zed(i):
         return lax.rem(z + jnp.where(i == 0, 2, jnp.where(i == 1, 1, jnp.where(i == 2, 3, 0))), 4)
 
+    def kind_of(s):
+        return jnp.where(s < 2, 0, jnp.where(s < 4, 3, 1 + lax.rem(s, 2)))
+
+    def zed_of(s, i):
+        return zed(2 * jnp.where(s < 4, lax.rem(s, 2), (s - 4) // 2) + i)
+
     def slot_of(s, i):
-        return column_of(s // 2) * 4 + zed(2 * lax.rem(s, 2) + i)
+        return column_of(kind_of(s)) * 4 + zed_of(s, i)
 
     def rows_load(s, i, buf):
         return local(wide.at[slot_of(s, i)], rows_in.at[buf, i], in_sem.at[buf, i])
@@ -401,10 +739,16 @@
         rows_load(0, i, 0).start()
     weights[0].start()
     weights[1].start()
-    dy_load = local(dy, dy_rows, dy_sem)
-    dy_load.start()
+    def dy_load(s, i):
+        return local(dy.at[slot_of(s, i)], dy_rows.at[slot_of(s, i)], dy_sem.at[s, i])
+
+    for i in range(2):
+        dy_load(0, i).start()
     for load in weights[2:]:
         load.start()
+    for s in range(1, 8):
+        for i in range(2):
+            dy_load(s, i).start()
     greet([(dp, e, lax.rem(z + d, 4)) for d in (1, 2, 3)] + [(dp, px, z), (dp, py, z), far_core])
 
     def part_write(s, i):
@@ -417,10 +761,10 @@
         return remote(part.at[slot, h], b_buf.at[h, zz], b_send.at[h, zz], b_sem.at[h, zz], (dp, target, z))
 
     def send_step(s):
-        c = s // 2
+        c = kind_of(s)
         for i in range(2):
             part_write(s, i).wait()
-            zz = zed(2 * lax.rem(s, 2) + i)
+            zz = zed_of(s, i)
 
             @pl.when(c == 0)
             def _():
@@ -438,17 +782,17 @@
                 b_copy(0, px * 4 + zz, zz, px).start()
 
     def addend_load(s, i):
-        h = jnp.where(s // 2 == 1, 1, 0)
-        zz = zed(2 * lax.rem(s, 2) + i)
+        h = jnp.where(kind_of(s) == 1, 1, 0)
+        zz = zed_of(s, i)
         return local(a_buf.at[h, 0, zz], addend.at[i], add_sem.at[i])
 
     mine = e * 4 + z
+    route_rows = turned
     lane = lax.broadcasted_iota(jnp.int32, (256, EXTRA), 1)
     at_high, at_low = lane == mine, lane == mine + 16
 
     weights[0].wait()
     weights[1].wait()
-    dy_load.wait()
 
     def step(s, _):
         buf = lax.rem(s, 2)
@@ -459,6 +803,7 @@
                 rows_load(s + 1, i, 1 - buf).start()
         for i in range(2):
             rows_load(s, i, buf).wait()
+            dy_load(s, i).wait()
         slots = [slot_of(s, i) for i in range(2)]
         extra = rows_in[buf, :, :, :, width:].reshape(256, EXTRA).astype(f32)
         gate = jnp.sum(jnp.where(at_high | at_low, extra, 0.0), axis=1, keepdims=True)
@@ -466,51 +811,52 @@
         def dy_step():
             return jnp.concatenate([dy_rows[slot].reshape(128, width) for slot in slots], axis=0)
 
-        def put(ref, values, lo, hi):
+        def put(ref, values, at):
             for i in range(2):
-                ref[slots[i], :, lo:hi] = values[i * 128:(i + 1) * 128]
+                ref[slots[i], :, pl.ds(pl.multiple_of(at, half_f), half_f)] = values[i * 128:(i + 1) * 128]
 
         dy_route = (gate * dy_step().astype(f32)).astype(bf)
-        for n in range(2):
-            if n == 1:
-                @pl.when(s == 0)
-                def _():
-                    for load in weights[3:]:
-                        load.wait()
-
-                @pl.when(s > 0)
-                def _():
-                    send_step(s - 1)
-
-                @pl.when((s >= 2) & (s < 6))
-                def _():
-                    for i in range(2):
-                        h = jnp.where(s // 2 == 1, 1, 0)
-                        zz = zed(2 * lax.rem(s, 2) + i)
-                        arrived(a_buf.at[h, 0, zz], a_sem.at[h, 0, zz], me)
-                        addend_load(s, i).start()
+        route_rows[...] = dy_route
+        acc[...] = jnp.zeros_like(acc)
+
+        def half_step(n, _):
+            @pl.when((s == 0) & (n == 1))
+            def _():
+                for load in weights[3:]:
+                    load.wait()
+
+            @pl.when((s > 0) & (n == 1))
+            def _():
+                send_step(s - 1)
+
+            @pl.when((s >= 4) & (n == 1))
+            def _():
+                for i in range(2):
+                    h = jnp.where(kind_of(s) == 1, 1, 0)
+                    zz = zed_of(s, i)
+                    arrived(a_buf.at[h, 0, zz], a_sem.at[h, 0, zz], me)
+                    addend_load(s, i).start()
             x = rows_in[buf, :, :, :, :width].reshape(256, width)
             gate_pre = times(x, WG[n])
             up_value = times(x, WU[n])
             sigmoid_gate = jax.nn.sigmoid(gate_pre)
             activated = gate_pre * sigmoid_gate
             inner = (activated * up_value).astype(bf)
-            put(hidden, inner, n * half_f, (n + 1) * half_f)
-            if n == 0:
-                @pl.when(s == 0)
-                def _():
-                    weights[2].wait()
-            d_inner = times_transposed(dy_route, WD[n])
+            put(hidden, inner, n * half_f)
+
+            @pl.when((s == 0) & (n == 0))
+            def _():
+                weights[2].wait()
+            d_inner = times_transposed(route_rows[...], WD[n])
             d_gate = (d_inner * up_value * (sigmoid_gate + gate_pre * sigmoid_gate * (1.0 - sigmoid_gate))).astype(bf)
             d_up = (d_inner * activated).astype(bf)
-            put(saved, d_gate, 2 * n * half_f, (2 * n + 1) * half_f)
-            put(saved, d_up, (2 * n + 1) * half_f, (2 * n + 2) * half_f)
-            if n == 0:
-                acc[0] = times(inner, WD[n])
-                acc[1] = times_transposed(d_gate, WG[n]) + times_transposed(d_up, WU[n])
-            else:
-                acc[0] += times(inner, WD[n])
-                acc[1] += times_transposed(d_gate, WG[n]) + times_transposed(d_up, WU[n])
+            put(saved, d_gate, 2 * n * half_f)
+            put(saved, d_up, (2 * n + 1) * half_f)
+            acc[0] += times(inner, WD[n])
+            acc[1] += times_transposed(d_gate, WG[n]) + times_transposed(d_up, WU[n])
+            return 0
+
+        lax.fori_loop(0, 2, half_step, 0)
         y_low = acc[0].astype(bf).astype(f32)
         d_own = jnp.sum(y_low * dy_step().astype(f32), axis=1, keepdims=True)
         high = d_own.astype(bf).astype(f32)
@@ -523,11 +869,11 @@
         stage[buf, :, :, :, width:width + EXTRA] = lay(tail)
         stage[buf, :, :, :, width + EXTRA:] = lay(acc[1].astype(bf))
         for i in range(2):
-            dy_rows[slots[i]] = dy_route[i * 128:(i + 1) * 128].reshape(2, 64, width)
-
-        @pl.when((s >= 2) & (s < 6))
+            dy_rows[slots[i]] = route_rows[i * 128:(i + 1) * 128].reshape(2, 64, width)
+
+        @pl.when(s >= 4)
         def _():
-            h = jnp.where(s // 2 == 1, 1, 0)
+            h = jnp.where(kind_of(s) == 1, 1, 0)
             for i in range(2):
                 addend_load(s, i).wait()
                 stage[buf, i, h] = (stage[buf, i, h].astype(f32) + addend[i].astype(f32)).astype(bf)
@@ -537,8 +883,7 @@
 
     lax.fori_loop(0, 8, step, 0)
     pl.semaphore_signal(free_sem, inc=1, device_id=far_core, device_id_type=MESH_ID)
-    for i in range(2):
-        part_write(7, i).wait()
+    send_step(7)
 
     def finish_loads(k):
         zz = zed(k)
@@ -559,7 +904,8 @@
 
     def c_copy(k):
         zz = zed(k)
-        return remote(part.at[e * 4 + zz], c_buf.at[z], c_send.at[k], c_sem.at[z], (dp, e, zz))
+        there = (0, 2, 1)[k]
+        return remote(part.at[e * 4 + zz], c_buf.at[there], c_send.at[k], c_sem.at[there], (dp, e, zz))
 
     def close(k):
         for load in finish_loads(k):
@@ -694,13 +1040,9 @@
     begin(3)
     close(3)
     for k in range(3):
-        zz = zed(k)
-        arrived(c_buf.at[zz], c_sem.at[zz], me)
-        load = local(c_buf.at[zz], stage.at[0, 0], fin_sem.at[0])
-        load.start()
-        load.wait()
+        arrived(c_buf.at[k], c_sem.at[k], me)
         for h in range(2):
-            res[h] += stage[0, 0, h].astype(f32)
+            res[h] += c_buf[k, h].astype(f32)
     for n in range(2):
         down_out(n).wait()
     for k in range(3):
@@ -736,11 +1078,11 @@
             shape((16, 2, rows, total_width), bf),
             shape((2, 2, 4, rows, total_width), bf),
             shape((2, 4, rows, total_width), bf),
-            shape((4, 2, rows, total_width), bf),
         ),
         in_specs=[ANY] * 8,
-        out_specs=(pl.BlockSpec(memory_space=pltpu.VMEM),) + (ANY,) * 7,
+        out_specs=(pl.BlockSpec(memory_space=pltpu.VMEM),) + (ANY,) * 6,
         scratch_shapes=[
+            pltpu.VMEM((3, 2, rows, total_width), bf),
             pltpu.VMEM((2, width, half_f), bf),
             pltpu.VMEM((2, width, half_f), bf),
             pltpu.VMEM((2, half_f, width), bf),
@@ -755,7 +1097,7 @@
             pltpu.VMEM((2, 16, 2, rows, 256), bf),
             pltpu.VMEM((2, 256, width), bf),
             dma((6,)),
-            dma(()),
+            dma((8, 2)),
             dma((2, 2)),
             dma((2, 2)),
             dma((2,)),
@@ -774,243 +1116,422 @@
             dma((2,)),
             pltpu.SemaphoreType.REGULAR,
         ],
-        compiler_params=pltpu.CompilerParams(collective_id=2, has_side_effects=True, vmem_limit_bytes=62 * 2**20),
+        compiler_params=pltpu.CompilerParams(collective_id=2, has_side_effects=True, vmem_limit_bytes=67043328),
         name="owned_expert",
     )(wide, dy, *near, *far)
     return outs[:4]
 
 
-def total_kernel(gq, gk, gv, go, small,
-                 out, small_out,
-                 far, a, b, c, mine, work, s_z, s_all,
-                 work_sem, far_sem, a_sem, b_sem, c_sem, sz_sem, sa_sem, g_sem,
-                 far_send, a_send, b_send, c_send, sz_send, sa_send, g_send, out_sem):
+def back_kernel(
+    sums, tok, route_ids, cosine, sine, dy, mixed, q_raw, k_raw, q_low, k_low, v_low, squares, lives, hidden, ffn_in,
+    router, small_rows, rows_all, w_cols, w_out,
+    mixed_out, grad_tokens, out, small_out,
+    Wo, Wc, R, d_hidden, d_heads, DH, d_mix, g_q, g_k, parts, means, X, D, turned, G, own_sum, hop, send_buf, mine,
+    far_rows, home_rows, small, s_z, s_all,
+    w_sem, load_sem, x_recv, x_send, x_relay, x_cross, d_sem, d_send, h_sem, h_send, q_sem, q_send,
+    hop_sem, hop_send, f_sem, f_send, r_sem, r_send, sz_sem, sz_send, sa_sem, sa_send,
+    g_sem, g_send, g_pass, g_far, out_sem,
+):
     dp, e, z = place()
     px, py = x_of(e), y_of(e)
-    diag = x_of(y_of(e))
-    firsts, seconds = (py, px), (px, py)
-    grads = (gq, gk, gv, go)
+    diag = x_of(py)
+    plane = (px, py, diag)
+    me, far = (dp, e, z), (1 - dp, e, z)
+    f32, bf = jnp.float32, jnp.bfloat16
+    rows, width = tok.shape
+    quarter = width // 4
+    slot_me = dp * 4 + e
     zs = [lax.rem(z + d, 4) for d in range(4)]
-    mates = [(lax.rem(dp + d // 4, 2), lax.rem(e + d % 4, 4), z) for d in range(1, 8)]
-    greet([(dp, e, zz) for zz in zs[1:]] + mates)
-
-    def copy(src, dst, send_sem, recv_sem, device):
+    mates = mates_of()
+    own_cols = columns_of(dp, e)
+
+    def local(src, dst, sem):
+        return pltpu.make_async_copy(src, dst, sem)
+
+    def remote(src, dst, send_sem, recv_sem, device):
         return pltpu.make_async_remote_copy(
             src_ref=src, dst_ref=dst, send_sem=send_sem, recv_sem=recv_sem,
             device_id=device, device_id_type=MESH_ID)
 
-    def rows_of(ee, zz, d, h):
-        return pl.ds(pl.multiple_of(zz * 512 + ee * 128 + d * 64 + h * 32, 32), 32)
-
-    def far_copy(m, ee, zz, h):
-        return copy(grads[m].at[rows_of(ee, zz, 1 - dp, h)], far.at[h, ee, zz, m],
-                    far_send.at[h, ee, zz, m], far_sem.at[h, ee, zz, m], (1 - dp, e, z))
-
-    def load(m, ee, zz, h, slot):
-        return pltpu.make_async_copy(grads[m].at[rows_of(ee, zz, dp, h)], work.at[slot, m], work_sem.at[slot, m])
-
-    def groups(h):
-        return (diag, firsts[h], seconds[h], e)
+    load_out = local(w_out, Wo, w_sem.at[0])
+    load_cols = local(w_cols, Wc, w_sem.at[1])
+    load_rows = local(rows_all, X.at[0], load_sem.at[0])
+    load_mixed = local(mixed, X.at[1, slot_me], load_sem.at[1])
+    for load in (load_out, load_mixed, load_cols, load_rows):
+        load.start()
+    greet([(dp, e, zz) for zz in zs[1:]] + mates)
+    m_plane = Plane(mixed, X.at[1], x_recv, x_send, x_relay, x_cross)
+    m_plane.begin()
+
+    def d_copy(n):
+        od, oe, _ = mates[n]
+        return remote(d_mix.at[:, columns_of(od, oe)], D.at[3, slot_me], d_send.at[n], d_sem.at[slot_me], mates[n])
+
+    def h_copy(n):
+        od, oe, _ = mates[n]
+        return remote(d_heads.at[:, columns_of(od, oe)], DH.at[slot_me], h_send.at[n], h_sem.at[slot_me], mates[n])
+
+    def q_copy(n):
+        return remote(parts.at[slot_me], parts.at[slot_me], q_send.at[n], q_sem.at[slot_me], mates[n])
+
+    def from_mates(ref, sem):
+        for n in range(7):
+            od, oe, _ = mates[n]
+            arrived(ref.at[od * 4 + oe], sem.at[od * 4 + oe], me)
+
+    def compute(m, i, buf):
+        turned[...] = D[m].reshape(8 * rows, 256).T
+
+        def block(zz, _):
+            at = pl.ds(pl.multiple_of(zz * 512, 512), 512)
+            G[buf, zz] = jnp.dot(turned[...], X[i, :, :, at].reshape(8 * rows, 512), preferred_element_type=f32)
+            return 0
+        lax.fori_loop(0, 4, block, 0)
+        own_sum[m] = G[buf, z]
+
+    middle = (z == 1) | (z == 2)
+    lower = z < 2
+    targets = (jnp.where(lower, 3, 0), jnp.where(lower, 2, 1), z + 1 - 2 * lax.rem(z, 2))
+
+    def hop_copy(m, j):
+        zt = targets[j]
+        up = zt > z
+        there = jnp.where(zt == z - 1, 4, zt)
+        return remote(send_buf.at[m, j], hop.at[m, there], hop_send.at[m, j], hop_sem.at[m, there],
+                      (dp, e, jnp.where(up, z + 1, z - 1)))
+
+    def pass_on(m, buf):
+        for j in range(3):
+            zt = targets[j]
+
+            @pl.when(middle)
+            def _():
+                arrived(hop.at[m, zt], hop_sem.at[m, zt], me)
+                send_buf[m, j] = (G[buf, zt] + hop[m, zt].astype(f32)).astype(bf)
+
+            @pl.when(jnp.logical_not(middle))
+            def _():
+                send_buf[m, j] = G[buf, zt].astype(bf)
+            hop_copy(m, j).start()
+
+    def out_at(m, d, ee, h):
+        return out.at[m, pl.ds(h * 256, 256), columns_of(d, ee)]
+
+    def g_copy(m, n, h):
+        return remote(mine.at[m, pl.ds(h * 256, 256)], out_at(m, dp, e, h), g_send.at[m, n, h],
+                      g_sem.at[m, h, slot_me], far if n == 2 else (dp, plane[n], z))
+
+    def g_relay(m, h):
+        ref = out_at(m, dp, plane[h], h)
+        return remote(ref, ref, g_pass.at[m, h], g_sem.at[m, h, dp * 4 + plane[h]], (dp, plane[1 - h], z))
+
+    def g_onward(m, n, h):
+        ref = out_at(m, dp, plane[n], h)
+        return remote(ref, ref, g_far.at[m, n, h], g_sem.at[m, h, dp * 4 + plane[n]], far)
+
+    def wait_g(m, h, d, ee):
+        arrived(out_at(m, d, ee, h), g_sem.at[m, h, d * 4 + ee], me)
+
+    def keep(m):
+        return local(mine.at[m], out.at[m, :, own_cols], out_sem.at[m])
+
+    def finish(m):
+        @pl.when(z > 0)
+        def _():
+            arrived(hop.at[m, z], hop_sem.at[m, z], me)
+            own_sum[m] += hop[m, z].astype(f32)
+
+        @pl.when(z < 3)
+        def _():
+            arrived(hop.at[m, 4], hop_sem.at[m, 4], me)
+            own_sum[m] += hop[m, 4].astype(f32)
+        mine[m] = own_sum[m].T.astype(bf)
+        for h in (0, 1):
+            for n in range(3):
+                g_copy(m, n, h).start()
+        keep(m).start()
+
+    def relay_out(m):
+        for h in (0, 1):
+            wait_g(m, h, dp, plane[h])
+            g_relay(m, h).start()
+            g_onward(m, h, h).start()
+
+    def end_out(m):
+        for h in (0, 1):
+            wait_g(m, h, dp, plane[1 - h])
+            g_onward(m, 1 - h, h).start()
+        for h in (0, 1):
+            wait_g(m, h, dp, diag)
+            g_onward(m, 2, h).start()
+
+    for zz in range(4):
+        R[:, zz * quarter:(zz + 1) * quarter] = small_rows[zz]
+
+    def gain(i):
+        return R[16 + i:17 + i, :].astype(f32)
+
+    def norm_grad(values, gain_vec, incoming):
+        factor = lax.rsqrt(jnp.mean(values * values, axis=1, keepdims=True) + EPSILON)
+        unit = values * factor
+        weighted = incoming * gain_vec
+        back_values = factor * (weighted - unit * jnp.mean(weighted * unit, axis=1, keepdims=True))
+        return back_values, jnp.sum(incoming * unit, axis=0, keepdims=True)
+
+    def put_small(at, count, values):
+        for zz in range(4):
+            small[zz, at:at + count] = values[:, zz * quarter:(zz + 1) * quarter]
+
+    for zz in range(4):
+        small[zz] = jnp.zeros(small.shape[1:], f32)
+    mixed_out[...] = (hidden[...] + sums[:, :width]).astype(bf)
+    extra = sums[:, width:width + EXTRA]
+    d_gates = extra + pltpu.roll(extra, EXTRA - 16, 1)
+    picks = router[...]
+    d_router = jnp.where(chosen_experts(route_ids[...]), d_gates, 0.0)
+    d_logits = (picks * (d_router - jnp.sum(picks * d_router, axis=1, keepdims=True))).astype(bf)
+    put_small(0, 16, jnp.dot(d_logits.T, ffn_in[...], preferred_element_type=f32)[:16])
+    d_ffn = sums[:, width + EXTRA:] + jnp.dot(d_logits, R[...], preferred_element_type=f32)
+    back_values, gain_grad = norm_grad(hidden[...], gain(1), d_ffn)
+    put_small(17, 1, gain_grad)
+    total = dy[...].astype(f32) + back_values
+    d_hidden[...] = total
+    d_mix[...] = total.astype(bf)
+    load_out.wait()
+
+    def heads_back(j, _):
+        at = pl.ds(pl.multiple_of(j * 512, 512), 512)
+        d_heads[:, at] = times_transposed(d_mix[...], Wo[at, :]).astype(bf)
+        return 0
+
+    lax.fori_loop(0, 4, heads_back, 0)
+    for n in range(7):
+        h_copy(n).start()
+    for n in range(7):
+        d_copy(n).start()
+    DH[slot_me] = d_heads[:, own_cols]
+    D[3, slot_me] = d_mix[:, own_cols]
+    m_plane.pass_on()
+    from_mates(DH, h_sem)
+
+    cos_t = jnp.concatenate([cosine[...]] * 2, axis=0)
+    sin_t = jnp.concatenate([sine[...]] * 2, axis=0)
+    scale = HDIM ** (-0.5)
+
+    def heads(d, grads):
+        allowed = allowed_keys(lives[d][0:1])
+        pieces = []
+        for hh in range(2):
+            cc = slice(hh * HDIM, (hh + 1) * HDIM)
+            q, k, v, dh = q_low[d, :, cc], k_low[d, :, cc], v_low[d, :, cc], DH[d, :, cc]
+            probs = softmax_rows(jnp.where(allowed, times_transposed(q, k) * scale, -1e30))
+            d_probs = times_transposed(dh, v)
+            D[2, d, :, cc] = jnp.dot(probs.astype(bf).T, dh, preferred_element_type=f32).astype(bf)
+            d_scores = (probs * (d_probs - jnp.sum(probs * d_probs, axis=1, keepdims=True))).astype(bf)
+            for z_in in (jnp.dot(d_scores, k, preferred_element_type=f32) * scale,
+                         jnp.dot(d_scores.T, q, preferred_element_type=f32) * scale):
+                pieces.append(z_in * cos_t - pltpu.roll(z_in, HDIM // 2, 1) * sin_t)
+        outs = []
+        for m, (raw, ref) in enumerate(((q_raw, g_q), (k_raw, g_k))):
+            incoming = jnp.concatenate([pieces[m], pieces[2 + m]], axis=1)
+            ref[d] = incoming
+            factor = lax.rsqrt(as_column(squares[m, pl.ds(d, 1), :], 256) + EPSILON)
+            unit = raw[d] * factor
+            gains = R[18 + m:19 + m, own_cols].astype(f32)
+            through = incoming * unit
+            parts[slot_me, m, pl.ds(d, 1), :] = as_row(jnp.sum(through * gains, axis=1, keepdims=True))
+            outs.append(grads[m] + jnp.sum(through, axis=0, keepdims=True))
+        return tuple(outs)
+
+    none = jnp.zeros((1, 256), f32)
+    gain_grads = lax.fori_loop(0, 8, heads, (none, none))
+    for n in range(7):
+        q_copy(n).start()
+    for m in range(2):
+        small[e, 18 + m:19 + m, pl.ds(pl.multiple_of(dp * 256, 256), 256)] = gain_grads[m]
+    m_plane.end()
+    from_mates(D.at[3], d_sem)
+    m_plane.end_cross()
+    load_mixed.wait()
+    compute(3, 1, 0)
+    pass_on(3, 0)
+    load_rows.wait()
+    compute(2, 0, 1)
+    from_mates(parts, q_sem)
+    means[...] = (((parts[0] + parts[1]) + (parts[2] + parts[3]))
+                  + ((parts[4] + parts[5]) + (parts[6] + parts[7]))) * (1.0 / width)
+
+    def raw_back(d, _):
+        for m, (raw, ref) in enumerate(((q_raw, g_q), (k_raw, g_k))):
+            factor = lax.rsqrt(as_column(squares[m, pl.ds(d, 1), :], 256) + EPSILON)
+            mean = as_column(means[m, pl.ds(d, 1), :], 256)
+            gains = R[18 + m:19 + m, own_cols].astype(f32)
+            D[m, d] = (factor * (ref[d] * gains - raw[d] * factor * mean)).astype(bf)
+        return 0
+
+    lax.fori_loop(0, 8, raw_back, 0)
+    pass_on(2, 1)
+
+    load_cols.wait()
+
+    def part_of(d):
+        values = times_transposed(D[0, d], Wc[0]) + times_transposed(D[1, d], Wc[1])
+        return values + times_transposed(D[2, d], Wc[2])
+
+    def f_copy(ee):
+        return remote(Wo.at[pl.ds(ee * rows, rows)], far_rows.at[ee], f_send.at[ee], f_sem.at[ee], far)
+
+    def r_copy(n):
+        return remote(home_rows.at[3 + n], home_rows.at[n], r_send.at[n], r_sem.at[n], (dp, plane[n], z))
+
+    for ee in range(4):
+        Wo[ee * rows:(ee + 1) * rows] = part_of((1 - dp) * 4 + ee).astype(bf)
+        f_copy(ee).start()
+    for n in range(3):
+        values = part_of(dp * 4 + plane[n])
+        arrived(far_rows.at[plane[n]], f_sem.at[plane[n]], me)
+        home_rows[3 + n] = (values + far_rows[plane[n]].astype(f32)).astype(bf)
+        r_copy(n).start()
+    compute(0, 0, 0)
+    pass_on(0, 0)
+    values = part_of(slot_me)
+    arrived(far_rows.at[e], f_sem.at[e], me)
+    grad_tokens[...] = values + far_rows[e].astype(f32)
+    finish(3)
+    compute(1, 0, 1)
+    pass_on(1, 1)
+    for n in range(3):
+        arrived(home_rows.at[n], r_sem.at[n], me)
+    back_values, gain_grad = norm_grad(
+        tok[...].astype(f32), gain(0),
+        (grad_tokens[...] + home_rows[0].astype(f32)) + (home_rows[1].astype(f32) + home_rows[2].astype(f32)))
+    put_small(16, 1, gain_grad)
+    grad_tokens[...] = d_hidden[...] + back_values
 
     def sz_copy(d):
-        return copy(small.at[zs[d]], s_z.at[z], sz_send.at[d - 1], sz_sem.at[z], (dp, e, zs[d]))
+        return remote(small.at[zs[d]], s_z.at[z], sz_send.at[d - 1], sz_sem.at[z], (dp, e, zs[d]))
+
+    def sa_copy(d):
+        return remote(s_all.at[slot_me], s_all.at[slot_me], sa_send.at[d - 1], sa_sem.at[slot_me], mates[d - 1])
 
     for d in (1, 2, 3):
         sz_copy(d).start()
-    for g in range(4):
-        for h in (0, 1):
-            def start_far(zz, _, g=g, h=h):
-                for m in range(4):
-                    far_copy(m, groups(h)[g], zz, h).start()
-                return 0
-            lax.fori_loop(0, 4, start_far, 0)
-
-    def a_copy(h, g, zz):
-        return copy(far.at[h, groups(h)[g], zz], a.at[h, g, zz], a_send.at[h, g, zz], a_sem.at[h, g, zz],
-                    (dp, firsts[h], z))
-
-    def b_copy(h, zz):
-        return copy(far.at[h, seconds[h], zz], b.at[h, zz], b_send.at[h, zz], b_sem.at[h, zz], (dp, seconds[h], z))
-
-    def c_copy(h, zz):
-        return copy(far.at[h, e, zz], c.at[h, z], c_send.at[h, zz], c_sem.at[h, z], (dp, e, zz))
-
-    def load_step(n, slot):
-        g, h, zz = n // 8, lax.rem(n // 4, 2), lax.rem(n, 4)
-        ee = pick(g, h)
-        for m in range(4):
-            load(m, ee, zz, h, slot).start()
-
-    def pick(g, h):
-        first = jnp.where(h == 0, py, px)
-        second = jnp.where(h == 0, px, py)
-        return jnp.where(g == 0, diag, jnp.where(g == 1, first, jnp.where(g == 2, second, e)))
-
-    load_step(0, 0)
-
-    def near(n, _):
-        slot = lax.rem(n, 2)
-
-        @pl.when(n + 1 < 32)
-        def _():
-            load_step(n + 1, 1 - slot)
-
-        g, h, zz = n // 8, lax.rem(n // 4, 2), lax.rem(n, 4)
-        ee = pick(g, h)
-        for m in range(4):
-            load(m, ee, zz, h, slot).wait()
-            arrived(far.at[h, ee, zz, m], far_sem.at[h, ee, zz, m], (dp, e, z))
-        far[h, ee, zz] = (far[h, ee, zz].astype(jnp.float32) + work[slot].astype(jnp.float32)).astype(far.dtype)
-
-        @pl.when(g < 2)
-        def _():
-            first = jnp.where(h == 0, py, px)
-            copy(far.at[h, ee, zz], a.at[h, g, zz], a_send.at[h, g, zz], a_sem.at[h, g, zz], (dp, first, z)).start()
-        return 0
-
-    lax.fori_loop(0, 32, near, 0)
-
-    for h in (0, 1):
-        def relay(d, _, h=h):
-            zz = lax.rem(z + d, 4)
-            arrived(a.at[h, 0, zz], a_sem.at[h, 0, zz], (dp, e, z))
-            far[h, seconds[h], zz] = (far[h, seconds[h], zz].astype(jnp.float32)
-                                      + a[h, 0, zz].astype(jnp.float32)).astype(far.dtype)
-            b_copy(h, zz).start()
-            return 0
-        lax.fori_loop(1, 5, relay, 0)
-    for h in (0, 1):
-        def finish(d, _, h=h):
-            zz = lax.rem(z + d, 4)
-            arrived(a.at[h, 1, zz], a_sem.at[h, 1, zz], (dp, e, z))
-            arrived(b.at[h, zz], b_sem.at[h, zz], (dp, e, z))
-            far[h, e, zz] = (far[h, e, zz].astype(jnp.float32) + a[h, 1, zz].astype(jnp.float32)
-                             + b[h, zz].astype(jnp.float32)).astype(far.dtype)
-
-            @pl.when(d < 4)
-            def _():
-                c_copy(h, zz).start()
-            return 0
-        lax.fori_loop(1, 5, finish, 0)
-
-    def sa_copy(d):
-        return copy(mine_small, s_all.at[dp * 4 + e], sa_send.at[d - 1], sa_sem.at[dp * 4 + e], mates[d - 1])
-
-    slot_me = dp * 4 + e
+    finish(2)
+    relay_out(3)
     for d in (1, 2, 3):
-        arrived(s_z.at[zs[d]], sz_sem.at[zs[d]], (dp, e, z))
+        arrived(s_z.at[zs[d]], sz_sem.at[zs[d]], me)
     s_all[slot_me] = (small[z] + s_z[zs[1]]) + (s_z[zs[2]] + s_z[zs[3]])
-    mine_small = s_all.at[slot_me]
     for d in range(1, 8):
         sa_copy(d).start()
-
-    def mine_at(d, ee):
-        return pl.ds(pl.multiple_of(ee * 128 + d * 64, 64), 64)
-
-    def g_copy(h, n):
-        return copy(mine.at[:, pl.ds(h * 32, 32)],
-                    out.at[:, pl.ds(pl.multiple_of(e * 128 + dp * 64 + h * 32, 32), 32)],
-                    g_send.at[h, n], g_sem.at[h, slot_me], mates[n])
-
-    locals_out = []
-    for h in (0, 1):
-        def last(m, _, h=h):
-            mine[m, pl.ds(h * 32, 32)] = (
-                (far[h, e, z, m].astype(jnp.float32) + c[h, zs[1], m].astype(jnp.float32))
-                + (c[h, zs[2], m].astype(jnp.float32) + c[h, zs[3], m].astype(jnp.float32))
-            ).astype(mine.dtype)
-            return 0
-        for d in (1, 2, 3):
-            arrived(c.at[h, zs[d]], c_sem.at[h, zs[d]], (dp, e, z))
-        lax.fori_loop(0, 4, last, 0)
-        for n in range(7):
-            g_copy(h, n).start()
-        keep = pltpu.make_async_copy(
-            mine.at[:, pl.ds(h * 32, 32)],
-            out.at[:, pl.ds(pl.multiple_of(e * 128 + dp * 64 + h * 32, 32), 32)],
-            out_sem.at[h])
-        keep.start()
-        locals_out.append(keep)
-    total = s_all[slot_me]
-    for d in range(1, 8):
-        other = lax.rem(dp + d // 4, 2) * 4 + lax.rem(e + d % 4, 4)
-        arrived(s_all.at[other], sa_sem.at[other], (dp, e, z))
+    finish(0)
+    relay_out(2)
+    end_out(3)
+    finish(1)
+    relay_out(0)
+    end_out(2)
+    from_mates(s_all, sa_sem)
     small_out[...] = (((s_all[0] + s_all[1]) + (s_all[2] + s_all[3]))
                       + ((s_all[4] + s_all[5]) + (s_all[6] + s_all[7])))
-    for h in (0, 1):
-        for d in range(1, 8):
-            od, oe = lax.rem(dp + d // 4, 2), lax.rem(e + d % 4, 4)
-            arrived(out.at[:, pl.ds(pl.multiple_of(oe * 128 + od * 64 + h * 32, 32), 32)],
-                    g_sem.at[h, od * 4 + oe], (dp, e, z))
-    for d in (1, 2, 3):
-        sz_copy(d).wait_send()
-    for d in range(1, 8):
-        sa_copy(d).wait_send()
-    for h in (0, 1):
-        for n in range(7):
-            g_copy(h, n).wait_send()
-        locals_out[h].wait()
-        for g in range(4):
-            def drain_far(zz, _, g=g, h=h):
-                for m in range(4):
-                    far_copy(m, groups(h)[g], zz, h).wait_send()
-                return 0
-            lax.fori_loop(0, 4, drain_far, 0)
-
-        def drain(d, _, h=h):
-            zz = lax.rem(z + d, 4)
-            a_copy(h, 0, zz).wait_send()
-            a_copy(h, 1, zz).wait_send()
-            b_copy(h, zz).wait_send()
-
-            @pl.when(d < 4)
-            def _():
-                c_copy(h, zz).wait_send()
-            return 0
-        lax.fori_loop(1, 5, drain, 0)
-
-
-def total(gq, gk, gv, go, small):
+    relay_out(1)
+    end_out(0)
+    end_out(1)
+    for m in range(4):
+        for h in (0, 1):
+            for ee in range(4):
+                wait_g(m, h, 1 - dp, ee)
+            for n in range(3):
+                g_copy(m, n, h).wait_send()
+                g_onward(m, n, h).wait_send()
+            g_relay(m, h).wait_send()
+        keep(m).wait()
+        for j in range(3):
+            hop_copy(m, j).wait_send()
+    m_plane.drain()
+    for n in range(7):
+        d_copy(n).wait_send()
+        h_copy(n).wait_send()
+        q_copy(n).wait_send()
+        sa_copy(n + 1).wait_send()
+    for ee in range(4):
+        f_copy(ee).wait_send()
+    for n in range(3):
+        r_copy(n).wait_send()
+        sz_copy(n + 1).wait_send()
+
+
+def back(*args):
     dma = pltpu.SemaphoreType.DMA
     bf, f32 = jnp.bfloat16, jnp.float32
+    shape = jax.ShapeDtypeStruct
     vmem = pl.BlockSpec(memory_space=pltpu.VMEM)
+    rows, width = args[1].shape
+    small_shape = (4, 24, width // 4)
     return pl.pallas_call(
-        total_kernel,
+        back_kernel,
         out_shape=(
-            jax.ShapeDtypeStruct((4, 512, 2048), bf),
-            jax.ShapeDtypeStruct(small.shape[1:], f32),
+            shape((rows, width), bf),
+            shape((rows, width), f32),
+            shape((4, width // 4, width), bf),
+            shape(small_shape[1:], f32),
         ),
-        in_specs=[ANY] * 4 + [vmem],
-        out_specs=(ANY, vmem),
+        in_specs=[vmem] * 18 + [ANY] * 3,
+        out_specs=(vmem, vmem, ANY, vmem),
         scratch_shapes=[
-            pltpu.VMEM((2, 4, 4, 4, 32, 2048), bf),
-            pltpu.VMEM((2, 2, 4, 4, 32, 2048), bf),
-            pltpu.VMEM((2, 4, 4, 32, 2048), bf),
-            pltpu.VMEM((2, 4, 4, 32, 2048), bf),
-            pltpu.VMEM((4, 64, 2048), bf),
-            pltpu.VMEM((2, 4, 32, 2048), bf),
-            pltpu.VMEM(small.shape, f32),
-            pltpu.VMEM((8,) + small.shape[1:], f32),
-            dma((2, 4)),
-            dma((2, 4, 4, 4)),
-            dma((2, 2, 4)),
-            dma((2, 4)),
-            dma((2, 4)),
+            pltpu.VMEM((width, width), bf),
+            pltpu.VMEM((3, width, 256), bf),
+            pltpu.VMEM((EXTRA, width), bf),
+            pltpu.VMEM((rows, width), f32),
+            pltpu.VMEM((rows, width), bf),
+            pltpu.VMEM((8, rows, 256), bf),
+            pltpu.VMEM((rows, width), bf),
+            pltpu.VMEM((8, rows, 256), f32),
+            pltpu.VMEM((8, rows, 256), f32),
+            pltpu.VMEM((8, 2, 8, rows), f32),
+            pltpu.VMEM((2, 8, rows), f32),
+            pltpu.VMEM((2, 8, rows, width), bf),
+            pltpu.VMEM((4, 8, rows, 256), bf),
+            pltpu.VMEM((256, 8 * rows), bf),
+            pltpu.VMEM((2, 4, 256, 512), f32),
+            pltpu.VMEM((4, 256, 512), f32),
+            pltpu.VMEM((4, 5, 256, 512), bf),
+            pltpu.VMEM((4, 3, 256, 512), bf),
+            pltpu.VMEM((4, 512, 256), bf),
+            pltpu.VMEM((4, rows, width), bf),
+            pltpu.VMEM((6, rows, width), bf),
+            pltpu.VMEM(small_shape, f32),
+            pltpu.VMEM(small_shape, f32),
+            pltpu.VMEM((8,) + small_shape[1:], f32),
+            dma((2,)),
+            dma((2,)),
+            dma((2, 8)),
+            dma((3, 2)),
+            dma((2,)),
+            dma((3, 2)),
+            dma((8,)),
+            dma((7,)),
+            dma((8,)),
+            dma((7,)),
+            dma((8,)),
+            dma((7,)),
+            dma((4, 5)),
+            dma((4, 3)),
             dma((4,)),
+            dma((4,)),
+            dma((3,)),
+            dma((3,)),
+            dma((4,)),
+            dma((3,)),
             dma((8,)),
-            dma((2, 8)),
-            dma((2, 4, 4, 4)),
-            dma((2, 2, 4)),
-            dma((2, 4)),
-            dma((2, 4)),
-            dma((3,)),
             dma((7,)),
-            dma((2, 7)),
-            dma((2,)),
+            dma((4, 2, 8)),
+            dma((4, 3, 2)),
+            dma((4, 2)),
+            dma((4, 3, 2)),
+            dma((4,)),
         ],
-        compiler_params=pltpu.CompilerParams(collective_id=3, has_side_effects=True, vmem_limit_bytes=52 * 2**20),
-        name="total_grads",
-    )(gq, gk, gv, go, small)
+        compiler_params=pltpu.CompilerParams(collective_id=3, has_side_effects=True, vmem_limit_bytes=63 * 2**20),
+        name="attention_back",
+    )(*args)
 
 
 def gathered(
@@ -1035,104 +1556,31 @@
     expert_count = w_router.shape[1]
     f32, bf = jnp.float32, jnp.bfloat16
     places = jnp.arange(seq_len)
-    score_scale = HDIM ** (-0.5)
     length = lengths[:, 0]
     live = places[None, :] < length[:, None]
-    dy = jnp.where(live[:, :, None], cotangent[:, 0], jnp.zeros((), bf))
-    small = jnp.concatenate(
-        [w_router.T, g_attn[None], g_ffn[None], g_query[None], g_key[None],
-         jnp.zeros((32 - expert_count - 4, w_router.shape[0]), bf)], axis=0)
-    full, small_all, gate_far, up_far, down_far, dy_all = collect(
-        w_query, w_key, w_value, w_out, small, w_gate[0], w_up[0], w_down[0], dy)
-    query_full, key_full, value_full, out_full = full[0], full[1], full[2], full[3]
-    small_rows = jnp.swapaxes(small_all, 0, 1).reshape(32, model_width)
-    route_full = small_rows[:expert_count].T
-    gain_attn, gain_ffn, gain_query, gain_key = (
-        small_rows[expert_count + i].astype(f32) for i in range(4))
-
     rows = micro_count * seq_len
-    cosine_one, sine_one = rope_tables(seq_len, HDIM)
-    cosine_table, sine_table = jnp.tile(cosine_one, (micro_count, 1)), jnp.tile(sine_one, (micro_count, 1))
-    inputs = tokens[:, 0].reshape(rows, model_width).astype(f32)
+    gains = jnp.pad(jnp.stack([g_attn, g_ffn, g_query, g_key]), ((0, EXTRA - expert_count - 4), (0, 0)))
+    half = HDIM // 2
+    angles = np.arange(seq_len)[:, None] * 10000.0 ** (-2.0 * np.arange(half) / HDIM)[None, :]
+    cosine_table = np.concatenate([np.cos(angles)] * 2, axis=1).astype(np.float32)
+    turned_sine = np.concatenate([-np.sin(angles), np.sin(angles)], axis=1).astype(np.float32)
+    live_rows = jnp.broadcast_to(live.astype(f32).reshape(1, rows), (8, rows))
     route_ids = routes[:, 0].reshape(rows, -1)
-    normed = rms_norm(inputs, gain_attn).astype(bf)
-    query_raw = matmul(normed, query_full)
-    key_raw = matmul(normed, key_full)
-    value_raw = matmul(normed, value_full)
-
-    def per_head(values):
-        return values.reshape(micro_count, seq_len, HEADS, HDIM)
-
-    value_low = per_head(value_raw.astype(bf))
-    query_low = per_head(rotate(
-        rms_norm(query_raw, gain_query).reshape(rows, HEADS, HDIM), cosine_table, sine_table).astype(bf))
-    key_low = per_head(rotate(
-        rms_norm(key_raw, gain_key).reshape(rows, HEADS, HDIM), cosine_table, sine_table).astype(bf))
-    allowed = (places[None, None, :] <= places[None, :, None]) & live[:, None, :]
-    scores = jnp.einsum("mqhd,mkhd->mhqk", query_low, key_low, preferred_element_type=f32) * score_scale
-    attn_probs = softmax_rows(jnp.where(allowed[:, None], scores, -1e30))
-    probs_low = attn_probs.astype(bf)
-    mixed_low = jnp.einsum("mhqk,mkhd->mqhd", probs_low, value_low, preferred_element_type=f32)
-    mixed_low = mixed_low.reshape(rows, model_width).astype(bf)
-    hidden_state = inputs + matmul(mixed_low, out_full)
-    ffn_in = rms_norm(hidden_state, gain_ffn).astype(bf)
-    router = softmax_rows(matmul(ffn_in, route_full))
-    expert_ids = jnp.arange(expert_count)
-    chosen = jnp.any(route_ids[:, :, None] == expert_ids[None, None, :], axis=1)
-    gates = jnp.where(chosen, router, 0.0)
-    gates_high = gates.astype(bf)
-    gates_low = (gates - gates_high.astype(f32)).astype(bf)
-    sent = jnp.concatenate(
-        [ffn_in, gates_high, gates_low, jnp.zeros((rows, EXTRA - 2 * expert_count), bf)], axis=1)
-    spread_rows = spread(sent.reshape(micro_count, seq_len, -1))
-
+    tokens_here = tokens[:, 0].reshape(rows, model_width)
+    (query_raw, key_raw, query_low, key_low, value_low, squares, lives, mixed_low, hidden_state, ffn_in, router,
+     small_rows, dy, rows_all, w_cols, out_full, spread_rows, dy_all, gate_far, up_far, down_far) = front(
+        tokens_here, cotangent[:, 0].reshape(rows, model_width), live_rows, route_ids, cosine_table, turned_sine,
+        w_router, gains,
+        w_query, w_key, w_value, w_out, w_gate[0], w_up[0], w_down[0])
     expert_sums, *expert_grads = experts(
         spread_rows, dy_all, (w_gate[0], w_up[0], w_down[0]), (gate_far, up_far, down_far))
-    y_all = expert_sums.reshape(rows, -1)
-    d_ffn_in = y_all[:, model_width + EXTRA:]
-    mixed_out = (hidden_state + y_all[:, :model_width]).astype(bf)
-    d_gates = y_all[:, model_width:model_width + expert_count] + y_all[
-        :, model_width + expert_count:model_width + 2 * expert_count]
-    d_router = jnp.where(chosen, d_gates, 0.0)
-    d_output = dy.reshape(rows, model_width).astype(f32)
-    d_logits = (router * (d_router - jnp.sum(router * d_router, axis=1, keepdims=True))).astype(bf)
-    grad_router = transposed_times(d_logits, ffn_in)
-    d_ffn_in = d_ffn_in + times_transposed(d_logits, route_full)
-    d_hidden_norm, d_gain_ffn = norm_back(hidden_state, gain_ffn, d_ffn_in)
-    d_hidden = d_output + d_hidden_norm
-    d_attn_low = d_hidden.astype(bf)
-    grad_out = transposed_times(mixed_low, d_attn_low).astype(bf)
-    d_mixed = per_head(times_transposed(d_attn_low, out_full).astype(bf))
-    d_probs = jnp.einsum("mqhd,mkhd->mhqk", d_mixed, value_low, preferred_element_type=f32)
-    d_value = jnp.einsum("mhqk,mqhd->mkhd", probs_low, d_mixed, preferred_element_type=f32)
-    d_value = d_value.reshape(rows, model_width).astype(bf)
-    d_scores = (attn_probs * (d_probs - jnp.sum(attn_probs * d_probs, axis=-1, keepdims=True))).astype(bf)
-    d_query = jnp.einsum("mhqk,mkhd->mqhd", d_scores, key_low, preferred_element_type=f32) * score_scale
-    d_key = jnp.einsum("mhqk,mqhd->mkhd", d_scores, query_low, preferred_element_type=f32) * score_scale
-
-    def raw_back(raw, gain_vec, d_heads):
-        turned = rotate_back(d_heads.reshape(rows, HEADS, HDIM), cosine_table, sine_table)
-        return norm_back(raw, gain_vec, turned.reshape(rows, model_width))
-
-    d_query_raw, d_gain_query = raw_back(query_raw, gain_query, d_query)
-    d_key_raw, d_gain_key = raw_back(key_raw, gain_key, d_key)
-    d_query_low, d_key_low = d_query_raw.astype(bf), d_key_raw.astype(bf)
-    grad_query = transposed_times(normed, d_query_low).astype(bf)
-    grad_key = transposed_times(normed, d_key_low).astype(bf)
-    grad_value = transposed_times(normed, d_value).astype(bf)
-    d_normed = (times_transposed(d_query_low, query_full) + times_transposed(d_key_low, key_full)
-                + times_transposed(d_value, value_full))
-    d_input_norm, d_gain_attn = norm_back(inputs, gain_attn, d_normed)
-    grad_tokens = (d_hidden + d_input_norm).reshape(micro_count, 1, seq_len, model_width)
-
-    small_grads = jnp.concatenate(
-        [grad_router, d_gain_attn[None], d_gain_ffn[None], d_gain_query[None], d_gain_key[None],
-         jnp.zeros((24 - expert_count - 4, model_width), f32)], axis=0)
-    small_grads = jnp.swapaxes(small_grads.reshape(24, 4, model_width // 4), 0, 1)
-    sums, small_sums = total(grad_query, grad_key, grad_value, grad_out, small_grads)
+    mixed_out, grad_tokens, sums, small_sums = back(
+        expert_sums.reshape(rows, -1), tokens_here, route_ids, cosine_table, turned_sine,
+        dy.reshape(rows, model_width), mixed_low, query_raw, key_raw, query_low, key_low, value_low, squares, lives,
+        hidden_state, ffn_in, router, small_rows, rows_all, w_cols, out_full)
     return (
         mixed_out.reshape(micro_count, 1, seq_len, model_width),
-        grad_tokens,
+        grad_tokens.reshape(micro_count, 1, seq_len, model_width),
         sums[0].astype(f32),
         sums[1].astype(f32),
         sums[2].astype(f32),

time: 948 us -> 597 us (0.63); the launches traced: 937 us -> 596 us
  Pallas kernels: 766 us -> 563 us
  matrix products: 86.2 us -> 0 us
  local copies, waits for them, and re-layouts: 51.3 us -> 20.3 us
  other arithmetic: 31.5 us -> 11.6 us
    pallas_call x3 -> x2, Pallas kernels: 538 us -> 358 us  [the longest x1 208 us: front(): pl.pallas_call(front_kernel, out_shape=(shape((8, rows, 256), f32), shape...]
    dot_general x21 -> x0, matrix products: 86.2 us -> none  [the longest x5 29.9 us: times_transposed(): lax.dot_general(left, right, (((1,), (1,)), ((), ())), preferred_element_...]
    pallas_call x1, Pallas kernels: 228 us -> 205 us  [experts(): pl.pallas_call(experts_kernel, out_shape=(shape((2, rows, total_width), f...]
    concatenate x8 -> x0, local copies, waits for them, and re-layouts: 11.6 us -> none  [the longest x4 9.63 us: rotate(): jnp.concatenate([-head_rows[..., half_dim:], head_rows[..., :half_dim]],...]
    unnamed x89 -> x17, local copies, waits for them, and re-layouts: 25.3 us -> 14.1 us
where the time goes in v3:
time: 597 us; the launch traced here: 596 us
  Pallas kernels  563 us (94%)
  local copies, waits for them, and re-layouts  20.3 us (3%)
  other arithmetic  11.6 us (2%)
    pallas_call x1, Pallas kernels, front(): pl.pallas_call(front_kernel, out_shape=(shape((8, rows, 256), f32), shape...  208 us
    pallas_call x1, Pallas kernels, experts(): pl.pallas_call(experts_kernel, out_shape=(shape((2, rows, total_width), f...  205 us
    pallas_call x1, Pallas kernels, back(): pl.pallas_call(back_kernel, out_shape=(shape((rows, width), bf), shape((r...  150 us
    unnamed x17, local copies, waits for them, and re-layouts  14.1 us

profile of v3, /device:TPU:13, one launch (start us, length us, event | category | flops | bytes accessed | tf_op | source)
XLA Modules:
  0.0 595.5 jit_solution(18223599790225273751)
XLA Ops:
  0.6 0.7 compare_convert_fusion
  1.4 0.1 reshape.70
  1.5 0.7 stack.15
  2.1 0.7 stack.16
  2.8 0.7 stack.17
  3.5 0.7 stack.18
  4.2 0.6 broadcast_in_dim.15.live
  4.8 1.4 copy.32
  6.2 0.7 fusion.6.gains_in
  6.9 1.5 copy.33.route_in
  8.3 208.0 %attention_front.1 = (f32[8,128,256]{2,1,0:T(8,128)}, f32[8,128,256]{2,1,0:T(8,128)}, bf16[8,128,256]{2,1,0:T(8,128)(2,1)}, bf16[8,128,256]{2,1,0:T(8,128)(2,1)}...) custom-call(bf16[128,2048]{1,0:T(8,128)(2,1)} %bitcast.46, ...), custom_call_target="tpu_custom_call" | custom-call | tf_op jit(solution)/shard_map/attention_front/pallas_call | solution.py:623
  216.4 204.5 %owned_expert.1 = (f32[2,64,4224]{2,1,0:T(8,128)}, f32[2048,512]{1,0:T(8,128)}, f32[2048,512]{1,0:T(8,128)}, f32[512,2048]{1,0:T(8,128)}, bf16[16,2,64,4224]{3,2...) custom-call(bf16[16,2,64,2176]{3,2,1,0:T(8,128)(2,1)} %get-tuple-element.43.wide, ...), custom_call_target="tpu_custom_call" | custom-call | tf_op jit(solution)/shard_map/owned_expert/pallas_call | solution.py:1071
  420.9 150.4 %attention_back.1 = (bf16[128,2048]{1,0:T(8,128)(2,1)}, f32[128,2048]{1,0:T(8,128)}, bf16[4,512,2048]{2,1,0:T(8,128)(2,1)}, f32[24,512]{1,0:T(8,128)}) custom-call(f32[128,4224]{1,0:T(8,128)} %bitcast.45, bf16[128,2048]{1,0:T(8,128)(2,1)} %bitcast.47, s32[128,8]{1,0:T(8,128)} %bitcast.50, f32[64,128]{1,0:T(8,128)} %constant.7.clone.cosine, ...), custom_call_target="tpu_custom_call" | custom-call | tf_op jit(solution)/shard_map/attention_back/pallas_call | solution.py:1469
  571.3 1.5 fusion.7
  572.7 1.4 slice_bitcast_fusion
  574.1 0.0 copy-start.4
  574.1 0.0 copy-start.3
  574.1 0.0 copy-start.2
  574.1 10.2 %bitcast_convert_fusion = (f32[512,2048]{1,0:T(8,128)}, f32[512,2048]{1,0:T(8,128)}, f32[512,2048]{1,0:T(8,128)}, f32[512,2048]{1,0:T(8,128)}) fusion(bf16[4,512,2048]{2,1,0:T(8,128)(2,1)} %get-tuple-element.67), kind=kLoop, calls=%fused_computation | loop fusion | flops 4194304 | bytes 25165824 | tf_op jit(solution)/shard_map/convert_element_type | solution.py:1587
  584.3 0.0 copy-done.4
  584.3 0.8 copy.41
  585.1 0.0 copy-done.3
  585.1 1.0 copy.42
  586.1 0.0 copy-done.2
  586.1 0.0 copy-start.1
  586.1 2.1 copy.43
  588.3 1.6 copy-done.1
  589.8 0.0 copy-start
  589.8 2.1 copy.44
  592.0 1.6 copy-done
  593.5 2.0 copy.45
Async XLA Ops:
  574.1 10.2 %copy-start.4 = (bf16[128,2048]{1,0:T(8,128)(2,1)S(1)}, bf16[128,2048]{1,0:T(8,128)(2,1)}, u32[]{:S(2)}) copy-start(bf16[128,2048]{1,0:T(8,128)(2,1)} %get-tuple-element.65) | copy-start | bytes 1572868
  574.1 11.0 %copy-start.3 = (f32[128,2048]{1,0:T(8,128)S(1)}, f32[128,2048]{1,0:T(8,128)}, u32[]{:S(2)}) copy-start(f32[128,2048]{1,0:T(8,128)} %get-tuple-element.66) | copy-start | bytes 3145732
  574.1 12.0 %copy-start.2 = (f32[2048,512]{1,0:T(8,128)S(1)}, f32[2048,512]{1,0:T(8,128)}, u32[]{:S(2)}) copy-start(f32[2048,512]{1,0:T(8,128)} %get-tuple-element.69) | copy-start | bytes 12582916
  586.1 3.7 copy-start.1
  589.8 3.7 copy-start

commit v4 on v3

--- a/solution.py
+++ b/solution.py
@@ -825,7 +825,7 @@
                 for load in weights[3:]:
                     load.wait()
 
-            @pl.when((s > 0) & (n == 1))
+            @pl.when((s > 1) & (n == 1))
             def _():
                 send_step(s - 1)
 
@@ -879,6 +879,10 @@
                 stage[buf, i, h] = (stage[buf, i, h].astype(f32) + addend[i].astype(f32)).astype(bf)
         for i in range(2):
             part_write(s, i).start()
+
+        @pl.when(s == 0)
+        def _():
+            send_step(s)
         return 0
 
     lax.fori_loop(0, 8, step, 0)
@@ -1534,6 +1538,34 @@
     )(*args)
 
 
+def lay_out_kernel(sums, eg, eu, ed, mixed, grad_in, o_q, o_k, o_v, o_o, o_eg, o_eu, o_ed, o_mixed, o_grad):
+    for m, ref in enumerate((o_q, o_k, o_v, o_o)):
+        ref[...] = sums[m].astype(jnp.float32)
+    for src, dst in ((eg, o_eg), (eu, o_eu), (ed, o_ed), (mixed, o_mixed), (grad_in, o_grad)):
+        dst[...] = src[...]
+
+
+def lay_out(sums, *arrays):
+    steps = 8
+    f32 = jnp.float32
+    wide = (sums.shape[1] // steps, sums.shape[2])
+
+    def rows_spec(array):
+        return pl.BlockSpec((array.shape[0] // steps, array.shape[1]), lambda i: (i, 0))
+
+    rows = [rows_spec(a) for a in arrays]
+    return pl.pallas_call(
+        lay_out_kernel,
+        grid=(steps,),
+        out_shape=tuple([jax.ShapeDtypeStruct(sums.shape[1:], f32)] * 4
+                        + [jax.ShapeDtypeStruct(a.shape, a.dtype) for a in arrays]),
+        in_specs=[pl.BlockSpec((4,) + wide, lambda i: (0, i, 0))] + rows,
+        out_specs=tuple([pl.BlockSpec(wide, lambda i: (i, 0))] * 4 + rows),
+        compiler_params=pltpu.CompilerParams(vmem_limit_bytes=60 * 2**20),
+        name="lay_out",
+    )(sums, *arrays)
+
+
 def gathered(
     tokens,
     cotangent,
@@ -1578,19 +1610,23 @@
         expert_sums.reshape(rows, -1), tokens_here, route_ids, cosine_table, turned_sine,
         dy.reshape(rows, model_width), mixed_low, query_raw, key_raw, query_low, key_low, value_low, squares, lives,
         hidden_state, ffn_in, router, small_rows, rows_all, w_cols, out_full)
+    *sums, grad_gate, grad_up, grad_down, mixed_out, grad_tokens = lay_out(
+        sums, *expert_grads, mixed_out, grad_tokens)
     return (
         mixed_out.reshape(micro_count, 1, seq_len, model_width),
         grad_tokens.reshape(micro_count, 1, seq_len, model_width),
-        sums[0].astype(f32),
-        sums[1].astype(f32),
-        sums[2].astype(f32),
-        sums[3].astype(f32),
+        sums[0],
+        sums[1],
+        sums[2],
+        sums[3],
         small_sums[:expert_count].T,
         small_sums[expert_count],
         small_sums[expert_count + 1],
         small_sums[expert_count + 2],
         small_sums[expert_count + 3],
-        *(g[None] for g in expert_grads),
+        grad_gate[None],
+        grad_up[None],
+        grad_down[None],
     )
 
 

time: 597 us -> 591 us (0.990)
  Pallas kernels: 563 us -> 578 us
  local copies, waits for them, and re-layouts: 20.3 us -> 9.14 us
  other arithmetic: 11.6 us -> 1.39 us
    pallas_call x0 -> x1, Pallas kernels: none -> 18.8 us  [lay_out(): pl.pallas_call(lay_out_kernel, grid=(steps,), out_shape=tuple([jax.ShapeD...]
    unnamed x17 -> x2, local copies, waits for them, and re-layouts: 14.1 us -> 2.9 us
    convert_element_type x1 -> x0, other arithmetic: 10.2 us -> none  [gathered(): sums[3].astype(f32)]
where the time goes in v4:
time: 591 us; the launch traced here: 590 us
  Pallas kernels  578 us (98%)
  local copies, waits for them, and re-layouts  9.14 us (2%)
    pallas_call x1, Pallas kernels, front(): pl.pallas_call(front_kernel, out_shape=(shape((8, rows, 256), f32), shape...  208 us
    pallas_call x1, Pallas kernels, experts(): pl.pallas_call(experts_kernel, out_shape=(shape((2, rows, total_width), f...  201 us
    pallas_call x1, Pallas kernels, back(): pl.pallas_call(back_kernel, out_shape=(shape((rows, width), bf), shape((r...  150 us
    pallas_call x1, Pallas kernels, lay_out(): pl.pallas_call(lay_out_kernel, grid=(steps,), out_shape=tuple([jax.ShapeD...  18.8 us

profile of v4, /device:TPU:13, one launch (start us, length us, event | category | flops | bytes accessed | tf_op | source)
XLA Modules:
  0.0 589.6 jit_solution(11065599974157702587)
XLA Ops:
  0.6 0.7 compare_convert_fusion
  1.4 0.1 reshape.62
  1.5 0.7 stack.15
  2.1 0.7 stack.16
  2.8 0.7 stack.17
  3.5 0.7 stack.18
  4.2 0.6 broadcast_in_dim.15.live
  4.8 1.4 copy.32
  6.2 0.7 fusion.6.gains_in
  6.9 1.5 copy.33.route_in
  8.3 208.0 %attention_front.1 = (f32[8,128,256]{2,1,0:T(8,128)}, f32[8,128,256]{2,1,0:T(8,128)}, bf16[8,128,256]{2,1,0:T(8,128)(2,1)}, bf16[8,128,256]{2,1,0:T(8,128)(2,1)}...) custom-call(bf16[128,2048]{1,0:T(8,128)(2,1)} %bitcast.31, ...), custom_call_target="tpu_custom_call" | custom-call | tf_op jit(solution)/shard_map/attention_front/pallas_call | solution.py:623
  216.4 201.3 %owned_expert.1 = (f32[2,64,4224]{2,1,0:T(8,128)}, f32[2048,512]{1,0:T(8,128)}, f32[2048,512]{1,0:T(8,128)}, f32[512,2048]{1,0:T(8,128)}, bf16[16,2,64,4224]{3,2...) custom-call(bf16[16,2,64,2176]{3,2,1,0:T(8,128)(2,1)} %get-tuple-element.52.wide, ...), custom_call_target="tpu_custom_call" | custom-call | tf_op jit(solution)/shard_map/owned_expert/pallas_call | solution.py:1075
  417.6 150.1 %attention_back.1 = (bf16[128,2048]{1,0:T(8,128)(2,1)}, f32[128,2048]{1,0:T(8,128)}, bf16[4,512,2048]{2,1,0:T(8,128)(2,1)}, f32[24,512]{1,0:T(8,128)}) custom-call(f32[128,4224]{1,0:T(8,128)} %bitcast.30, bf16[128,2048]{1,0:T(8,128)(2,1)} %bitcast.32, s32[128,8]{1,0:T(8,128)} %bitcast.34, f32[64,128]{1,0:T(8,128)} %constant.7.clone.cosine, ...), custom_call_target="tpu_custom_call" | custom-call | tf_op jit(solution)/shard_map/attention_back/pallas_call | solution.py:1473
  567.8 1.5 fusion.7
  569.2 1.4 slice_bitcast_fusion
  570.6 18.8 %lay_out.1 = (f32[512,2048]{1,0:T(8,128)}, f32[512,2048]{1,0:T(8,128)}, f32[512,2048]{1,0:T(8,128)}, f32[512,2048]{1,0:T(8,128)}, f32[2048,512]{1,0:T(8,128)}, /...) custom-call(bf16[4,512,2048]{2,1,0:T(8,128)(2,1)} %get-tuple-element.74.sums, ...), custom_call_target="tpu_custom_call" | custom-call | tf_op jit(solution)/shard_map/lay_out/pallas_call | solution.py:1557

commit v5 on v4

--- a/solution.py
+++ b/solution.py
@@ -1014,8 +1014,11 @@
         @pl.when(n > 0)
         def _():
             settle(n - 1)
-        for at, act in ((2, lambda: begin(0)), (3, lambda: close(0)), (4, lambda: fire(0)),
-                        (5, lambda: begin(1)), (6, lambda: close(1)), (7, lambda: fire(1))):
+        def now(k):
+            close(k)
+            fire(k)
+
+        for at, act in ((1, lambda: begin(0)), (2, lambda: now(0)), (4, lambda: begin(1)), (5, lambda: now(1))):
             pl.when(n == at)(act)
         return 0
 

time: 591 us -> 585 us (0.990)
  Pallas kernels: 578 us -> 572 us
    pallas_call x1, Pallas kernels: 201 us -> 195 us  [experts(): pl.pallas_call(experts_kernel, out_shape=(shape((2, rows, total_width), f...]
where the time goes in v5:
time: 585 us; the launch traced here: 583 us
  Pallas kernels  572 us (98%)
  local copies, waits for them, and re-layouts  9.14 us (2%)
    pallas_call x1, Pallas kernels, front(): pl.pallas_call(front_kernel, out_shape=(shape((8, rows, 256), f32), shape...  208 us
    pallas_call x1, Pallas kernels, experts(): pl.pallas_call(experts_kernel, out_shape=(shape((2, rows, total_width), f...  195 us
    pallas_call x1, Pallas kernels, back(): pl.pallas_call(back_kernel, out_shape=(shape((rows, width), bf), shape((r...  150 us
    pallas_call x1, Pallas kernels, lay_out(): pl.pallas_call(lay_out_kernel, grid=(steps,), out_shape=tuple([jax.ShapeD...  18.8 us

profile of v5, /device:TPU:13, one launch (start us, length us, event | category | flops | bytes accessed | tf_op | source)
XLA Modules:
  0.0 583.0 jit_solution(12795895266782651524)
XLA Ops:
  0.6 0.7 compare_convert_fusion
  1.4 0.1 reshape.62
  1.5 0.7 stack.15
  2.1 0.7 stack.16
  2.8 0.7 stack.17
  3.5 0.7 stack.18
  4.2 0.6 broadcast_in_dim.15.live
  4.8 1.4 copy.32
  6.2 0.7 fusion.6.gains_in
  6.9 1.5 copy.33.route_in
  8.3 208.0 %attention_front.1 = (f32[8,128,256]{2,1,0:T(8,128)}, f32[8,128,256]{2,1,0:T(8,128)}, bf16[8,128,256]{2,1,0:T(8,128)(2,1)}, bf16[8,128,256]{2,1,0:T(8,128)(2,1)}...) custom-call(bf16[128,2048]{1,0:T(8,128)(2,1)} %bitcast.31, ...), custom_call_target="tpu_custom_call" | custom-call | tf_op jit(solution)/shard_map/attention_front/pallas_call | solution.py:623
  216.4 194.9 %owned_expert.1 = (f32[2,64,4224]{2,1,0:T(8,128)}, f32[2048,512]{1,0:T(8,128)}, f32[2048,512]{1,0:T(8,128)}, f32[512,2048]{1,0:T(8,128)}, bf16[16,2,64,4224]{3,2...) custom-call(bf16[16,2,64,2176]{3,2,1,0:T(8,128)(2,1)} %get-tuple-element.52.wide, ...), custom_call_target="tpu_custom_call" | custom-call | tf_op jit(solution)/shard_map/owned_expert/pallas_call | solution.py:1078
  411.3 149.9 %attention_back.1 = (bf16[128,2048]{1,0:T(8,128)(2,1)}, f32[128,2048]{1,0:T(8,128)}, bf16[4,512,2048]{2,1,0:T(8,128)(2,1)}, f32[24,512]{1,0:T(8,128)}) custom-call(f32[128,4224]{1,0:T(8,128)} %bitcast.30, bf16[128,2048]{1,0:T(8,128)(2,1)} %bitcast.32, s32[128,8]{1,0:T(8,128)} %bitcast.34, f32[64,128]{1,0:T(8,128)} %constant.7.clone.cosine, ...), custom_call_target="tpu_custom_call" | custom-call | tf_op jit(solution)/shard_map/attention_back/pallas_call | solution.py:1476
  561.2 1.5 fusion.7
  562.6 1.4 slice_bitcast_fusion
  564.0 18.8 %lay_out.1 = (f32[512,2048]{1,0:T(8,128)}, f32[512,2048]{1,0:T(8,128)}, f32[512,2048]{1,0:T(8,128)}, f32[512,2048]{1,0:T(8,128)}, f32[2048,512]{1,0:T(8,128)}, /...) custom-call(bf16[4,512,2048]{2,1,0:T(8,128)(2,1)} %get-tuple-element.74.sums, ...), custom_call_target="tpu_custom_call" | custom-call | tf_op jit(solution)/shard_map/lay_out/pallas_call | solution.py:1560
